TPU v7x, 256 devices: a whole 4x4x8 slice. The times are simulated.
256 devices in a mesh: seq: 64 (over y, z_hi, x), ch: 4 (over z_lo, core).
Axes of the slice: x: 4, y: 4, z: 8 (z_hi: 4, z_lo: 2; z = z_hi * 2 + z_lo), core: 2. Of those that a mesh axis runs over, the one named last changes fastest.
Arguments:
- features: bfloat16 [16384, 3, 2048], P('seq', None, 'ch'), may hold values from -6 to 6
- short_weight: float32 [3, 3, 2048], P(None, None, 'ch'), may hold values from -3 to 3
- residue: float32 [2048, 16], P('ch'), may hold values from -1.5 to 1.5
- decay_rate: float32 [2048, 16], P('ch'), may hold values from 1.5258789e-05 to 0.04
- skip_gain: float32 [2048], P('ch'), may hold values from -2.5 to 2.5
- out_weight: bfloat16 [2048, 4096], P('ch'), may hold values from -0.125 to 0.125
- out_grad: bfloat16 [16384, 4096], P('seq', 'ch'), may hold values from -6 to 6
Outputs:
- block_out: bfloat16 [16384, 4096], P('seq', 'ch')
- feature_grad: bfloat16 [16384, 3, 2048], P('seq', None, 'ch')
- short_grad: float32 [3, 3, 2048], P(None, None, 'ch')
- residue_grad: float32 [2048, 16], P('ch')
- skip_grad: float32 [2048], P('ch')
- weight_grad: bfloat16 [4096, 2048], P('seq', 'ch')
All inputs are finite; a program needn't handle non-finite values.
Results may differ from a plain program's by a relative error of at most 0.012.
Values may be sent and summed in bfloat16 or wider, within the bound.
No kernel may reach another device: no remote copies, remote signals or barrier semaphores. Data moves between devices by JAX's collectives and lax.ppermute only.
A program may use at most 128 MiB of HBM per device.

v0:
```python
import math

import jax
import jax.numpy as jnp
from jax import lax
from jax.sharding import PartitionSpec as P

HIGHEST = lax.Precision.HIGHEST


def from_behind(block, axis, distance):
    devices = range(lax.axis_size(axis))
    route = [(i - distance, i) for i in devices if i - distance in devices]
    return lax.ppermute(block, axis, route)


def pair_combine(earlier, later):
    return (earlier[0] * later[0], later[0] * earlier[1] + later[1])


def block_conv(field, amplitude, log_pole):
    channels, length = field.shape
    block_size = min(64, length)
    block_count = length // block_size
    blocks = field.reshape(channels, block_count, block_size)
    offsets = jnp.arange(block_size).astype(jnp.float32)
    powers = jnp.exp(log_pole[:, :, None] * offsets)
    kernel = jnp.einsum("cr,cri->ci", amplitude, powers, precision=HIGHEST)
    lag_grid = offsets[:, None] - offsets[None, :]
    onehot = (lag_grid[None, :, :] == offsets[:, None, None]).astype(jnp.float32)
    toeplitz = jnp.einsum("ck,kij->cij", kernel, onehot, precision=HIGHEST)
    local_part = jnp.einsum("cij,cbj->cbi", toeplitz, blocks, precision=HIGHEST)
    tail_table = jnp.exp(log_pole[:, :, None] * (block_size - 1.0 - offsets))
    block_sums = jnp.einsum("crj,cbj->crb", tail_table, blocks, precision=HIGHEST)
    lift_factor = jnp.broadcast_to(jnp.exp(log_pole * block_size)[:, :, None], block_sums.shape)
    prefix = lax.associative_scan(pair_combine, (lift_factor, block_sums), axis=2)[1]
    entering = jnp.concatenate([jnp.zeros_like(prefix[:, :, :1]), prefix[:, :, :-1]], axis=2)
    head_table = amplitude[:, :, None] * powers * jnp.exp(log_pole)[:, :, None]
    cross_part = jnp.einsum("cri,crb->cbi", head_table, entering, precision=HIGHEST)
    return ((local_part + cross_part).reshape(channels, length), prefix[:, :, -1])


def body(features, short_weight, residue, decay_rate, skip_gain, out_weight, out_grad):
    rows_here = features.shape[0]
    channels = features.shape[2]
    kernel_taps = short_weight.shape[1]
    seq_count = lax.axis_size("seq")
    grad_scale = 1.0 / math.sqrt(rows_here * seq_count)
    before = from_behind(features[rows_here - (kernel_taps - 1) :], "seq", 1)
    padded = jnp.concatenate([before, features], axis=0).astype(jnp.float32)
    filtered = jnp.zeros((rows_here, 3, channels), jnp.float32)
    for shift_index in range(kernel_taps):
        start_row = kernel_taps - 1 - shift_index
        filtered = (
            filtered + short_weight[:, shift_index, :] * padded[start_row : start_row + rows_here]
        )
    queries = filtered[:, 0]
    key_field = filtered[:, 1]
    value_field = filtered[:, 2]
    product = (key_field * value_field).astype(jnp.bfloat16)
    amplitude = residue * jnp.sqrt(2.0 * decay_rate)
    log_pole = -decay_rate
    slice_width = channels // seq_count
    first_channel = lax.axis_index("seq") * slice_width
    amp_here = lax.dynamic_slice_in_dim(amplitude, first_channel, slice_width, 0)
    pole_here = lax.dynamic_slice_in_dim(log_pole, first_channel, slice_width, 0)
    norm_here = lax.dynamic_slice_in_dim(jnp.sqrt(2.0 * decay_rate), first_channel, slice_width, 0)
    skip_here = lax.dynamic_slice_in_dim(skip_gain, first_channel, slice_width, 0)
    product_lanes = lax.all_to_all(product.T, "seq", split_axis=0, concat_axis=1, tiled=True)
    product_float = product_lanes.astype(jnp.float32)
    conv_part = block_conv(product_float, amp_here, pole_here)[0]
    gated_lanes = (conv_part + skip_here[:, None] * product_float).astype(jnp.bfloat16)
    gated_mix = lax.all_to_all(gated_lanes, "seq", split_axis=1, concat_axis=0, tiled=True).T
    gated_float = gated_mix.astype(jnp.float32)
    mixed_out = (queries * gated_float).astype(jnp.bfloat16)
    partial_out = jnp.dot(mixed_out, out_weight, preferred_element_type=jnp.float32)
    block_out = lax.psum_scatter(
        partial_out.astype(jnp.bfloat16), "ch", scatter_dimension=1, tiled=True
    )
    grad_full = lax.all_gather(out_grad, "ch", axis=1, tiled=True)
    mixed_grad = lax.dot_general(
        grad_full, out_weight, (((1,), (1,)), ((), ())), preferred_element_type=jnp.float32
    )
    gate_grad = (mixed_grad * queries).astype(jnp.bfloat16)
    query_grad = mixed_grad * gated_float
    weight_grad = (
        lax.psum_scatter(
            lax.dot_general(
                grad_full, mixed_out, (((0,), (0,)), ((), ())), preferred_element_type=jnp.float32
            ),
            "seq",
            scatter_dimension=0,
            tiled=True,
        )
        * grad_scale
    ).astype(jnp.bfloat16)
    gate_lanes = lax.all_to_all(gate_grad.T, "seq", split_axis=0, concat_axis=1, tiled=True)
    gate_float = gate_lanes.astype(jnp.float32)
    back_part = block_conv(gate_float[:, ::-1], amp_here, pole_here)[0][:, ::-1]
    product_lanes_grad = (back_part + skip_here[:, None] * gate_float).astype(jnp.bfloat16)
    product_grad = lax.all_to_all(
        product_lanes_grad, "seq", split_axis=1, concat_axis=0, tiled=True
    ).T

    def conv_of(amp_value):
        return block_conv(product_float, amp_value, pole_here)[0]

    pull_back = jax.vjp(conv_of, amp_here)[1]
    residue_piece = pull_back(gate_float)[0] * norm_here * grad_scale
    skip_piece = jnp.sum(gate_float * product_float, axis=1) * grad_scale
    residue_grad, skip_grad = (
        lax.all_gather(residue_piece, "seq", axis=0, tiled=True),
        lax.all_gather(skip_piece, "seq", axis=0, tiled=True),
    )
    product_back = product_grad.astype(jnp.float32)
    filtered_grad = jnp.stack(
        [query_grad, product_back * value_field, product_back * key_field], axis=1
    )
    after_rows = from_behind(filtered_grad[: kernel_taps - 1], "seq", -1)
    padded_grad = jnp.concatenate([filtered_grad, after_rows], axis=0)
    feature_grad = jnp.zeros_like(filtered_grad)
    short_terms = []
    for shift_index in range(kernel_taps):
        start_row = kernel_taps - 1 - shift_index
        feature_grad = (
            feature_grad
            + short_weight[:, shift_index, :] * padded_grad[shift_index : shift_index + rows_here]
        )
        short_terms.append(
            jnp.sum(filtered_grad * padded[start_row : start_row + rows_here], axis=0)
        )
    short_local = jnp.stack(short_terms, axis=1) * grad_scale
    short_grad = lax.psum(short_local, "seq")
    return (
        block_out,
        feature_grad.astype(jnp.bfloat16),
        short_grad,
        residue_grad,
        skip_grad,
        weight_grad,
    )


def solution(mesh):
    in_specs = (
        P("seq", None, "ch"),
        P(None, None, "ch"),
        P("ch", None),
        P("ch", None),
        P("ch"),
        P("ch", None),
        P("seq", "ch"),
    )
    out_specs = (
        P("seq", "ch"),
        P("seq", None, "ch"),
        P(None, None, "ch"),
        P("ch", None),
        P("ch"),
        P("seq", "ch"),
    )
    return jax.shard_map(body, mesh=mesh, in_specs=in_specs, out_specs=out_specs, check_vma=False)
```

profile of v0, /device:TPU:32, one launch (start us, length us, event | category | flops | bytes accessed | tf_op | source)
XLA Modules:
  0.0 1023.7 jit_solution(7974157381745783256)
XLA Ops:
  8.7 3.4 collective-permute-start
  19.9 22.5 %all-gather.2.cloned.1.call-done = bf16[256,4096]{1,0:T(8,128)(2,1)} async-done(((bf16[256,1024]{1,0:T(8,128)(2,1)}), bf16[256,4096]{1,0:T(8,128)(2,1)}) %all-gather.2.cloned.1.call-update) | async-done | bytes 2097168 | tf_op jit(solution)/shard_map/all_gather | solution.py:80
  42.4 4.1 fusion.75
  48.3 13.4 %all-to-all-start.2 = ((bf16[64,8,256]{2,1,0:T(8,128)(2,1)}), bf16[64,8,256]{2,1,0:T(8,128)(2,1)S(1)}, u32[]{:S(2)}, u32[]{:S(2)}) async-start(bf16[64,8,256]{2,1,0:T(8,128)(2,1)} %bitcast.17), calls=%async_computation.3 | async-start | bytes 524288 | tf_op jit(solution)/shard_map/all_to_all | solution.py:97
  63.7 2.2 fusion.2
  65.9 11.5 %all-to-all-done.2 = bf16[64,8,256]{2,1,0:T(8,128)(2,1)S(1)} async-done(((bf16[64,8,256]{2,1,0:T(8,128)(2,1)}), bf16[64,8,256]{2,1,0:T(8,128)(2,1)S(1)}, u32[]{:S(2)}, u32[]{:S(2)}) %all-to-all-start.2) | async-done | bytes 262176 | tf_op jit(solution)/shard_map/all_to_all | solution.py:97
  78.2 9.1 rev.6
  89.4 2.8 slice.509
  92.2 2.2 slice.475
  94.4 2.2 slice.474
  114.2 3.2 pad.135
  133.1 2.7 pad.192
  135.8 2.7 pad.267
  139.3 2.3 convolution_add_fusion
  142.3 42.3 %rev.7 = f32[8,16384]{1,0:T(8,128)} reverse(f32[8,16384]{1,0:T(8,128)S(1)} %reshape.123), dimensions={1} | reverse | bytes 1048576 | tf_op jit(solution)/shard_map/rev | solution.py:99
  186.1 19.0 %all_to_all.55 = bf16[8,64,256]{2,0,1:T(8,128)(2,1)S(1)} all-to-all(bf16[8,64,256]{2,0,1:T(8,128)(2,1)S(1)} %bitcast.134), channel_id=1, replica_groups=mesh['seq'=64,'ch'=4] {'seq'}, dimensions={1} | all-to-all | bytes 524288 | tf_op jit(solution)/shard_map/all_to_all | solution.py:101
  208.0 2.2 fusion.16
  212.0 18.7 %all_to_all.56 = bf16[64,8,256]{2,1,0:T(8,128)(2,1)S(1)} all-to-all(bf16[64,8,256]{2,1,0:T(8,128)(2,1)} %bitcast.135), channel_id=1, replica_groups=mesh['seq'=64,'ch'=4] {'seq'}, dimensions={0} | all-to-all | bytes 524288 | tf_op jit(solution)/shard_map/all_to_all | solution.py:69
  234.2 2.3 fusion.43
  236.4 3.7 slice.471
  240.2 3.7 slice.426
  243.9 3.7 slice.425
  259.0 2.1 slice.436
  289.5 2.6 fusion.24
  292.1 3.3 pad.119
  297.0 4.9 pad.118
  305.3 3.4 pad.120
  308.6 4.9 pad.121
  317.6 4.9 pad.122
  322.6 5.0 pad.123
  331.6 5.0 pad.124
  336.5 5.0 pad.125
  345.6 5.1 pad.126
  350.8 5.1 pad.127
  359.1 3.8 pad.128
  362.9 5.4 pad.129
  371.7 4.7 pad.190
  376.4 6.0 pad.266
  384.1 2.7 convolution_add_fusion.1
  386.7 2.4 copy.146
  389.1 2.3 reshape.121
  393.0 18.0 %all_to_all.57 = bf16[8,64,256]{2,0,1:T(8,128)(2,1)S(1)} all-to-all(bf16[8,64,256]{2,0,1:T(8,128)(2,1)S(1)} %get-tuple-element.50), channel_id=1, replica_groups=mesh['seq'=64,'ch'=4] {'seq'}, dimensions={1} | all-to-all | bytes 524288 | tf_op jit(solution)/shard_map/all_to_all | solution.py:73
  413.8 2.3 fusion.19
  416.8 4.5 convolution_bitcast_fusion
  421.4 9.1 copy.179
  431.4 4.8 convolution_convert_fusion
  446.2 190.0 %all_gather.10 = f32[512,16]{1,0:T(8,128)S(1)} all-gather(f32[8,16]{1,0:T(8,128)S(1)} %copy.164), channel_id=1, replica_groups=mesh['seq'=64,'ch'=4] {'seq'}, dimensions={0}, use_global_device_ids=true | all-gather | bytes 33280 | tf_op jit(solution)/shard_map/all_gather | solution.py:112
  639.6 375.0 %all-reduce.35 = (f32[3,3,512]{2,0,1:T(4,128)S(1)}, f32[512]{0:T(512)}) all-reduce(f32[3,3,512]{2,0,1:T(4,128)S(1)} %maximum_multiply_fusion, f32[512]{0:T(512)S(1)} %multiply_dynamic-update-slice_fusion), channel_id=1, replica_groups=mesh['seq'=64,'ch'=4] {'seq'}, use_global_device_ids=true, to_apply=%region_4.0 | all-reduce | flops 5120 | bytes 40960 | tf_op jit(solution)/shard_map/psum | solution.py:133
  (266 shorter events, 145.8 us)
Async XLA Ops:
  7.2 12.0 %copy-start.17 = (bf16[256,3,512]{2,0,1:T(8,128)(2,1)S(1)}, bf16[256,3,512]{2,0,1:T(8,128)(2,1)}, u32[]{:S(2)}) copy-start(bf16[256,3,512]{2,0,1:T(8,128)(2,1)} %param.7) | copy-start | bytes 2359300
  7.2 35.2 %all-gather.2.cloned.1.call-start = ((), (), s32[]{:S(2)}) async-start(), calls=%async_computation.7 | async-start | bytes 2621440 | tf_op jit(solution)/shard_map/all_gather | solution.py:80
  8.7 10.5 %collective-permute-start = (bf16[2,3,512]{2,0,1:T(2,128)(2,1)S(1)}, bf16[2,3,512]{2,0,1:T(2,128)(2,1)S(1)}, u32[]{:S(2)}, u32[]{:S(2)}) collective-permute-start(bf16[2,3,512]{2,0,1:T(2,128)(2,1)S(1)} %slice.413), channel_id=1, source_target_pairs={{0,4},{4,8},{8,12},{12,16},{16,20},{20,24},{24,28},{28,32},{32,36}... | collective-permute-start | bytes 18440 | tf_op jit(solution)/shard_map/ppermute | solution.py:14
  12.8 6.5 copy-start.27
  13.8 6.1 copy-start.33
  14.7 5.2 copy-start.21
  14.7 5.2 copy-start.23
  17.6 2.3 copy-start.25
  18.2 1.7 copy-start.28
  19.1 94.3 %copy-start.18 = (f32[8,16,1]{2,1,0:T(8,128)}, f32[8,16,1]{2,1,0:T(8,128)S(1)}, u32[]{:S(2)}) copy-start(f32[8,16,1]{2,1,0:T(8,128)S(1)} %copy.143) | copy-start | bytes 1540
  19.9 26.6 %copy-start = (f32[256,3,512]{2,0,1:T(8,128)}, f32[256,3,512]{2,0,1:T(8,128)S(1)}, u32[]{:S(2)}) copy-start(f32[256,3,512]{2,0,1:T(8,128)S(1)} %multiply_add_fusion) | copy-start | bytes 4718596
  46.5 0.8 copy-start.8
  48.3 29.1 %all-to-all-start.2 = ((bf16[64,8,256]{2,1,0:T(8,128)(2,1)}), bf16[64,8,256]{2,1,0:T(8,128)(2,1)S(1)}, u32[]{:S(2)}, u32[]{:S(2)}) async-start(bf16[64,8,256]{2,1,0:T(8,128)(2,1)} %bitcast.17), calls=%async_computation.3 | async-start | bytes 524288 | tf_op jit(solution)/shard_map/all_to_all | solution.py:97
  61.7 953.5 %reduce-scatter.7.cloned.1.call-start = ((), (), s32[]{:S(2)}) async-start(), calls=%async_computation.8 | async-start | bytes 8519680
  63.1 0.6 copy-start.31
  77.4 0.8 copy-start.6
  89.3 19.3 %copy-start.14 = (f32[8,16,256]{2,1,0:T(8,128)}, f32[8,16,256]{2,1,0:T(8,128)S(1)}, u32[]{:S(2)}) copy-start(f32[8,16,256]{2,1,0:T(8,128)S(1)} %fusion.42) | copy-start | bytes 393220
  114.2 7.0 copy-start.20
  122.0 10.9 %copy-start.19 = (f32[8,16,127]{2,1,0:T(8,128)S(1)}, f32[8,16,127]{2,1,0:T(8,128)}, u32[]{:S(2)}) copy-start(f32[8,16,127]{2,1,0:T(8,128)} %slice.509) | copy-start | bytes 195076
  122.7 10.3 %slice-start = ((f32[8,16,256]{2,1,0:T(8,128)}), f32[8,16,1]{2,1,0:T(8,128)S(1)}, s32[]{:S(2)}) async-start(f32[8,16,256]{2,1,0:T(8,128)} %copy-done.14), calls=%async_computation.9 | async-start | bytes 131072 | tf_op jit(solution)/shard_map/slice | solution.py:36
  125.4 13.1 %copy-start.29 = (f32[8,16]{1,0:T(8,128)S(1)}, f32[8,16]{1,0:T(8,128)}, u32[]{:S(2)}) copy-start(f32[8,16]{1,0:T(8,128)} %copy.144) | copy-start | bytes 1540
  125.4 13.1 %copy-start.34 = (f32[64]{0:T(128)S(1)}, f32[64]{0:T(128)}, u32[]{:S(2)}) copy-start(f32[64]{0:T(128)} %copy-done.33) | copy-start | bytes 772
  141.9 42.7 %copy-start.36 = (f32[8]{0:T(128)S(1)}, f32[8]{0:T(128)}, u32[]{:S(2)}) copy-start(f32[8]{0:T(128)} %dynamic_slice.14) | copy-start | bytes 100
  184.7 23.3 %copy-start.1 = (f32[256,3,512]{2,0,1:T(8,128)S(1)}, f32[256,3,512]{2,0,1:T(8,128)}, u32[]{:S(2)}) copy-start(f32[256,3,512]{2,0,1:T(8,128)} %copy-done) | copy-start | bytes 4718596
  210.1 24.0 %copy-start.38 = (f32[64]{0:T(128)S(1)}, f32[64]{0:T(128)}, u32[]{:S(2)}) copy-start(f32[64]{0:T(128)} %broadcast_subtract_fusion.1) | copy-start | bytes 772
  230.7 0.7 copy-start.7
  250.1 31.3 %copy-start.10 = (f32[8,16,128]{2,1,0:T(8,128)}, f32[8,16,128]{2,1,0:T(8,128)S(1)}, u32[]{:S(2)}) copy-start(f32[8,16,128]{2,1,0:T(8,128)S(1)} %multiply_add_fusion.14) | copy-start | bytes 196612
  313.5 44.9 %copy-start.11 = (f32[8,16,128]{2,1,0:T(8,128)S(1)}, f32[8,16,128]{2,1,0:T(8,128)}, u32[]{:S(2)}) copy-start(f32[8,16,128]{2,1,0:T(8,128)} %copy-done.10) | copy-start | bytes 196612
  343.1 41.0 %copy-start.30 = (f32[8,16]{1,0:T(8,128)S(1)}, f32[8,16]{1,0:T(8,128)}, u32[]{:S(2)}) copy-start(f32[8,16]{1,0:T(8,128)} %copy.144) | copy-start | bytes 1540
  343.1 41.0 %copy-start.35 = (f32[64]{0:T(128)S(1)}, f32[64]{0:T(128)}, u32[]{:S(2)}) copy-start(f32[64]{0:T(128)} %copy-done.33) | copy-start | bytes 772
  383.4 0.6 copy-start.12
  386.7 4.7 copy-start.37
  413.8 3.0 copy-start.9
  416.1 0.7 copy-start.15
  430.5 0.9 copy-start.16
  430.5 586.5 %reduce-scatter.5.cloned.1.call-start = ((), (), s32[]{:S(2)}) async-start(), calls=%async_computation.6 | async-start | bytes 2621440 | tf_op jit(solution)/shard_map/reduce_scatter | solution.py:77
  436.2 0.7 copy-start.39
  436.2 3.0 copy-start.4
  436.2 4.5 copy-start.32
  438.2 4.1 copy-start.13
  439.2 5.6 copy-start.2
  439.2 5.6 copy-start.3
  440.7 4.1 copy-start.5
  444.9 192.0 %collective-permute-start.1 = (f32[2,3,512]{2,0,1:T(2,128)S(1)}, f32[2,3,512]{2,0,1:T(2,128)S(1)}, u32[]{:S(2)}, u32[]{:S(2)}) collective-permute-start(f32[2,3,512]{2,0,1:T(2,128)S(1)} %slice.568), channel_id=1, source_target_pairs={{4,0},{8,4},{12,8},{16,12},{20,16},{24,20},{28,24},{32,28},{36,32}... | collective-permute-start | bytes 36872 | tf_op jit(solution)/shard_map/ppermute | solution.py:14
  636.9 0.7 copy-start.22
  636.9 0.7 copy-start.24
  636.9 0.7 copy-start.26
Sparse Core Ops, SparseCore 0:
  9.8 32.5 all-gather.1
  430.6 399.0 reduce-scatter.6
  832.9 27.1 reduce-scatter.4
where the time goes:
time: 1040 us; the launch traced here: 1020 us
  blocking collectives  621 us (60%)
  local copies, waits for them, and re-layouts  237 us (23%)
  other arithmetic  63.7 us (6%)
  waiting for transfers between devices  34.7 us (3%)
  matrix products  33.1 us (3%)
  starting transfers between devices  18.2 us (2%)
  between operations  15.9 us (2%)
    psum x1, blocking collectives, body(): short_grad = lax.psum(short_local, 'seq')  375 us
    all_gather x1, blocking collectives, body(): lax.all_gather(residue_piece, 'seq', axis=0, tiled=True)  190 us
    pad x24, local copies, waits for them, and re-layouts, block_conv(): lax.associative_scan(pair_combine, (lift_factor, block_sums), axis=2)[1]  69.1 us
    slice x43, local copies, waits for them, and re-layouts, block_conv(): lax.associative_scan(pair_combine, (lift_factor, block_sums), axis=2)[1]  59.7 us
    rev x2, local copies, waits for them, and re-layouts, body(): back_part = block_conv(gate_float[:, ::-1], amp_here, pole_here)[0][:, ::-1]  51.4 us
    unnamed x91, local copies, waits for them, and re-layouts  27.9 us
    add x28, other arithmetic, pair_combine(): return (earlier[0] * later[0], later[0] * earlier[1] + later[1])  23.7 us
    all_gather x1, waiting for transfers between devices, body(): grad_full = lax.all_gather(out_grad, 'ch', axis=1, tiled=True)  22.5 us
  transfers between devices with their start and end apart: 6, of which 2 were waited for; matrix products, arithmetic and copies ran while one was open for 3% of the time, Pallas kernels for 0%

commit v1 on v0

v1 whole, which is shorter than its diff:
```python
import functools
import math

import jax
import jax.numpy as jnp
from jax import lax
from jax.experimental import pallas as pl
from jax.experimental.pallas import tpu as pltpu
from jax.sharding import PartitionSpec as P

F32 = jnp.float32
BF16 = jnp.bfloat16
CHUNKS = 8
LANES = 128
STRIDES = {"x": 1, "z": 4, "y": 16}


def digit(name):
    return (lax.axis_index("seq") // STRIDES[name]) % 4


def ring(block, name, step):
    stride = STRIDES[name]
    route = []
    for source in range(64):
        place = (source // stride) % 4
        route.append((source, source + ((place + step) % 4 - place) * stride))
    return lax.ppermute(block, "seq", route)


def flip_ch(block, mask):
    return lax.ppermute(block, "ch", [(i, i ^ mask) for i in range(4)])


def from_behind(block, distance):
    route = [(i - distance, i) for i in range(64) if 0 <= i - distance < 64]
    return lax.ppermute(block, "seq", route)


def step_rows(index, steps, reverse):
    offset = steps - 1 - index if reverse else index
    return pl.ds(offset, CHUNKS, stride=steps)


def shifted(rows, places, order, reverse):
    moved = pltpu.roll(rows, CHUNKS - places if reverse else places, 0)
    return jnp.where(order >= places, moved, 0.0)


def state_kernel(signal_ref, rate_ref, entry_ref, total_ref, *, reverse):
    steps = signal_ref.shape[0] // CHUNKS
    modes = rate_ref.shape[0]
    order = lax.broadcasted_iota(jnp.int32, (CHUNKS, LANES), 0)
    if reverse:
        order = CHUNKS - 1 - order
    decay = [
        jnp.exp(jnp.broadcast_to(-rate_ref[pl.ds(r, 1), :], (CHUNKS, LANES))) for r in range(modes)
    ]

    def advance(index, states):
        row = signal_ref[step_rows(index, steps, reverse), :]
        return tuple(decay[r] * states[r] + row for r in range(modes))

    zero = jnp.zeros((CHUNKS, LANES), F32)
    states = lax.fori_loop(0, steps, advance, (zero,) * modes, unroll=4)
    last = 0 if reverse else CHUNKS - 1
    for r in range(modes):
        rate = rate_ref[pl.ds(r, 1), :]
        prefix = states[r]
        for places in (1, 2, 4):
            prefix = prefix + jnp.exp(-rate * (places * steps)) * shifted(
                prefix, places, order, reverse
            )
        entry_ref[r] = shifted(prefix, 1, order, reverse)
        total_ref[pl.ds(r, 1), :] = prefix[last : last + 1]


def entry_states(entry_ref, incoming_ref, rate_ref, steps, reverse):
    order = lax.broadcasted_iota(jnp.int32, (CHUNKS, LANES), 0)
    if reverse:
        order = CHUNKS - 1 - order
    span = (order * steps).astype(F32)
    states = []
    for r in range(rate_ref.shape[0]):
        fade = jnp.exp(-rate_ref[pl.ds(r, 1), :] * span)
        states.append(entry_ref[r] + fade * incoming_ref[pl.ds(r, 1), :])
    return tuple(states)


def mode_sum(terms):
    while len(terms) > 1:
        terms = [a + b for a, b in zip(terms[::2], terms[1::2])]
    return terms[0]


def forward_kernel(signal_ref, rate_ref, amp_ref, skip_ref, entry_ref, incoming_ref, out_ref):
    steps = signal_ref.shape[0] // CHUNKS
    modes = rate_ref.shape[0]
    wide = (CHUNKS, LANES)
    decay = [jnp.exp(jnp.broadcast_to(-rate_ref[pl.ds(r, 1), :], wide)) for r in range(modes)]
    amp = [jnp.broadcast_to(amp_ref[pl.ds(r, 1), :], wide) for r in range(modes)]
    skip = jnp.broadcast_to(skip_ref[...], wide)

    def advance(index, states):
        rows = step_rows(index, steps, False)
        row = signal_ref[rows, :]
        states = tuple(decay[r] * states[r] + row for r in range(modes))
        out_ref[rows, :] = mode_sum([amp[r] * states[r] for r in range(modes)]) + skip * row
        return states

    start = entry_states(entry_ref, incoming_ref, rate_ref, steps, False)
    lax.fori_loop(0, steps, advance, start, unroll=2)


def backward_kernel(
    signal_ref, other_ref, rate_ref, amp_ref, skip_ref, entry_ref, incoming_ref, out_ref, dot_ref
):
    steps = signal_ref.shape[0] // CHUNKS
    modes = rate_ref.shape[0]
    wide = (CHUNKS, LANES)
    decay = [jnp.exp(jnp.broadcast_to(-rate_ref[pl.ds(r, 1), :], wide)) for r in range(modes)]
    amp = [jnp.broadcast_to(amp_ref[pl.ds(r, 1), :], wide) for r in range(modes)]
    skip = jnp.broadcast_to(skip_ref[...], wide)

    def advance(index, carry):
        states, sums, direct = carry
        rows = step_rows(index, steps, True)
        row = signal_ref[rows, :]
        other = other_ref[rows, :]
        states = tuple(decay[r] * states[r] + row for r in range(modes))
        out_ref[rows, :] = mode_sum([amp[r] * states[r] for r in range(modes)]) + skip * row
        sums = tuple(sums[r] + other * states[r] for r in range(modes))
        return states, sums, direct + row * other

    zero = jnp.zeros(wide, F32)
    start = entry_states(entry_ref, incoming_ref, rate_ref, steps, True)
    _, sums, direct = lax.fori_loop(0, steps, advance, (start, (zero,) * modes, zero), unroll=2)
    for r in range(modes):
        dot_ref[pl.ds(r, 1), :] = jnp.sum(sums[r], axis=0, keepdims=True)
    dot_ref[pl.ds(modes, 1), :] = jnp.sum(direct, axis=0, keepdims=True)


def column(rows):
    return pl.BlockSpec((rows, LANES), lambda i: (0, i))


def entry_spec(modes):
    return pl.BlockSpec((modes, CHUNKS, LANES), lambda i: (0, 0, i))


def local_states(signal, rate, reverse):
    rows, channels = signal.shape
    modes = rate.shape[0]
    return pl.pallas_call(
        functools.partial(state_kernel, reverse=reverse),
        grid=(channels // LANES,),
        in_specs=[column(rows), column(modes)],
        out_specs=[entry_spec(modes), column(modes)],
        out_shape=[
            jax.ShapeDtypeStruct((modes, CHUNKS, channels), F32),
            jax.ShapeDtypeStruct((modes, channels), F32),
        ],
    )(signal, rate)


def forward_apply(signal, rate, amp, skip, entry, incoming):
    rows, channels = signal.shape
    modes = rate.shape[0]
    return pl.pallas_call(
        forward_kernel,
        grid=(channels // LANES,),
        in_specs=[
            column(rows),
            column(modes),
            column(modes),
            column(1),
            entry_spec(modes),
            column(modes),
        ],
        out_specs=column(rows),
        out_shape=jax.ShapeDtypeStruct((rows, channels), F32),
    )(signal, rate, amp, skip, entry, incoming)


def backward_apply(signal, other, rate, amp, skip, entry, incoming):
    rows, channels = signal.shape
    modes = rate.shape[0]
    return pl.pallas_call(
        backward_kernel,
        grid=(channels // LANES,),
        in_specs=[
            column(rows),
            column(rows),
            column(modes),
            column(modes),
            column(1),
            entry_spec(modes),
            column(modes),
        ],
        out_specs=[column(rows), column(modes + 1)],
        out_shape=[
            jax.ShapeDtypeStruct((rows, channels), F32),
            jax.ShapeDtypeStruct((modes + 1, channels), F32),
        ],
    )(signal, other, rate, amp, skip, entry, incoming)


def entering(total, rate, rows, reverse):
    direction = -1 if reverse else 1
    span = rows
    passed = jnp.zeros((), jnp.int32)
    result = jnp.zeros_like(total)
    for name in ("x", "z", "y"):
        place = digit(name)
        if reverse:
            place = 3 - place
        pieces = [total] + [ring(total, name, direction * k) for k in (1, 2, 3)]
        before = jnp.zeros_like(total)
        whole = jnp.zeros_like(total)
        for k in range(4):
            if k:
                fade = jnp.exp(-rate * (span * (k - 1)))
                before = before + jnp.where(place >= k, fade * pieces[k], 0.0)
            gap = (3 - (place - k) % 4) * span
            whole = whole + jnp.exp(-rate * gap.astype(F32)) * pieces[k]
        result = result + jnp.exp(-rate * passed.astype(F32)) * before
        passed = passed + place * span
        total = whole
        span = span * 4
    return result


def sum_over_seq(block):
    for name in ("x", "z", "y"):
        pieces = [ring(block, name, k) for k in (1, 2, 3)]
        block = (block + pieces[0]) + (pieces[1] + pieces[2])
    return block


def gather_ch(block):
    chip = flip_ch(block, 2)
    core = flip_ch(block, 1)
    both = flip_ch(chip, 1)
    return [block, core, chip, both]


def body(features, short_weight, residue, decay_rate, skip_gain, out_weight, out_grad):
    rows = features.shape[0]
    channels = features.shape[2]
    taps = short_weight.shape[1]
    width = out_grad.shape[1]
    grad_scale = 1.0 / math.sqrt(rows * 64)
    ch = lax.axis_index("ch")
    here = lax.axis_index("seq")

    rate = decay_rate.T
    norm = jnp.sqrt(2.0 * rate)
    amp = residue.T * norm
    skip = skip_gain[None, :]

    before = from_behind(features[rows - (taps - 1) :], 1)
    grad_pieces = gather_ch(out_grad)

    route = []
    for source in range(256):
        s, j = divmod(source, 4)
        y = s // 16
        route.append((source, (s - 16 * y + 16 * j) * 4 + y))
    turned = lax.ppermute(out_grad, ("seq", "ch"), route)

    padded = jnp.concatenate([before, features], axis=0).astype(F32)
    streams = [padded[:, i] for i in range(3)]
    filtered = []
    for i in range(3):
        total = jnp.zeros((rows, channels), F32)
        for j in range(taps):
            start = taps - 1 - j
            total = total + short_weight[i, j] * streams[i][start : start + rows]
        filtered.append(total)
    queries, keys, values = filtered
    product = (keys * values).astype(BF16).astype(F32)

    entry, total = local_states(product, rate, False)
    incoming = entering(total, rate, rows, False)

    def weight_block(mask):
        return lax.dynamic_slice_in_dim(out_weight, (ch ^ mask) * width, width, 1)

    mixed_grad = jnp.zeros((rows, channels), F32)
    for mask in range(4):
        mixed_grad = mixed_grad + lax.dot_general(
            grad_pieces[mask],
            weight_block(mask),
            (((1,), (1,)), ((), ())),
            preferred_element_type=F32,
        )
    gate_grad = (mixed_grad * queries).astype(BF16).astype(F32)
    back_entry, back_total = local_states(gate_grad, rate, True)

    gated = forward_apply(product, rate, amp, skip, entry, incoming).astype(BF16).astype(F32)
    mixed_out = (queries * gated).astype(BF16)
    query_grad = mixed_grad * gated

    back_incoming = entering(back_total, rate, rows, True)

    def out_block(mask):
        return jnp.dot(mixed_out, weight_block(mask), preferred_element_type=F32)

    sent = jnp.concatenate([out_block(1).astype(BF16), out_block(3).astype(BF16)], axis=0)
    got = flip_ch(sent, 1).astype(F32)
    far = flip_ch((out_block(2) + got[rows:]).astype(BF16), 2)
    block_out = (out_block(0) + got[:rows] + far.astype(F32)).astype(BF16)

    turned_pieces = jnp.concatenate(gather_ch(turned), axis=0)
    y_here = digit("y")
    around = jnp.stack([mixed_out] + [ring(mixed_out, "y", k) for k in (1, 2, 3)], axis=0)
    mixed_pieces = jnp.concatenate(
        [
            lax.dynamic_index_in_dim(around, (y_here - (ch ^ mask)) % 4, 0, False)
            for mask in range(4)
        ],
        axis=0,
    )
    share = lax.dot_general(
        turned_pieces, mixed_pieces, (((0,), (0,)), ((), ())), preferred_element_type=F32
    ).astype(BF16)
    groups = [[16 * y + i for i in range(16)] for y in range(4)]
    shares = lax.all_to_all(
        share, "seq", split_axis=0, concat_axis=0, axis_index_groups=groups, tiled=True
    )
    weight_grad = (
        jnp.sum(shares.reshape(16, width // 16, channels).astype(F32), axis=0) * grad_scale
    ).astype(BF16)

    back, dots = backward_apply(gate_grad, product, rate, amp, skip, back_entry, back_incoming)
    back = back.astype(BF16).astype(F32)
    filtered_grad = [query_grad, back * values, back * keys]
    edge = from_behind(jnp.stack([g[: taps - 1] for g in filtered_grad]), -1)
    feature_grad = []
    short_terms = []
    for i in range(3):
        padded_grad = jnp.concatenate([filtered_grad[i], edge[i]], axis=0)
        grad = jnp.zeros((rows, channels), F32)
        for j in range(taps):
            start = taps - 1 - j
            grad = grad + short_weight[i, j] * padded_grad[j : j + rows]
            short_terms.append(jnp.sum(filtered_grad[i] * streams[i][start : start + rows], axis=0))
        feature_grad.append(grad.astype(BF16))
    modes = rate.shape[0]
    sums = sum_over_seq(jnp.concatenate([dots, jnp.stack(short_terms)], axis=0))
    residue_grad = (sums[:modes] * norm * grad_scale).T
    skip_grad = sums[modes] * grad_scale
    short_grad = (sums[modes + 1 :] * grad_scale).reshape(3, taps, channels)
    return (
        block_out,
        jnp.stack(feature_grad, axis=1),
        short_grad,
        residue_grad,
        skip_grad,
        weight_grad,
    )


def solution(mesh):
    in_specs = (
        P("seq", None, "ch"),
        P(None, None, "ch"),
        P("ch", None),
        P("ch", None),
        P("ch"),
        P("ch", None),
        P("seq", "ch"),
    )
    out_specs = (
        P("seq", "ch"),
        P("seq", None, "ch"),
        P(None, None, "ch"),
        P("ch", None),
        P("ch"),
        P("seq", "ch"),
    )
    return jax.shard_map(body, mesh=mesh, in_specs=in_specs, out_specs=out_specs, check_vma=False)
```

time: 1040 us -> 191 us (0.18)
  the two profiles are of different devices: /device:TPU:32 before, /device:TPU:4 now
where the time goes in v1:
time: 191 us; the launch traced here: 189 us
  starting transfers between devices  92 us (48%)
  waiting for transfers between devices  43.2 us (23%)
  matrix products  18.9 us (10%)
  Pallas kernels  17.4 us (9%)
  other arithmetic  12.9 us (7%)
  local copies, waits for them, and re-layouts  3.66 us (2%)
    ppermute x30, starting transfers between devices, ring(): return lax.ppermute(block, 'seq', route)  63.3 us
    ppermute x30, waiting for transfers between devices, ring(): return lax.ppermute(block, 'seq', route)  21.7 us
    ppermute x8, waiting for transfers between devices, flip_ch(): return lax.ppermute(block, 'ch', [(i, i ^ mask) for i in range(4)])  19.8 us
    all_to_all x1, starting transfers between devices, body(): lax.all_to_all(share, 'seq', split_axis=0, concat_axis=0, axis_index_grou...  8.7 us
    dot_general x4, matrix products, out_block(): return jnp.dot(mixed_out, weight_block(mask), preferred_element_type=F32)  7.78 us
    ppermute x8, starting transfers between devices, flip_ch(): return lax.ppermute(block, 'ch', [(i, i ^ mask) for i in range(4)])  7.72 us
    pallas_call x2, Pallas kernels, local_states(): pl.pallas_call(functools.partial(state_kernel, reverse=reverse), grid=(ch...  7.52 us
    dot_general x4, matrix products, body(): lax.dot_general(grad_pieces[mask], weight_block(mask), (((1,), (1,)), (()...  7.29 us
  transfers between devices with their start and end apart: 42, of which 14 were waited for; matrix products, arithmetic and copies ran while one was open for 18% of the time, Pallas kernels for 9%

profile of v1, /device:TPU:4, one launch (start us, length us, event | category | flops | bytes accessed | tf_op | source)
XLA Modules:
  0.0 189.1 jit_solution(18260840752555300674)
XLA Ops:
  0.8 2.0 %collective-permute-start.13 = (bf16[256,1024]{1,0:T(8,128)(2,1)}, bf16[256,1024]{1,0:T(8,128)(2,1)}, u32[]{:S(2)}, u32[]{:S(2)}) collective-permute-start(bf16[256,1024]{1,0:T(8,128)(2,1)} %param.13), channel_id=1, source_target_pairs={{0,2},{1,3},{2,0},{3,1},{4,6},{5,7},{6,4},{7,5},{8,10},{9,11},{10,... | collective-permute-start | bytes 1572872 | tf_op jit(solution)/shard_map/ppermute | solution.py:32
  2.8 5.4 %collective-permute-start.34 = (bf16[256,1024]{1,0:T(8,128)(2,1)}, bf16[256,1024]{1,0:T(8,128)(2,1)}, u32[]{:S(2)}, u32[]{:S(2)}) collective-permute-start(bf16[256,1024]{1,0:T(8,128)(2,1)} %param.13), channel_id=1, source_target_pairs={{0,0},{1,64},{2,128},{3,192},{4,4},{5,68},{6,132},{7,196},{8,8},{9... | collective-permute-start | bytes 1572872 | tf_op jit(solution)/shard_map/ppermute | solution.py:269
  8.9 3.1 %collective-permute-start = (bf16[2,3,512]{2,0,1:T(2,128)(2,1)S(1)}, bf16[2,3,512]{2,0,1:T(2,128)(2,1)S(1)}, u32[]{:S(2)}, u32[]{:S(2)}) collective-permute-start(bf16[2,3,512]{2,0,1:T(2,128)(2,1)S(1)} %slice.166), channel_id=1, source_target_pairs={{0,4},{4,8},{8,12},{12,16},{16,20},{20,24},{24,28},{28,32},{32,36}... | collective-permute-start | bytes 18440 | tf_op jit(solution)/shard_map/ppermute | solution.py:37
  12.0 1.8 fusion.31
  15.9 1.7 convolution_add_fusion.2
  17.6 1.5 convolution_add_fusion.1
  19.2 2.2 %fusion.54 = (f32[256,512]{1,0:T(8,128)}, f32[256,512]{1,0:T(8,128)}, f32[256,512]{1,0:T(8,128)}, f32[256,512]{1,0:T(8,128)}, f32[256,512]{1,0:T(8,128)}, /*index=5*/f32[256,512]{1,0:T(8,128)}) fusion(f32[258,3,512]{2,0,1:T(8,128)S(1)} %maximum_convert_fusion, f32[512]{0:T(512)S(1)} %bitcast.150, f32[512]{0:T(512)S(1)} %bitcast.152, f32[512]{0:T(512)S(1)} %bitcast.148, ...), kind=kOutput, calls=%fused_computation.98 | convolution fusion | flops 271319040 | bytes 9979908 | tf_op jit(solution)/shard_map/dot_general | solution.py:291
  21.4 3.7 %shard_map.118 = (f32[16,8,512]{2,1,0:T(8,128)}, f32[16,512]{1,0:T(8,128)}) custom-call(f32[256,512]{1,0:T(8,128)} %get-tuple-element.38.signal_ref.other_ref, f32[16,512]{1,0:T(8,128)} %bitcast.138), custom_call_target="tpu_custom_call" | custom-call | tf_op jit(solution)/shard_map/pallas_call | solution.py:154
  25.1 2.0 %collective-permute-start.1 = (f32[16,512]{1,0:T(8,128)}, f32[16,512]{1,0:T(8,128)S(1)}, u32[]{:S(2)}, u32[]{:S(2)}) collective-permute-start(f32[16,512]{1,0:T(8,128)} %get-tuple-element.13), channel_id=1, source_target_pairs={{0,4},{4,8},{8,12},{12,0},{16,20},{20,24},{24,28},{28,16},{32,36},... | collective-permute-start | bytes 98312 | tf_op jit(solution)/shard_map/ppermute | solution.py:28
  27.5 2.5 %collective-permute-start.3 = (f32[16,512]{1,0:T(8,128)}, f32[16,512]{1,0:T(8,128)S(1)}, u32[]{:S(2)}, u32[]{:S(2)}) collective-permute-start(f32[16,512]{1,0:T(8,128)} %get-tuple-element.13), channel_id=1, source_target_pairs={{0,12},{4,0},{8,4},{12,8},{16,28},{20,16},{24,20},{28,24},{32,44},... | collective-permute-start | bytes 98312 | tf_op jit(solution)/shard_map/ppermute | solution.py:28
  30.0 3.8 %shard_map.120 = (f32[16,8,512]{2,1,0:T(8,128)}, f32[16,512]{1,0:T(8,128)}) custom-call(f32[256,512]{1,0:T(8,128)} %get-tuple-element.41.signal_ref, f32[16,512]{1,0:T(8,128)} %bitcast.139), custom_call_target="tpu_custom_call" | custom-call | tf_op jit(solution)/shard_map/pallas_call | solution.py:154
  35.4 2.4 %collective-permute-start.17 = (f32[16,512]{1,0:T(8,128)}, f32[16,512]{1,0:T(8,128)S(1)}, u32[]{:S(2)}, u32[]{:S(2)}) collective-permute-start(f32[16,512]{1,0:T(8,128)} %get-tuple-element.15), channel_id=1, source_target_pairs={{0,4},{4,8},{8,12},{12,0},{16,20},{20,24},{24,28},{28,16},{32,36},... | collective-permute-start | bytes 98312 | tf_op jit(solution)/shard_map/ppermute | solution.py:28
  37.7 1.5 collective-permute-start.36
  39.2 1.5 collective-permute-done.16
  41.5 6.4 %collective-permute-start.18 = (f32[16,512]{1,0:T(8,128)S(1)}, f32[16,512]{1,0:T(8,128)S(1)}, u32[]{:S(2)}, u32[]{:S(2)}) collective-permute-start(f32[16,512]{1,0:T(8,128)S(1)} %get-tuple-element.51), channel_id=1, source_target_pairs={{0,48},{4,52},{8,56},{12,60},{16,0},{20,4},{24,8},{28,12},{32,16},... | collective-permute-start | bytes 98312 | tf_op jit(solution)/shard_map/ppermute | solution.py:28
  48.7 2.6 %collective-permute-start.20 = (f32[16,512]{1,0:T(8,128)S(1)}, f32[16,512]{1,0:T(8,128)S(1)}, u32[]{:S(2)}, u32[]{:S(2)}) collective-permute-start(f32[16,512]{1,0:T(8,128)S(1)} %get-tuple-element.51), channel_id=1, source_target_pairs={{0,16},{4,20},{8,24},{12,28},{16,32},{20,36},{24,40},{28,44},{32,4... | collective-permute-start | bytes 98312 | tf_op jit(solution)/shard_map/ppermute | solution.py:28
  51.3 3.1 %collective-permute-start.4 = (f32[16,512]{1,0:T(8,128)S(1)}, f32[16,512]{1,0:T(8,128)S(1)}, u32[]{:S(2)}, u32[]{:S(2)}) collective-permute-start(f32[16,512]{1,0:T(8,128)S(1)} %get-tuple-element.52), channel_id=1, source_target_pairs={{0,16},{4,20},{8,24},{12,28},{16,32},{20,36},{24,40},{28,44},{32,4... | collective-permute-start | bytes 98312 | tf_op jit(solution)/shard_map/ppermute | solution.py:28
  55.2 6.0 %collective-permute-done.19 = f32[16,512]{1,0:T(8,128)S(1)} collective-permute-done((f32[16,512]{1,0:T(8,128)S(1)}, f32[16,512]{1,0:T(8,128)S(1)}, u32[]{:S(2)}, u32[]{:S(2)}) %collective-permute-start.19) | collective-permute-done | bytes 32800 | tf_op jit(solution)/shard_map/ppermute | solution.py:28
  62.3 3.9 %collective-permute-done.6 = f32[16,512]{1,0:T(8,128)S(1)} collective-permute-done((f32[16,512]{1,0:T(8,128)S(1)}, f32[16,512]{1,0:T(8,128)S(1)}, u32[]{:S(2)}, u32[]{:S(2)}) %collective-permute-start.6) | collective-permute-done | bytes 32800 | tf_op jit(solution)/shard_map/ppermute | solution.py:28
  66.8 12.9 %collective-permute-start.21 = (f32[16,512]{1,0:T(8,128)S(1)}, f32[16,512]{1,0:T(8,128)S(1)}, u32[]{:S(2)}, u32[]{:S(2)}) collective-permute-start(f32[16,512]{1,0:T(8,128)S(1)} %get-tuple-element.48), channel_id=1, source_target_pairs={{0,192},{4,196},{8,200},{12,204},{16,208},{20,212},{24,216},{28,22... | collective-permute-start | bytes 98312 | tf_op jit(solution)/shard_map/ppermute | solution.py:28
  79.9 1.4 collective-permute-start.23
  81.9 1.9 collective-permute-start.7
  83.7 1.5 collective-permute-done.22
  87.2 5.5 %shard_map.121 = (f32[256,512]{1,0:T(8,128)}, f32[17,512]{1,0:T(8,128)}) custom-call(f32[256,512]{1,0:T(8,128)} %get-tuple-element.41.signal_ref, f32[256,512]{1,0:T(8,128)} %get-tuple-element.38.signal_ref.other_ref, f32[16,512]{1,0:T(8,128)} %bitcast.140, f32[16,512]{1,0:T(8,128)} %get-tuple-element.49.amp_ref, f32[1,512]{1,0:T(1,128)} %bitcast.146, ...), custom_call_target="tpu_custom_call" | custom-call | tf_op jit(solution)/shard_map/pallas_call | solution.py:188
  93.5 4.4 %shard_map.119 = f32[256,512]{1,0:T(8,128)} custom-call(f32[256,512]{1,0:T(8,128)} %get-tuple-element.38.signal_ref.other_ref, f32[16,512]{1,0:T(8,128)} %bitcast.141, f32[16,512]{1,0:T(8,128)} %get-tuple-element.49.amp_ref, f32[1,512]{1,0:T(1,128)} %bitcast.147, f32[16,8,512]{2,1,0:T(8,128)} %get-tuple-element.12.entry_ref, ...), custom_call_target="tpu_custom_call" | custom-call | tf_op jit(solution)/shard_map/pallas_call | solution.py:169
  97.8 3.1 %multiply_reduce_fusion = (f32[512]{0:T(512)S(1)}, f32[512]{0:T(512)S(1)}, f32[512]{0:T(512)S(1)}, f32[512]{0:T(512)S(1)}, f32[512]{0:T(512)}, /*index=5*/f32[51...) fusion(f32[258,3,512]{2,0,1:T(8,128)S(1)} %maximum_convert_fusi, ...), kind=kLoop, calls=%fused_computation.84 | loop fusion | flops 3534336 | bytes 9717760 | tf_op jit(solution)/shard_map/reduce_sum | solution.py:347
  101.7 1.6 collective-permute-start.25
  103.3 1.7 convolution_convert_fusion.1
  105.0 1.7 convolution_convert_fusion
  106.7 3.8 %collective-permute-start.24 = (f32[3,2,512]{2,1,0:T(2,128)S(1)}, f32[3,2,512]{2,1,0:T(2,128)S(1)}, u32[]{:S(2)}, u32[]{:S(2)}) collective-permute-start(f32[3,2,512]{2,1,0:T(2,128)S(1)} %pad_maximum_fusion.6), channel_id=1, source_target_pairs={{4,0},{8,4},{12,8},{16,12},{20,16},{24,20},{28,24},{32,28},{36,32}... | collective-permute-start | bytes 36872 | tf_op jit(solution)/shard_map/ppermute | solution.py:37
  112.9 1.4 collective-permute-start.27
  114.2 1.9 collective-permute-start.38
  116.1 2.4 %collective-permute-start.39 = (bf16[256,512]{1,0:T(8,128)(2,1)S(1)}, bf16[256,512]{1,0:T(8,128)(2,1)S(1)}, u32[]{:S(2)}, u32[]{:S(2)}) collective-permute-start(bf16[256,512]{1,0:T(8,128)(2,1)S(1)} %get-tuple-element.47), channel_id=1, source_target_pairs={{0,128},{4,132},{8,136},{12,140},{16,144},{20,148},{24,152},{28,15... | collective-permute-start | bytes 786440 | tf_op jit(solution)/shard_map/ppermute | solution.py:28
  118.5 1.6 collective-permute-done.27
  120.1 2.9 %collective-permute-start.40 = (bf16[256,512]{1,0:T(8,128)(2,1)S(1)}, bf16[256,512]{1,0:T(8,128)(2,1)S(1)}, u32[]{:S(2)}, u32[]{:S(2)}) collective-permute-start(bf16[256,512]{1,0:T(8,128)(2,1)S(1)} %get-tuple-element.47), channel_id=1, source_target_pairs={{0,192},{4,196},{8,200},{12,204},{16,208},{20,212},{24,216},{28,22... | collective-permute-start | bytes 786440 | tf_op jit(solution)/shard_map/ppermute | solution.py:28
  124.3 3.0 %collective-permute-done.38 = bf16[256,512]{1,0:T(8,128)(2,1)S(1)} collective-permute-done((bf16[256,512]{1,0:T(8,128)(2,1)S(1)}, bf16[256,512]{1,0:T(8,128)(2,1)S(1)}, u32[]{:S(2)}, u32[]{:S(2)}) %collective-permute-start.38) | collective-permute-done | bytes 262176 | tf_op jit(solution)/shard_map/ppermute | solution.py:28
  127.3 3.1 %collective-permute-start.28 = (f32[26,512]{1,0:T(8,128)S(1)}, f32[26,512]{1,0:T(8,128)}, u32[]{:S(2)}, u32[]{:S(2)}) collective-permute-start(f32[26,512]{1,0:T(8,128)S(1)} %add_add_fusion.2), channel_id=1, source_target_pairs={{0,16},{4,20},{8,24},{12,28},{16,32},{20,36},{24,40},{28,44},{32,4... | collective-permute-start | bytes 159752 | tf_op jit(solution)/shard_map/ppermute | solution.py:28
  130.3 2.5 %collective-permute-start.29 = (f32[26,512]{1,0:T(8,128)S(1)}, f32[26,512]{1,0:T(8,128)}, u32[]{:S(2)}, u32[]{:S(2)}) collective-permute-start(f32[26,512]{1,0:T(8,128)S(1)} %add_add_fusion.2), channel_id=1, source_target_pairs={{0,32},{4,36},{8,40},{12,44},{16,48},{20,52},{24,56},{28,60},{32,0... | collective-permute-start | bytes 159752 | tf_op jit(solution)/shard_map/ppermute | solution.py:28
  133.1 3.4 %collective-permute-start.30 = (f32[26,512]{1,0:T(8,128)S(1)}, f32[26,512]{1,0:T(8,128)}, u32[]{:S(2)}, u32[]{:S(2)}) collective-permute-start(f32[26,512]{1,0:T(8,128)S(1)} %add_add_fusion.2), channel_id=1, source_target_pairs={{0,48},{4,52},{8,56},{12,60},{16,0},{20,4},{24,8},{28,12},{32,16},... | collective-permute-start | bytes 159752 | tf_op jit(solution)/shard_map/ppermute | solution.py:28
  136.5 3.8 %fusion.8 = bf16[1024,512]{1,0:T(8,128)(2,1)} fusion(bf16[256,1024]{1,0:T(8,128)(2,1)} %collective-permute-done.37, bf16[256,1024]{1,0:T(8,128)(2,1)} %collective-permute-done.36, bf16[256,1024]{1,0:T(8,128)(2,1)} %collective-permute-done.35, bf16[256,1024]{1,0:T(8,128)(2,1)} %collective-permute-done.34, bf16[256,512]{1,0:T(8,128)(2,1)S(1)} %get-tuple-element.44, ...), kind=kOutput, calls=%fused_computation.9 | convolution fusion | flops 1086849024 | bytes 4194304 | tf_op jit(solution)/shard_map/dot_general | solution.py:324
  140.3 8.7 %all-to-all-start = ((bf16[16,64,512]{2,1,0:T(8,128)(2,1)}), bf16[16,64,512]{2,1,0:T(8,128)(2,1)S(1)}, u32[]{:S(2)}, u32[]{:S(2)}) async-start(bf16[16,64,512]{2,1,0:T(8,128)(2,1)} %bitcast.142), calls=%async_computation | async-start | bytes 2097152 | tf_op jit(solution)/shard_map/all_to_all | solution.py:328
  150.7 3.2 %collective-permute-start.32 = (f32[26,512]{1,0:T(8,128)S(1)}, f32[26,512]{1,0:T(8,128)S(1)}, u32[]{:S(2)}, u32[]{:S(2)}) collective-permute-start(f32[26,512]{1,0:T(8,128)S(1)} %add_add_fusion.1), channel_id=1, source_target_pairs={{0,128},{4,132},{8,136},{12,140},{16,144},{20,148},{24,152},{28,15... | collective-permute-start | bytes 159752 | tf_op jit(solution)/shard_map/ppermute | solution.py:28
  156.9 1.3 collective-permute-done.33
  158.5 1.3 copy-done.1
  159.8 1.7 fusion.12
  161.5 3.6 %collective-permute-start.11 = (bf16[256,1024]{1,0:T(8,128)(2,1)S(1)}, bf16[256,1024]{1,0:T(8,128)(2,1)S(1)}, u32[]{:S(2)}, u32[]{:S(2)}) collective-permute-start(bf16[256,1024]{1,0:T(8,128)(2,1)S(1)} %fusion.12), channel_id=1, source_target_pairs={{0,2},{1,3},{2,0},{3,1},{4,6},{5,7},{6,4},{7,5},{8,10},{9,11},{10,... | collective-permute-start | bytes 1572872 | tf_op jit(solution)/shard_map/ppermute | solution.py:32
  167.0 18.5 %collective-permute-done.11 = bf16[256,1024]{1,0:T(8,128)(2,1)S(1)} collective-permute-done((bf16[256,1024]{1,0:T(8,128)(2,1)S(1)}, bf16[256,1024]{1,0:T(8,128)(2,1)S(1)}, u32[]{:S(2)}, u32[]{:S(2)}) %collective-permute-start.11) | collective-permute-done | bytes 524320 | tf_op jit(solution)/shard_map/ppermute | solution.py:32
  185.5 2.8 %fusion.14 = bf16[256,1024]{1,0:T(8,128)(2,1)} fusion(f32[512,1024]{1,0:T(8,128)} %copy-done.1, bf16[256,1024]{1,0:T(8,128)(2,1)S(1)} %collective-permute-done.11, bf16[256,512]{1,0:T(8,128)(2,1)S(1)} %get-tuple-element.47, bf16[512,4096]{1,0:T(8,128)(2,1)} %param.12, s32[]{:T(128)S(6)} %select_n.285), kind=kOutput, calls=%fused_computation.20 | convolution fusion | flops 269484032 | bytes 3407876 | tf_op jit(solution)/shard_map/dot_general | solution.py:307
  (103 shorter events, 24.3 us)
Async XLA Ops:
  0.6 13.8 %copy-start.5 = (bf16[256,3,512]{2,0,1:T(8,128)(2,1)S(1)}, bf16[256,3,512]{2,0,1:T(8,128)(2,1)}, u32[]{:S(2)}) copy-start(bf16[256,3,512]{2,0,1:T(8,128)(2,1)} %param.7) | copy-start | bytes 2359300
  0.6 13.2 %copy-start.9 = (f32[3,3,512]{2,1,0:T(4,128)S(1)}, f32[3,3,512]{2,1,0:T(4,128)}, u32[]{:S(2)}) copy-start(f32[3,3,512]{2,1,0:T(4,128)} %param.8) | copy-start | bytes 55300
  0.7 15.2 %collective-permute-start.12 = (bf16[256,1024]{1,0:T(8,128)(2,1)}, bf16[256,1024]{1,0:T(8,128)(2,1)S(1)}, u32[]{:S(2)}, u32[]{:S(2)}) collective-permute-start(bf16[256,1024]{1,0:T(8,128)(2,1)} %param.13), channel_id=1, source_target_pairs={{0,1},{1,0},{2,3},{3,2},{4,5},{5,4},{6,7},{7,6},{8,9},{9,8},{10,11... | collective-permute-start | bytes 1572872 | tf_op jit(solution)/shard_map/ppermute | solution.py:32
  0.8 15.1 %collective-permute-start.13 = (bf16[256,1024]{1,0:T(8,128)(2,1)}, bf16[256,1024]{1,0:T(8,128)(2,1)}, u32[]{:S(2)}, u32[]{:S(2)}) collective-permute-start(bf16[256,1024]{1,0:T(8,128)(2,1)} %param.13), channel_id=1, source_target_pairs={{0,2},{1,3},{2,0},{3,1},{4,6},{5,7},{6,4},{7,5},{8,10},{9,11},{10,... | collective-permute-start | bytes 1572872 | tf_op jit(solution)/shard_map/ppermute | solution.py:32
  2.8 32.3 %collective-permute-start.34 = (bf16[256,1024]{1,0:T(8,128)(2,1)}, bf16[256,1024]{1,0:T(8,128)(2,1)}, u32[]{:S(2)}, u32[]{:S(2)}) collective-permute-start(bf16[256,1024]{1,0:T(8,128)(2,1)} %param.13), channel_id=1, source_target_pairs={{0,0},{1,64},{2,128},{3,192},{4,4},{5,68},{6,132},{7,196},{8,8},{9... | collective-permute-start | bytes 1572872 | tf_op jit(solution)/shard_map/ppermute | solution.py:269
  8.9 5.5 %collective-permute-start = (bf16[2,3,512]{2,0,1:T(2,128)(2,1)S(1)}, bf16[2,3,512]{2,0,1:T(2,128)(2,1)S(1)}, u32[]{:S(2)}, u32[]{:S(2)}) collective-permute-start(bf16[2,3,512]{2,0,1:T(2,128)(2,1)S(1)} %slice.166), channel_id=1, source_target_pairs={{0,4},{4,8},{8,12},{12,16},{16,20},{20,24},{24,28},{28,32},{32,36}... | collective-permute-start | bytes 18440 | tf_op jit(solution)/shard_map/ppermute | solution.py:37
  15.9 3.3 %collective-permute-start.14 = (bf16[256,1024]{1,0:T(8,128)(2,1)}, bf16[256,1024]{1,0:T(8,128)(2,1)S(1)}, u32[]{:S(2)}, u32[]{:S(2)}) collective-permute-start(bf16[256,1024]{1,0:T(8,128)(2,1)} %collective-permute-done.13), channel_id=1, source_target_pairs={{0,1},{1,0},{2,3},{3,2},{4,5},{5,4},{6,7},{7,6},{8,9},{9,8},{10,11... | collective-permute-start | bytes 1572872 | tf_op jit(solution)/shard_map/ppermute | solution.py:32
  19.1 21.5 %copy-start.2 = (f32[512,16]{0,1:T(8,128)S(1)}, f32[512,16]{0,1:T(8,128)}, u32[]{:S(2)}) copy-start(f32[512,16]{0,1:T(8,128)} %param.10) | copy-start | bytes 98308
  19.2 47.0 %copy-start.8 = (f32[512,16]{0,1:T(8,128)S(1)}, f32[512,16]{0,1:T(8,128)}, u32[]{:S(2)}) copy-start(f32[512,16]{0,1:T(8,128)} %param.9) | copy-start | bytes 98308
  21.4 71.4 %copy-start.3 = (f32[512,16]{0,1:T(8,128)S(1)}, f32[512,16]{0,1:T(8,128)}, u32[]{:S(2)}) copy-start(f32[512,16]{0,1:T(8,128)} %param.10) | copy-start | bytes 98308
  25.1 10.2 %collective-permute-start.1 = (f32[16,512]{1,0:T(8,128)}, f32[16,512]{1,0:T(8,128)S(1)}, u32[]{:S(2)}, u32[]{:S(2)}) collective-permute-start(f32[16,512]{1,0:T(8,128)} %get-tuple-element.13), channel_id=1, source_target_pairs={{0,4},{4,8},{8,12},{12,0},{16,20},{20,24},{24,28},{28,16},{32,36},... | collective-permute-start | bytes 98312 | tf_op jit(solution)/shard_map/ppermute | solution.py:28
  27.1 10.6 %collective-permute-start.2 = (f32[16,512]{1,0:T(8,128)}, f32[16,512]{1,0:T(8,128)S(1)}, u32[]{:S(2)}, u32[]{:S(2)}) collective-permute-start(f32[16,512]{1,0:T(8,128)} %get-tuple-element.13), channel_id=1, source_target_pairs={{0,8},{4,12},{8,0},{12,4},{16,24},{20,28},{24,16},{28,20},{32,40},... | collective-permute-start | bytes 98312 | tf_op jit(solution)/shard_map/ppermute | solution.py:28
  27.5 11.7 %collective-permute-start.3 = (f32[16,512]{1,0:T(8,128)}, f32[16,512]{1,0:T(8,128)S(1)}, u32[]{:S(2)}, u32[]{:S(2)}) collective-permute-start(f32[16,512]{1,0:T(8,128)} %get-tuple-element.13), channel_id=1, source_target_pairs={{0,12},{4,0},{8,4},{12,8},{16,28},{20,16},{24,20},{28,24},{32,44},... | collective-permute-start | bytes 98312 | tf_op jit(solution)/shard_map/ppermute | solution.py:28
  33.8 5.4 %collective-permute-start.15 = (f32[16,512]{1,0:T(8,128)}, f32[16,512]{1,0:T(8,128)S(1)}, u32[]{:S(2)}, u32[]{:S(2)}) collective-permute-start(f32[16,512]{1,0:T(8,128)} %get-tuple-element.15), channel_id=1, source_target_pairs={{0,12},{4,0},{8,4},{12,8},{16,28},{20,16},{24,20},{28,24},{32,44},... | collective-permute-start | bytes 98312 | tf_op jit(solution)/shard_map/ppermute | solution.py:28
  35.0 5.6 %collective-permute-start.16 = (f32[16,512]{1,0:T(8,128)}, f32[16,512]{1,0:T(8,128)S(1)}, u32[]{:S(2)}, u32[]{:S(2)}) collective-permute-start(f32[16,512]{1,0:T(8,128)} %get-tuple-element.15), channel_id=1, source_target_pairs={{0,8},{4,12},{8,0},{12,4},{16,24},{20,28},{24,16},{28,20},{32,40},... | collective-permute-start | bytes 98312 | tf_op jit(solution)/shard_map/ppermute | solution.py:28
  35.4 5.3 %collective-permute-start.17 = (f32[16,512]{1,0:T(8,128)}, f32[16,512]{1,0:T(8,128)S(1)}, u32[]{:S(2)}, u32[]{:S(2)}) collective-permute-start(f32[16,512]{1,0:T(8,128)} %get-tuple-element.15), channel_id=1, source_target_pairs={{0,4},{4,8},{8,12},{12,0},{16,20},{20,24},{24,28},{28,16},{32,36},... | collective-permute-start | bytes 98312 | tf_op jit(solution)/shard_map/ppermute | solution.py:28
  37.7 43.6 %collective-permute-start.36 = (bf16[256,1024]{1,0:T(8,128)(2,1)}, bf16[256,1024]{1,0:T(8,128)(2,1)}, u32[]{:S(2)}, u32[]{:S(2)}) collective-permute-start(bf16[256,1024]{1,0:T(8,128)(2,1)} %collective-permute-done.34), channel_id=1, source_target_pairs={{0,2},{1,3},{2,0},{3,1},{4,6},{5,7},{6,4},{7,5},{8,10},{9,11},{10,... | collective-permute-start | bytes 1572872 | tf_op jit(solution)/shard_map/ppermute | solution.py:32
  41.5 12.9 %collective-permute-start.18 = (f32[16,512]{1,0:T(8,128)S(1)}, f32[16,512]{1,0:T(8,128)S(1)}, u32[]{:S(2)}, u32[]{:S(2)}) collective-permute-start(f32[16,512]{1,0:T(8,128)S(1)} %get-tuple-element.51), channel_id=1, source_target_pairs={{0,48},{4,52},{8,56},{12,60},{16,0},{20,4},{24,8},{28,12},{32,16},... | collective-permute-start | bytes 98312 | tf_op jit(solution)/shard_map/ppermute | solution.py:28
  47.9 13.3 %collective-permute-start.19 = (f32[16,512]{1,0:T(8,128)S(1)}, f32[16,512]{1,0:T(8,128)S(1)}, u32[]{:S(2)}, u32[]{:S(2)}) collective-permute-start(f32[16,512]{1,0:T(8,128)S(1)} %get-tuple-element.51), channel_id=1, source_target_pairs={{0,32},{4,36},{8,40},{12,44},{16,48},{20,52},{24,56},{28,60},{32,0... | collective-permute-start | bytes 98312 | tf_op jit(solution)/shard_map/ppermute | solution.py:28
  48.7 12.5 %collective-permute-start.20 = (f32[16,512]{1,0:T(8,128)S(1)}, f32[16,512]{1,0:T(8,128)S(1)}, u32[]{:S(2)}, u32[]{:S(2)}) collective-permute-start(f32[16,512]{1,0:T(8,128)S(1)} %get-tuple-element.51), channel_id=1, source_target_pairs={{0,16},{4,20},{8,24},{12,28},{16,32},{20,36},{24,40},{28,44},{32,4... | collective-permute-start | bytes 98312 | tf_op jit(solution)/shard_map/ppermute | solution.py:28
  51.3 9.9 %collective-permute-start.4 = (f32[16,512]{1,0:T(8,128)S(1)}, f32[16,512]{1,0:T(8,128)S(1)}, u32[]{:S(2)}, u32[]{:S(2)}) collective-permute-start(f32[16,512]{1,0:T(8,128)S(1)} %get-tuple-element.52), channel_id=1, source_target_pairs={{0,16},{4,20},{8,24},{12,28},{16,32},{20,36},{24,40},{28,44},{32,4... | collective-permute-start | bytes 98312 | tf_op jit(solution)/shard_map/ppermute | solution.py:28
  54.4 7.8 %collective-permute-start.5 = (f32[16,512]{1,0:T(8,128)S(1)}, f32[16,512]{1,0:T(8,128)S(1)}, u32[]{:S(2)}, u32[]{:S(2)}) collective-permute-start(f32[16,512]{1,0:T(8,128)S(1)} %get-tuple-element.52), channel_id=1, source_target_pairs={{0,32},{4,36},{8,40},{12,44},{16,48},{20,52},{24,56},{28,60},{32,0... | collective-permute-start | bytes 98312 | tf_op jit(solution)/shard_map/ppermute | solution.py:28
  61.2 4.9 %collective-permute-start.6 = (f32[16,512]{1,0:T(8,128)S(1)}, f32[16,512]{1,0:T(8,128)S(1)}, u32[]{:S(2)}, u32[]{:S(2)}) collective-permute-start(f32[16,512]{1,0:T(8,128)S(1)} %get-tuple-element.52), channel_id=1, source_target_pairs={{0,48},{4,52},{8,56},{12,60},{16,0},{20,4},{24,8},{28,12},{32,16},... | collective-permute-start | bytes 98312 | tf_op jit(solution)/shard_map/ppermute | solution.py:28
  66.8 15.1 %collective-permute-start.21 = (f32[16,512]{1,0:T(8,128)S(1)}, f32[16,512]{1,0:T(8,128)S(1)}, u32[]{:S(2)}, u32[]{:S(2)}) collective-permute-start(f32[16,512]{1,0:T(8,128)S(1)} %get-tuple-element.48), channel_id=1, source_target_pairs={{0,192},{4,196},{8,200},{12,204},{16,208},{20,212},{24,216},{28,22... | collective-permute-start | bytes 98312 | tf_op jit(solution)/shard_map/ppermute | solution.py:28
  79.7 5.5 %collective-permute-start.22 = (f32[16,512]{1,0:T(8,128)S(1)}, f32[16,512]{1,0:T(8,128)S(1)}, u32[]{:S(2)}, u32[]{:S(2)}) collective-permute-start(f32[16,512]{1,0:T(8,128)S(1)} %get-tuple-element.48), channel_id=1, source_target_pairs={{0,128},{4,132},{8,136},{12,140},{16,144},{20,148},{24,152},{28,15... | collective-permute-start | bytes 98312 | tf_op jit(solution)/shard_map/ppermute | solution.py:28
  79.9 6.4 %collective-permute-start.23 = (f32[16,512]{1,0:T(8,128)S(1)}, f32[16,512]{1,0:T(8,128)S(1)}, u32[]{:S(2)}, u32[]{:S(2)}) collective-permute-start(f32[16,512]{1,0:T(8,128)S(1)} %get-tuple-element.48), channel_id=1, source_target_pairs={{0,64},{4,68},{8,72},{12,76},{16,80},{20,84},{24,88},{28,92},{32,9... | collective-permute-start | bytes 98312 | tf_op jit(solution)/shard_map/ppermute | solution.py:28
  81.3 51.7 %collective-permute-start.35 = (bf16[256,1024]{1,0:T(8,128)(2,1)}, bf16[256,1024]{1,0:T(8,128)(2,1)}, u32[]{:S(2)}, u32[]{:S(2)}) collective-permute-start(bf16[256,1024]{1,0:T(8,128)(2,1)} %collective-permute-done.34), channel_id=1, source_target_pairs={{0,1},{1,0},{2,3},{3,2},{4,5},{5,4},{6,7},{7,6},{8,9},{9,8},{10,11... | collective-permute-start | bytes 1572872 | tf_op jit(solution)/shard_map/ppermute | solution.py:32
  81.3 55.1 %collective-permute-start.37 = (bf16[256,1024]{1,0:T(8,128)(2,1)}, bf16[256,1024]{1,0:T(8,128)(2,1)}, u32[]{:S(2)}, u32[]{:S(2)}) collective-permute-start(bf16[256,1024]{1,0:T(8,128)(2,1)} %collective-permute-done.36), channel_id=1, source_target_pairs={{0,1},{1,0},{2,3},{3,2},{4,5},{5,4},{6,7},{7,6},{8,9},{9,8},{10,11... | collective-permute-start | bytes 1572872 | tf_op jit(solution)/shard_map/ppermute | solution.py:32
  81.9 10.9 %collective-permute-start.7 = (f32[16,512]{1,0:T(8,128)S(1)}, f32[16,512]{1,0:T(8,128)S(1)}, u32[]{:S(2)}, u32[]{:S(2)}) collective-permute-start(f32[16,512]{1,0:T(8,128)S(1)} %get-tuple-element.50), channel_id=1, source_target_pairs={{0,64},{4,68},{8,72},{12,76},{16,80},{20,84},{24,88},{28,92},{32,9... | collective-permute-start | bytes 98312 | tf_op jit(solution)/shard_map/ppermute | solution.py:28
  85.3 7.5 %collective-permute-start.8 = (f32[16,512]{1,0:T(8,128)S(1)}, f32[16,512]{1,0:T(8,128)S(1)}, u32[]{:S(2)}, u32[]{:S(2)}) collective-permute-start(f32[16,512]{1,0:T(8,128)S(1)} %get-tuple-element.50), channel_id=1, source_target_pairs={{0,128},{4,132},{8,136},{12,140},{16,144},{20,148},{24,152},{28,15... | collective-permute-start | bytes 98312 | tf_op jit(solution)/shard_map/ppermute | solution.py:28
  86.3 6.4 %collective-permute-start.9 = (f32[16,512]{1,0:T(8,128)S(1)}, f32[16,512]{1,0:T(8,128)S(1)}, u32[]{:S(2)}, u32[]{:S(2)}) collective-permute-start(f32[16,512]{1,0:T(8,128)S(1)} %get-tuple-element.50), channel_id=1, source_target_pairs={{0,192},{4,196},{8,200},{12,204},{16,208},{20,212},{24,216},{28,22... | collective-permute-start | bytes 98312 | tf_op jit(solution)/shard_map/ppermute | solution.py:28
  101.7 12.5 %collective-permute-start.25 = (f32[26,512]{1,0:T(8,128)S(1)}, f32[26,512]{1,0:T(8,128)S(1)}, u32[]{:S(2)}, u32[]{:S(2)}) collective-permute-start(f32[26,512]{1,0:T(8,128)S(1)} %concatenate.29), channel_id=1, source_target_pairs={{0,4},{4,8},{8,12},{12,0},{16,20},{20,24},{24,28},{28,16},{32,36},... | collective-permute-start | bytes 159752 | tf_op jit(solution)/shard_map/ppermute | solution.py:28
  103.3 12.8 %collective-permute-start.26 = (f32[26,512]{1,0:T(8,128)S(1)}, f32[26,512]{1,0:T(8,128)S(1)}, u32[]{:S(2)}, u32[]{:S(2)}) collective-permute-start(f32[26,512]{1,0:T(8,128)S(1)} %concatenate.29), channel_id=1, source_target_pairs={{0,8},{4,12},{8,0},{12,4},{16,24},{20,28},{24,16},{28,20},{32,40},... | collective-permute-start | bytes 159752 | tf_op jit(solution)/shard_map/ppermute | solution.py:28
  105.0 18.1 %copy-start.11 = (f32[1,1,512]{2,1,0:T(1,128)S(1)}, f32[1,1,512]{2,1,0:T(1,128)}, u32[]{:S(2)}) copy-start(f32[1,1,512]{2,1,0:T(1,128)} %copy-done.10) | copy-start | bytes 6148
  106.7 6.1 %collective-permute-start.24 = (f32[3,2,512]{2,1,0:T(2,128)S(1)}, f32[3,2,512]{2,1,0:T(2,128)S(1)}, u32[]{:S(2)}, u32[]{:S(2)}) collective-permute-start(f32[3,2,512]{2,1,0:T(2,128)S(1)} %pad_maximum_fusion.6), channel_id=1, source_target_pairs={{4,0},{8,4},{12,8},{16,12},{20,16},{24,20},{28,24},{32,28},{36,32}... | collective-permute-start | bytes 36872 | tf_op jit(solution)/shard_map/ppermute | solution.py:37
  112.9 7.3 %collective-permute-start.27 = (f32[26,512]{1,0:T(8,128)S(1)}, f32[26,512]{1,0:T(8,128)S(1)}, u32[]{:S(2)}, u32[]{:S(2)}) collective-permute-start(f32[26,512]{1,0:T(8,128)S(1)} %concatenate.29), channel_id=1, source_target_pairs={{0,12},{4,0},{8,4},{12,8},{16,28},{20,16},{24,20},{28,24},{32,44},... | collective-permute-start | bytes 159752 | tf_op jit(solution)/shard_map/ppermute | solution.py:28
  114.2 13.0 %collective-permute-start.38 = (bf16[256,512]{1,0:T(8,128)(2,1)S(1)}, bf16[256,512]{1,0:T(8,128)(2,1)S(1)}, u32[]{:S(2)}, u32[]{:S(2)}) collective-permute-start(bf16[256,512]{1,0:T(8,128)(2,1)S(1)} %get-tuple-element.47), channel_id=1, source_target_pairs={{0,64},{4,68},{8,72},{12,76},{16,80},{20,84},{24,88},{28,92},{32,9... | collective-permute-start | bytes 786440 | tf_op jit(solution)/shard_map/ppermute | solution.py:28
  116.1 11.2 %collective-permute-start.39 = (bf16[256,512]{1,0:T(8,128)(2,1)S(1)}, bf16[256,512]{1,0:T(8,128)(2,1)S(1)}, u32[]{:S(2)}, u32[]{:S(2)}) collective-permute-start(bf16[256,512]{1,0:T(8,128)(2,1)S(1)} %get-tuple-element.47), channel_id=1, source_target_pairs={{0,128},{4,132},{8,136},{12,140},{16,144},{20,148},{24,152},{28,15... | collective-permute-start | bytes 786440 | tf_op jit(solution)/shard_map/ppermute | solution.py:28
  120.1 10.2 %collective-permute-start.40 = (bf16[256,512]{1,0:T(8,128)(2,1)S(1)}, bf16[256,512]{1,0:T(8,128)(2,1)S(1)}, u32[]{:S(2)}, u32[]{:S(2)}) collective-permute-start(bf16[256,512]{1,0:T(8,128)(2,1)S(1)} %get-tuple-element.47), channel_id=1, source_target_pairs={{0,192},{4,196},{8,200},{12,204},{16,208},{20,212},{24,216},{28,22... | collective-permute-start | bytes 786440 | tf_op jit(solution)/shard_map/ppermute | solution.py:28
  127.3 31.0 %collective-permute-start.10 = (bf16[512,1024]{1,0:T(8,128)(2,1)}, bf16[512,1024]{1,0:T(8,128)(2,1)S(1)}, u32[]{:S(2)}, u32[]{:S(2)}) collective-permute-start(bf16[512,1024]{1,0:T(8,128)(2,1)} %pad_maximum_fusion), channel_id=1, source_target_pairs={{0,1},{1,0},{2,3},{3,2},{4,5},{5,4},{6,7},{7,6},{8,9},{9,8},{10,11... | collective-permute-start | bytes 3145736 | tf_op jit(solution)/shard_map/ppermute | solution.py:32
  127.3 21.9 %collective-permute-start.28 = (f32[26,512]{1,0:T(8,128)S(1)}, f32[26,512]{1,0:T(8,128)}, u32[]{:S(2)}, u32[]{:S(2)}) collective-permute-start(f32[26,512]{1,0:T(8,128)S(1)} %add_add_fusion.2), channel_id=1, source_target_pairs={{0,16},{4,20},{8,24},{12,28},{16,32},{20,36},{24,40},{28,44},{32,4... | collective-permute-start | bytes 159752 | tf_op jit(solution)/shard_map/ppermute | solution.py:28
  130.3 18.9 %collective-permute-start.29 = (f32[26,512]{1,0:T(8,128)S(1)}, f32[26,512]{1,0:T(8,128)}, u32[]{:S(2)}, u32[]{:S(2)}) collective-permute-start(f32[26,512]{1,0:T(8,128)S(1)} %add_add_fusion.2), channel_id=1, source_target_pairs={{0,32},{4,36},{8,40},{12,44},{16,48},{20,52},{24,56},{28,60},{32,0... | collective-permute-start | bytes 159752 | tf_op jit(solution)/shard_map/ppermute | solution.py:28
  133.1 16.1 %collective-permute-start.30 = (f32[26,512]{1,0:T(8,128)S(1)}, f32[26,512]{1,0:T(8,128)}, u32[]{:S(2)}, u32[]{:S(2)}) collective-permute-start(f32[26,512]{1,0:T(8,128)S(1)} %add_add_fusion.2), channel_id=1, source_target_pairs={{0,48},{4,52},{8,56},{12,60},{16,0},{20,4},{24,8},{28,12},{32,16},... | collective-permute-start | bytes 159752 | tf_op jit(solution)/shard_map/ppermute | solution.py:28
  140.3 48.0 %all-to-all-start = ((bf16[16,64,512]{2,1,0:T(8,128)(2,1)}), bf16[16,64,512]{2,1,0:T(8,128)(2,1)S(1)}, u32[]{:S(2)}, u32[]{:S(2)}) async-start(bf16[16,64,512]{2,1,0:T(8,128)(2,1)} %bitcast.142), calls=%async_computation | async-start | bytes 2097152 | tf_op jit(solution)/shard_map/all_to_all | solution.py:328
  150.1 5.6 %collective-permute-start.31 = (f32[26,512]{1,0:T(8,128)S(1)}, f32[26,512]{1,0:T(8,128)S(1)}, u32[]{:S(2)}, u32[]{:S(2)}) collective-permute-start(f32[26,512]{1,0:T(8,128)S(1)} %add_add_fusion.1), channel_id=1, source_target_pairs={{0,64},{4,68},{8,72},{12,76},{16,80},{20,84},{24,88},{28,92},{32,9... | collective-permute-start | bytes 159752 | tf_op jit(solution)/shard_map/ppermute | solution.py:28
  150.7 6.2 %collective-permute-start.32 = (f32[26,512]{1,0:T(8,128)S(1)}, f32[26,512]{1,0:T(8,128)S(1)}, u32[]{:S(2)}, u32[]{:S(2)}) collective-permute-start(f32[26,512]{1,0:T(8,128)S(1)} %add_add_fusion.1), channel_id=1, source_target_pairs={{0,128},{4,132},{8,136},{12,140},{16,144},{20,148},{24,152},{28,15... | collective-permute-start | bytes 159752 | tf_op jit(solution)/shard_map/ppermute | solution.py:28
  153.9 4.3 %collective-permute-start.33 = (f32[26,512]{1,0:T(8,128)S(1)}, f32[26,512]{1,0:T(8,128)S(1)}, u32[]{:S(2)}, u32[]{:S(2)}) collective-permute-start(f32[26,512]{1,0:T(8,128)S(1)} %add_add_fusion.1), channel_id=1, source_target_pairs={{0,192},{4,196},{8,200},{12,204},{16,208},{20,212},{24,216},{28,22... | collective-permute-start | bytes 159752 | tf_op jit(solution)/shard_map/ppermute | solution.py:28
  161.5 24.0 %collective-permute-start.11 = (bf16[256,1024]{1,0:T(8,128)(2,1)S(1)}, bf16[256,1024]{1,0:T(8,128)(2,1)S(1)}, u32[]{:S(2)}, u32[]{:S(2)}) collective-permute-start(bf16[256,1024]{1,0:T(8,128)(2,1)S(1)} %fusion.12), channel_id=1, source_target_pairs={{0,2},{1,3},{2,0},{3,1},{4,6},{5,7},{6,4},{7,5},{8,10},{9,11},{10,... | collective-permute-start | bytes 1572872 | tf_op jit(solution)/shard_map/ppermute | solution.py:32
  (6 other events, 31.0 us)

commit v2 on v1

--- a/solution.py
+++ b/solution.py
@@ -19,12 +19,12 @@
     return (lax.axis_index("seq") // STRIDES[name]) % 4
 
 
-def ring(block, name, step):
+def swap(block, name, mask):
     stride = STRIDES[name]
     route = []
     for source in range(64):
         place = (source // stride) % 4
-        route.append((source, source + ((place + step) % 4 - place) * stride))
+        route.append((source, source + ((place ^ mask) - place) * stride))
     return lax.ppermute(block, "seq", route)
 
 
@@ -205,34 +205,33 @@
     )(signal, other, rate, amp, skip, entry, incoming)
 
 
-def entering(total, rate, rows, reverse):
-    direction = -1 if reverse else 1
+def entering(totals, rate, rows):
     span = rows
-    passed = jnp.zeros((), jnp.int32)
-    result = jnp.zeros_like(total)
+    passed = jnp.zeros((2, 1, 1), jnp.int32)
+    result = jnp.zeros_like(totals)
     for name in ("x", "z", "y"):
         place = digit(name)
-        if reverse:
-            place = 3 - place
-        pieces = [total] + [ring(total, name, direction * k) for k in (1, 2, 3)]
-        before = jnp.zeros_like(total)
-        whole = jnp.zeros_like(total)
-        for k in range(4):
-            if k:
-                fade = jnp.exp(-rate * (span * (k - 1)))
-                before = before + jnp.where(place >= k, fade * pieces[k], 0.0)
-            gap = (3 - (place - k) % 4) * span
-            whole = whole + jnp.exp(-rate * gap.astype(F32)) * pieces[k]
-        result = result + jnp.exp(-rate * passed.astype(F32)) * before
-        passed = passed + place * span
-        total = whole
+        pieces = [totals] + [swap(totals, name, mask) for mask in (1, 2, 3)]
+        outside = jnp.zeros_like(totals)
+        whole = jnp.zeros_like(totals)
+        for mask in range(4):
+            source = place ^ mask
+            if mask:
+                gap = jnp.stack([place - 1 - source, source - 1 - place]).reshape(2, 1, 1)
+                fade = jnp.exp(-rate * (jnp.maximum(gap, 0) * span).astype(F32))
+                outside = outside + jnp.where(gap >= 0, fade * pieces[mask], 0.0)
+            rest = jnp.stack([3 - source, source]).reshape(2, 1, 1)
+            whole = whole + jnp.exp(-rate * (rest * span).astype(F32)) * pieces[mask]
+        result = result + jnp.exp(-rate * passed.astype(F32)) * outside
+        passed = passed + jnp.stack([place, 3 - place]).reshape(2, 1, 1) * span
+        totals = whole
         span = span * 4
     return result
 
 
 def sum_over_seq(block):
     for name in ("x", "z", "y"):
-        pieces = [ring(block, name, k) for k in (1, 2, 3)]
+        pieces = [swap(block, name, mask) for mask in (1, 2, 3)]
         block = (block + pieces[0]) + (pieces[1] + pieces[2])
     return block
 
@@ -251,7 +250,6 @@
     width = out_grad.shape[1]
     grad_scale = 1.0 / math.sqrt(rows * 64)
     ch = lax.axis_index("ch")
-    here = lax.axis_index("seq")
 
     rate = decay_rate.T
     norm = jnp.sqrt(2.0 * rate)
@@ -281,8 +279,6 @@
     product = (keys * values).astype(BF16).astype(F32)
 
     entry, total = local_states(product, rate, False)
-    incoming = entering(total, rate, rows, False)
-
     def weight_block(mask):
         return lax.dynamic_slice_in_dim(out_weight, (ch ^ mask) * width, width, 1)
 
@@ -296,27 +292,26 @@
         )
     gate_grad = (mixed_grad * queries).astype(BF16).astype(F32)
     back_entry, back_total = local_states(gate_grad, rate, True)
+    incoming, back_incoming = entering(jnp.stack([total, back_total]), rate, rows)
 
     gated = forward_apply(product, rate, amp, skip, entry, incoming).astype(BF16).astype(F32)
     mixed_out = (queries * gated).astype(BF16)
     query_grad = mixed_grad * gated
 
-    back_incoming = entering(back_total, rate, rows, True)
-
     def out_block(mask):
         return jnp.dot(mixed_out, weight_block(mask), preferred_element_type=F32)
 
     sent = jnp.concatenate([out_block(1).astype(BF16), out_block(3).astype(BF16)], axis=0)
+    back_incoming, sent = lax.optimization_barrier((back_incoming, sent))
     got = flip_ch(sent, 1).astype(F32)
-    far = flip_ch((out_block(2) + got[rows:]).astype(BF16), 2)
-    block_out = (out_block(0) + got[:rows] + far.astype(F32)).astype(BF16)
+    far_sent = (out_block(2) + got[rows:]).astype(BF16)
 
     turned_pieces = jnp.concatenate(gather_ch(turned), axis=0)
     y_here = digit("y")
-    around = jnp.stack([mixed_out] + [ring(mixed_out, "y", k) for k in (1, 2, 3)], axis=0)
+    around = jnp.stack([mixed_out] + [swap(mixed_out, "y", k) for k in (1, 2, 3)], axis=0)
     mixed_pieces = jnp.concatenate(
         [
-            lax.dynamic_index_in_dim(around, (y_here - (ch ^ mask)) % 4, 0, False)
+            lax.dynamic_index_in_dim(around, y_here ^ ch ^ mask, 0, False)
             for mask in range(4)
         ],
         axis=0,
@@ -347,7 +342,11 @@
             short_terms.append(jnp.sum(filtered_grad[i] * streams[i][start : start + rows], axis=0))
         feature_grad.append(grad.astype(BF16))
     modes = rate.shape[0]
-    sums = sum_over_seq(jnp.concatenate([dots, jnp.stack(short_terms)], axis=0))
+    parts = jnp.concatenate([dots, jnp.stack(short_terms)], axis=0)
+    parts, far_sent = lax.optimization_barrier((parts, far_sent))
+    far = flip_ch(far_sent, 2)
+    block_out = (out_block(0) + got[:rows] + far.astype(F32)).astype(BF16)
+    sums = sum_over_seq(parts)
     residue_grad = (sums[:modes] * norm * grad_scale).T
     skip_grad = sums[modes] * grad_scale
     short_grad = (sums[modes + 1 :] * grad_scale).reshape(3, taps, channels)

time: 191 us -> 190 us (level)
  starting transfers between devices: 92 us -> 75.6 us
  other arithmetic: 12.9 us -> 21.3 us
  waiting for transfers between devices: 43.2 us -> 48.1 us
    ppermute x30 -> x21, starting transfers between devices: 63.3 us -> 45.1 us  [swap(): return lax.ppermute(block, 'seq', route)]
    ppermute x30 -> x21, waiting for transfers between devices: 21.7 us -> 32.9 us  [swap(): return lax.ppermute(block, 'seq', route)]
    another operation x3 -> x4, other arithmetic: 1.48 us -> 6.95 us  [body(): jnp.stack(feature_grad, axis=1)]
    ppermute x8, waiting for transfers between devices: 19.8 us -> 15.1 us  [flip_ch(): return lax.ppermute(block, 'ch', [(i, i ^ mask) for i in range(4)])]
  transfers between devices with their start and end apart: 42 -> 33, of which waited for: 14 -> 11; matrix products, arithmetic and copies ran while one was open for 18% -> 23% of each run, Pallas kernels for 9% -> 9%
where the time goes in v2:
time: 190 us; the launch traced here: 188 us
  starting transfers between devices  75.6 us (40%)
  waiting for transfers between devices  48.1 us (25%)
  other arithmetic  21.3 us (11%)
  matrix products  19.3 us (10%)
  Pallas kernels  17.5 us (9%)
  local copies, waits for them, and re-layouts  5.53 us (3%)
    ppermute x21, starting transfers between devices, swap(): return lax.ppermute(block, 'seq', route)  45.1 us
    ppermute x21, waiting for transfers between devices, swap(): return lax.ppermute(block, 'seq', route)  32.9 us
    ppermute x8, waiting for transfers between devices, flip_ch(): return lax.ppermute(block, 'ch', [(i, i ^ mask) for i in range(4)])  15.1 us
    ppermute x8, starting transfers between devices, flip_ch(): return lax.ppermute(block, 'ch', [(i, i ^ mask) for i in range(4)])  9.38 us
    dot_general x4, matrix products, out_block(): return jnp.dot(mixed_out, weight_block(mask), preferred_element_type=F32)  8.41 us
    all_to_all x1, starting transfers between devices, body(): lax.all_to_all(share, 'seq', split_axis=0, concat_axis=0, axis_index_grou...  8.14 us
    pallas_call x2, Pallas kernels, local_states(): pl.pallas_call(functools.partial(state_kernel, reverse=reverse), grid=(ch...  7.57 us
    ppermute x2, starting transfers between devices, from_behind(): return lax.ppermute(block, 'seq', route)  7.56 us
  transfers between devices with their start and end apart: 33, of which 11 were waited for; matrix products, arithmetic and copies ran while one was open for 23% of the time, Pallas kernels for 9%

profile of v2, /device:TPU:4, one launch (start us, length us, event | category | flops | bytes accessed | tf_op | source)
XLA Modules:
  0.0 188.5 jit_solution(8412701916248368111)
XLA Ops:
  0.7 2.0 %collective-permute-start.2 = (bf16[256,1024]{1,0:T(8,128)(2,1)}, bf16[256,1024]{1,0:T(8,128)(2,1)}, u32[]{:S(2)}, u32[]{:S(2)}) collective-permute-start(bf16[256,1024]{1,0:T(8,128)(2,1)} %param.13), channel_id=1, source_target_pairs={{0,2},{1,3},{2,0},{3,1},{4,6},{5,7},{6,4},{7,5},{8,10},{9,11},{10,... | collective-permute-start | bytes 1572872 | tf_op jit(solution)/shard_map/ppermute | solution.py:32
  2.7 5.3 %collective-permute-start.25 = (bf16[256,1024]{1,0:T(8,128)(2,1)}, bf16[256,1024]{1,0:T(8,128)(2,1)}, u32[]{:S(2)}, u32[]{:S(2)}) collective-permute-start(bf16[256,1024]{1,0:T(8,128)(2,1)} %param.13), channel_id=1, source_target_pairs={{0,0},{1,64},{2,128},{3,192},{4,4},{5,68},{6,132},{7,196},{8,8},{9... | collective-permute-start | bytes 1572872 | tf_op jit(solution)/shard_map/ppermute | solution.py:267
  8.8 3.1 %collective-permute-start = (bf16[2,3,512]{2,0,1:T(2,128)(2,1)S(1)}, bf16[2,3,512]{2,0,1:T(2,128)(2,1)S(1)}, u32[]{:S(2)}, u32[]{:S(2)}) collective-permute-start(bf16[2,3,512]{2,0,1:T(2,128)(2,1)S(1)} %slice.166), channel_id=1, source_target_pairs={{0,4},{4,8},{8,12},{12,16},{16,20},{20,24},{24,28},{28,32},{32,36}... | collective-permute-start | bytes 18440 | tf_op jit(solution)/shard_map/ppermute | solution.py:37
  13.7 1.4 bitcast_multiply_fusion
  15.3 1.8 fusion.33
  17.6 2.0 %convolution_add_fusion.2 = f32[512,256]{0,1:T(8,128)S(1)} fusion(f32[512,256]{0,1:T(8,128)S(1)} %fusion.33, bf16[256,1024]{1,0:T(8,128)(2,1)} %collective-permute-done.1, bf16[512,4096]{1,0:T(8,128)(2,1)} %param.12, s32[]{:T(128)S(6)} %select_n.85), kind=kOutput, calls=%fused_computation.15 | convolution fusion | flops 268566528 | bytes 2621444 | tf_op jit(solution)/shard_map/dot_general | solution.py:287
  19.9 1.5 convolution_add_fusion.1
  21.5 2.0 %fusion.56 = (f32[256,512]{1,0:T(8,128)}, f32[256,512]{1,0:T(8,128)}, f32[256,512]{1,0:T(8,128)}, f32[256,512]{1,0:T(8,128)}, f32[256,512]{1,0:T(8,128)S(1)}, /*index=5*/f32[256,512]{1,0:T(8,128)}) fusion(f32[258,3,512]{2,0,1:T(8,128)S(1)} %maximum_convert_fusion, f32[512]{0:T(512)S(1)} %bitcast.212, f32[512]{0:T(512)S(1)} %bitcast.214, ...), kind=kOutput, calls=%fused_computation.98 | convolution fusion | flops 271319040 | bytes 9979908 | tf_op jit(solution)/shard_map/dot_general | solution.py:287
  23.6 3.8 %shard_map.119 = (f32[16,8,512]{2,1,0:T(8,128)}, f32[16,512]{1,0:T(8,128)}) custom-call(f32[256,512]{1,0:T(8,128)} %get-tuple-element.49.signal_ref, f32[16,512]{1,0:T(8,128)} %bitcast.175), custom_call_target="tpu_custom_call" | custom-call | tf_op jit(solution)/shard_map/pallas_call | solution.py:154
  27.4 3.8 %shard_map.118 = (f32[16,8,512]{2,1,0:T(8,128)}, f32[16,512]{1,0:T(8,128)}) custom-call(f32[256,512]{1,0:T(8,128)} %get-tuple-element.44.signal_ref.other_ref, f32[16,512]{1,0:T(8,128)} %bitcast.176), custom_call_target="tpu_custom_call" | custom-call | tf_op jit(solution)/shard_map/pallas_call | solution.py:154
  32.8 4.4 %collective-permute-start.5 = (f32[2,16,512]{2,1,0:T(8,128)S(1)}, f32[2,16,512]{2,1,0:T(8,128)S(1)}, u32[]{:S(2)}, u32[]{:S(2)}) collective-permute-start(f32[2,16,512]{2,1,0:T(8,128)S(1)} %pad_maximum_fusion.6), channel_id=1, source_target_pairs={{0,8},{4,12},{8,0},{12,4},{16,24},{20,28},{24,16},{28,20},{32,40},... | collective-permute-start | bytes 196616 | tf_op jit(solution)/shard_map/ppermute | solution.py:28
  37.3 2.7 %collective-permute-done.5 = f32[2,16,512]{2,1,0:T(8,128)S(1)} collective-permute-done((f32[2,16,512]{2,1,0:T(8,128)S(1)}, f32[2,16,512]{2,1,0:T(8,128)S(1)}, u32[]{:S(2)}, u32[]{:S(2)}) %collective-permute-start.5) | collective-permute-done | bytes 65568 | tf_op jit(solution)/shard_map/ppermute | solution.py:28
  39.9 1.5 collective-permute-done.4
  42.4 3.2 %collective-permute-start.9 = (f32[2,16,512]{2,1,0:T(8,128)S(1)}, f32[2,16,512]{2,1,0:T(8,128)S(1)}, u32[]{:S(2)}, u32[]{:S(2)}) collective-permute-start(f32[2,16,512]{2,1,0:T(8,128)S(1)} %multiply_add_fusion.5), channel_id=1, source_target_pairs={{0,48},{4,52},{8,56},{12,60},{16,32},{20,36},{24,40},{28,44},{32,1... | collective-permute-start | bytes 196616 | tf_op jit(solution)/shard_map/ppermute | solution.py:28
  45.6 4.0 %collective-permute-start.8 = (f32[2,16,512]{2,1,0:T(8,128)S(1)}, f32[2,16,512]{2,1,0:T(8,128)S(1)}, u32[]{:S(2)}, u32[]{:S(2)}) collective-permute-start(f32[2,16,512]{2,1,0:T(8,128)S(1)} %multiply_add_fusion.5), channel_id=1, source_target_pairs={{0,32},{4,36},{8,40},{12,44},{16,48},{20,52},{24,56},{28,60},{32,0... | collective-permute-start | bytes 196616 | tf_op jit(solution)/shard_map/ppermute | solution.py:28
  49.7 6.2 %collective-permute-done.8 = f32[2,16,512]{2,1,0:T(8,128)S(1)} collective-permute-done((f32[2,16,512]{2,1,0:T(8,128)S(1)}, f32[2,16,512]{2,1,0:T(8,128)S(1)}, u32[]{:S(2)}, u32[]{:S(2)}) %collective-permute-start.8) | collective-permute-done | bytes 65568 | tf_op jit(solution)/shard_map/ppermute | solution.py:28
  56.3 11.6 %collective-permute-start.12 = (f32[2,16,512]{2,1,0:T(8,128)S(1)}, f32[2,16,512]{2,1,0:T(8,128)S(1)}, u32[]{:S(2)}, u32[]{:S(2)}) collective-permute-start(f32[2,16,512]{2,1,0:T(8,128)S(1)} %multiply_add_fusion.4), channel_id=1, source_target_pairs={{0,192},{4,196},{8,200},{12,204},{16,208},{20,212},{24,216},{28,22... | collective-permute-start | bytes 196616 | tf_op jit(solution)/shard_map/ppermute | solution.py:28
  67.9 1.5 collective-permute-start.11
  70.2 3.5 %collective-permute-done.11 = f32[2,16,512]{2,1,0:T(8,128)S(1)} collective-permute-done((f32[2,16,512]{2,1,0:T(8,128)S(1)}, f32[2,16,512]{2,1,0:T(8,128)S(1)}, u32[]{:S(2)}, u32[]{:S(2)}) %collective-permute-start.11) | collective-permute-done | bytes 65568 | tf_op jit(solution)/shard_map/ppermute | solution.py:28
  74.6 4.4 %shard_map.120 = f32[256,512]{1,0:T(8,128)} custom-call(f32[256,512]{1,0:T(8,128)} %get-tuple-element.44.signal_ref.other_ref, f32[16,512]{1,0:T(8,128)} %bitcast.177, f32[16,512]{1,0:T(8,128)} %get-tuple-element.57.amp_ref, f32[1,512]{1,0:T(1,128)} %bitcast.187, f32[16,8,512]{2,1,0:T(8,128)} %get-tuple-element.16.entry_ref, ...), custom_call_target="tpu_custom_call" | custom-call | tf_op jit(solution)/shard_map/pallas_call | solution.py:169
  79.0 1.1 fusion.52
  80.1 1.7 convolution_convert_fusion
  81.7 1.7 convolution_convert_fusion.1
  83.4 1.1 pad_maximum_fusion
  84.5 5.5 %shard_map.121 = (f32[256,512]{1,0:T(8,128)}, f32[17,512]{1,0:T(8,128)}) custom-call(f32[256,512]{1,0:T(8,128)} %get-tuple-element.49.signal_ref, f32[256,512]{1,0:T(8,128)} %get-tuple-element.44.signal_ref.other_ref, f32[16,512]{1,0:T(8,128)} %bitcast.178, f32[16,512]{1,0:T(8,128)} %get-tuple-element.57.amp_ref, f32[1,512]{1,0:T(1,128)} %bitcast.188, ...), custom_call_target="tpu_custom_call" | custom-call | tf_op jit(solution)/shard_map/pallas_call | solution.py:188
  90.0 2.7 %multiply_reduce_fusion = (f32[512]{0:T(512)}, f32[512]{0:T(512)}, f32[512]{0:T(512)}, f32[512]{0:T(512)}, f32[512]{0:T(512)}, /*index=5*/f32[512]{0:T(512)}, f3...) fusion(f32[258,3,512]{2,0,1:T(8,128)S(1)} %maximum_convert_fusi, ...), kind=kLoop, calls=%fused_computation.84 | loop fusion | flops 3272192 | bytes 8931328 | tf_op jit(solution)/shard_map/reduce_sum | solution.py:342
  93.6 4.5 %collective-permute-start.15 = (f32[3,2,512]{2,1,0:T(2,128)S(1)}, f32[3,2,512]{2,1,0:T(2,128)S(1)}, u32[]{:S(2)}, u32[]{:S(2)}) collective-permute-start(f32[3,2,512]{2,1,0:T(2,128)S(1)} %pad_maximum_fusion.7), channel_id=1, source_target_pairs={{4,0},{8,4},{12,8},{16,12},{20,16},{24,20},{28,24},{32,28},{36,32}... | collective-permute-start | bytes 36872 | tf_op jit(solution)/shard_map/ppermute | solution.py:37
  98.2 1.3 collective-permute-start.31
  100.4 1.5 concatenate.141
  101.8 2.1 %collective-permute-start.29 = (bf16[256,512]{1,0:T(8,128)(2,1)S(1)}, bf16[256,512]{1,0:T(8,128)(2,1)S(1)}, u32[]{:S(2)}, u32[]{:S(2)}) collective-permute-start(bf16[256,512]{1,0:T(8,128)(2,1)S(1)} %fusion.52), channel_id=1, source_target_pairs={{0,64},{4,68},{8,72},{12,76},{16,80},{20,84},{24,88},{28,92},{32,9... | collective-permute-start | bytes 786440 | tf_op jit(solution)/shard_map/ppermute | solution.py:28
  103.9 1.6 fusion.60
  105.5 1.5 fusion.59
  107.0 5.5 %collective-permute-done.27 = bf16[256,1024]{1,0:T(8,128)(2,1)} collective-permute-done((bf16[256,1024]{1,0:T(8,128)(2,1)}, bf16[256,1024]{1,0:T(8,128)(2,1)}, u32[]{:S(2)}, u32[]{:S(2)}) %collective-permute-start.27) | collective-permute-done | bytes 524320 | tf_op jit(solution)/shard_map/ppermute | solution.py:32
  114.4 1.5 convert_element_type.247
  115.8 2.5 %fusion.12 = bf16[256,1024]{1,0:T(8,128)(2,1)} fusion(f32[512,1024]{1,0:T(8,128)S(1)} %convert_element_type.247, bf16[256,512]{1,0:T(8,128)(2,1)S(1)} %fusion.52, bf16[512,4096]{1,0:T(8,128)(2,1)} %param.12, s32[]{:T(128)S(6)} %select_n.86), kind=kOutput, calls=%fused_computation.17 | convolution fusion | flops 268959744 | bytes 2883588 | tf_op jit(solution)/shard_map/dot_general | solution.py:302
  118.3 3.5 %collective-permute-start.17 = (f32[26,512]{1,0:T(8,128)S(1)}, f32[26,512]{1,0:T(8,128)}, u32[]{:S(2)}, u32[]{:S(2)}) collective-permute-start(f32[26,512]{1,0:T(8,128)S(1)} %concatenate.141), channel_id=1, source_target_pairs={{0,8},{4,12},{8,0},{12,4},{16,24},{20,28},{24,16},{28,20},{32,40},... | collective-permute-start | bytes 159752 | tf_op jit(solution)/shard_map/ppermute | solution.py:28
  121.8 1.2 collective-permute-start.16
  123.0 3.5 %fusion.8 = bf16[1024,512]{1,0:T(8,128)(2,1)} fusion(bf16[256,1024]{1,0:T(8,128)(2,1)S(1)} %collective-permute-done.28, bf16[256,1024]{1,0:T(8,128)(2,1)} %collective-permute-done.27, bf16[256,1024]{1,0:T(8,128)(2,1)S(1)} %collective-permute-done.26, bf16[256,1024]{1,0:T(8,128)(2,1)} %collective-permute-done.25, bf16[256,512]{1,0:T(8,128)(2,1)S(1)} %get-tuple-element.52, ...), kind=kOutput, calls=%fused_computation.9 | convolution fusion | flops 1086849024 | bytes 4194304 | tf_op jit(solution)/shard_map/dot_general | solution.py:319
  126.5 8.1 %all-to-all-start = ((bf16[16,64,512]{2,1,0:T(8,128)(2,1)}), bf16[16,64,512]{2,1,0:T(8,128)(2,1)S(1)}, u32[]{:S(2)}, u32[]{:S(2)}) async-start(bf16[16,64,512]{2,1,0:T(8,128)(2,1)} %bitcast.179), calls=%async_computation | async-start | bytes 2097152 | tf_op jit(solution)/shard_map/all_to_all | solution.py:323
  135.6 5.5 %collective-permute-start.20 = (f32[26,512]{1,0:T(8,128)S(1)}, f32[26,512]{1,0:T(8,128)S(1)}, u32[]{:S(2)}, u32[]{:S(2)}) collective-permute-start(f32[26,512]{1,0:T(8,128)S(1)} %add_add_fusion.2), channel_id=1, source_target_pairs={{0,32},{4,36},{8,40},{12,44},{16,48},{20,52},{24,56},{28,60},{32,0... | collective-permute-start | bytes 159752 | tf_op jit(solution)/shard_map/ppermute | solution.py:28
  142.2 1.8 fusion.58
  144.1 16.4 %collective-permute-done.20 = f32[26,512]{1,0:T(8,128)S(1)} collective-permute-done((f32[26,512]{1,0:T(8,128)S(1)}, f32[26,512]{1,0:T(8,128)S(1)}, u32[]{:S(2)}, u32[]{:S(2)}) %collective-permute-start.20) | collective-permute-done | bytes 53280 | tf_op jit(solution)/shard_map/ppermute | solution.py:28
  160.5 2.0 %collective-permute-start.23 = (f32[26,512]{1,0:T(8,128)S(1)}, f32[26,512]{1,0:T(8,128)S(1)}, u32[]{:S(2)}, u32[]{:S(2)}) collective-permute-start(f32[26,512]{1,0:T(8,128)S(1)} %add_add_fusion.1), channel_id=1, source_target_pairs={{0,128},{4,132},{8,136},{12,140},{16,144},{20,148},{24,152},{28,15... | collective-permute-start | bytes 159752 | tf_op jit(solution)/shard_map/ppermute | solution.py:28
  162.5 2.0 %collective-permute-start.24 = (f32[26,512]{1,0:T(8,128)S(1)}, f32[26,512]{1,0:T(8,128)S(1)}, u32[]{:S(2)}, u32[]{:S(2)}) collective-permute-start(f32[26,512]{1,0:T(8,128)S(1)} %add_add_fusion.1), channel_id=1, source_target_pairs={{0,192},{4,196},{8,200},{12,204},{16,208},{20,212},{24,216},{28,22... | collective-permute-start | bytes 159752 | tf_op jit(solution)/shard_map/ppermute | solution.py:28
  164.5 2.0 %pad_maximum_fusion.2 = bf16[256,3,512]{2,0,1:T(8,128)(2,1)} fusion(bf16[256,1,512]{2,0,1:T(8,128)(2,1)} %fusion.60, bf16[256,1,512]{2,0,1:T(8,128)(2,1)} %fusion.59, bf16[256,1,512]{2,0,1:T(8,128)(2,1)S(1)} %fusion.58), kind=kLoop, calls=%fused_computation.42 | loop fusion | flops 786432 | bytes 1572864 | tf_op jit(solution)/shard_map/stack | solution.py:355
  166.5 7.1 %collective-permute-start.14 = (bf16[256,1024]{1,0:T(8,128)(2,1)}, bf16[256,1024]{1,0:T(8,128)(2,1)}, u32[]{:S(2)}, u32[]{:S(2)}) collective-permute-start(bf16[256,1024]{1,0:T(8,128)(2,1)} %fusion.12), channel_id=1, source_target_pairs={{0,2},{1,3},{2,0},{3,1},{4,6},{5,7},{6,4},{7,5},{8,10},{9,11},{10,... | collective-permute-start | bytes 1572872 | tf_op jit(solution)/shard_map/ppermute | solution.py:32
  175.5 9.6 %collective-permute-done.14 = bf16[256,1024]{1,0:T(8,128)(2,1)} collective-permute-done((bf16[256,1024]{1,0:T(8,128)(2,1)}, bf16[256,1024]{1,0:T(8,128)(2,1)}, u32[]{:S(2)}, u32[]{:S(2)}) %collective-permute-start.14) | collective-permute-done | bytes 524320 | tf_op jit(solution)/shard_map/ppermute | solution.py:32
  185.1 2.6 %fusion.14 = bf16[256,1024]{1,0:T(8,128)(2,1)} fusion(f32[512,1024]{1,0:T(8,128)S(1)} %convert_element_type.247, bf16[256,1024]{1,0:T(8,128)(2,1)} %collective-permute-done.14, bf16[256,512]{1,0:T(8,128)(2,1)S(1)} %fusion.52, bf16[512,4096]{1,0:T(8,128)(2,1)} %param.12, s32[]{:T(128)S(6)} %select_n.84), kind=kOutput, calls=%fused_computation.20 | convolution fusion | flops 269484032 | bytes 3407876 | tf_op jit(solution)/shard_map/dot_general | solution.py:302
  (116 shorter events, 16.4 us)
Async XLA Ops:
  0.6 16.6 %copy-start.4 = (bf16[256,3,512]{2,0,1:T(8,128)(2,1)S(1)}, bf16[256,3,512]{2,0,1:T(8,128)(2,1)}, u32[]{:S(2)}) copy-start(bf16[256,3,512]{2,0,1:T(8,128)(2,1)} %param.7) | copy-start | bytes 2359300
  0.6 17.0 %collective-permute-start.1 = (bf16[256,1024]{1,0:T(8,128)(2,1)}, bf16[256,1024]{1,0:T(8,128)(2,1)}, u32[]{:S(2)}, u32[]{:S(2)}) collective-permute-start(bf16[256,1024]{1,0:T(8,128)(2,1)} %param.13), channel_id=1, source_target_pairs={{0,1},{1,0},{2,3},{3,2},{4,5},{5,4},{6,7},{7,6},{8,9},{9,8},{10,11... | collective-permute-start | bytes 1572872 | tf_op jit(solution)/shard_map/ppermute | solution.py:32
  0.7 16.8 %collective-permute-start.2 = (bf16[256,1024]{1,0:T(8,128)(2,1)}, bf16[256,1024]{1,0:T(8,128)(2,1)}, u32[]{:S(2)}, u32[]{:S(2)}) collective-permute-start(bf16[256,1024]{1,0:T(8,128)(2,1)} %param.13), channel_id=1, source_target_pairs={{0,2},{1,3},{2,0},{3,1},{4,6},{5,7},{6,4},{7,5},{8,10},{9,11},{10,... | collective-permute-start | bytes 1572872 | tf_op jit(solution)/shard_map/ppermute | solution.py:32
  2.7 95.3 %collective-permute-start.25 = (bf16[256,1024]{1,0:T(8,128)(2,1)}, bf16[256,1024]{1,0:T(8,128)(2,1)}, u32[]{:S(2)}, u32[]{:S(2)}) collective-permute-start(bf16[256,1024]{1,0:T(8,128)(2,1)} %param.13), channel_id=1, source_target_pairs={{0,0},{1,64},{2,128},{3,192},{4,4},{5,68},{6,132},{7,196},{8,8},{9... | collective-permute-start | bytes 1572872 | tf_op jit(solution)/shard_map/ppermute | solution.py:267
  8.8 8.4 %collective-permute-start = (bf16[2,3,512]{2,0,1:T(2,128)(2,1)S(1)}, bf16[2,3,512]{2,0,1:T(2,128)(2,1)S(1)}, u32[]{:S(2)}, u32[]{:S(2)}) collective-permute-start(bf16[2,3,512]{2,0,1:T(2,128)(2,1)S(1)} %slice.166), channel_id=1, source_target_pairs={{0,4},{4,8},{8,12},{12,16},{16,20},{20,24},{24,28},{28,32},{32,36}... | collective-permute-start | bytes 18440 | tf_op jit(solution)/shard_map/ppermute | solution.py:37
  13.6 7.9 %copy-start.6 = (f32[1,1,512]{2,1,0:T(1,128)}, f32[1,1,512]{2,1,0:T(1,128)S(1)}, u32[]{:S(2)}) copy-start(f32[1,1,512]{2,1,0:T(1,128)S(1)} %get-tuple-element.64) | copy-start | bytes 6148
  13.6 7.9 %copy-start.8 = (f32[1,1,512]{2,1,0:T(1,128)}, f32[1,1,512]{2,1,0:T(1,128)S(1)}, u32[]{:S(2)}) copy-start(f32[1,1,512]{2,1,0:T(1,128)S(1)} %get-tuple-element.65) | copy-start | bytes 6148
  13.6 7.9 %copy-start.10 = (f32[1,1,512]{2,1,0:T(1,128)}, f32[1,1,512]{2,1,0:T(1,128)S(1)}, u32[]{:S(2)}) copy-start(f32[1,1,512]{2,1,0:T(1,128)S(1)} %get-tuple-element.66) | copy-start | bytes 6148
  13.6 7.9 %copy-start.12 = (f32[1,1,512]{2,1,0:T(1,128)}, f32[1,1,512]{2,1,0:T(1,128)S(1)}, u32[]{:S(2)}) copy-start(f32[1,1,512]{2,1,0:T(1,128)S(1)} %get-tuple-element.60) | copy-start | bytes 6148
  13.6 7.9 %copy-start.13 = (f32[1,1,512]{2,1,0:T(1,128)}, f32[1,1,512]{2,1,0:T(1,128)S(1)}, u32[]{:S(2)}) copy-start(f32[1,1,512]{2,1,0:T(1,128)S(1)} %get-tuple-element.62) | copy-start | bytes 6148
  13.6 7.9 %copy-start.14 = (f32[1,1,512]{2,1,0:T(1,128)}, f32[1,1,512]{2,1,0:T(1,128)S(1)}, u32[]{:S(2)}) copy-start(f32[1,1,512]{2,1,0:T(1,128)S(1)} %get-tuple-element.63) | copy-start | bytes 6148
  13.7 7.9 %copy-start.15 = (f32[1,1,512]{2,1,0:T(1,128)}, f32[1,1,512]{2,1,0:T(1,128)S(1)}, u32[]{:S(2)}) copy-start(f32[1,1,512]{2,1,0:T(1,128)S(1)} %get-tuple-element.61) | copy-start | bytes 6148
  13.7 7.9 %copy-start.16 = (f32[1,1,512]{2,1,0:T(1,128)}, f32[1,1,512]{2,1,0:T(1,128)S(1)}, u32[]{:S(2)}) copy-start(f32[1,1,512]{2,1,0:T(1,128)S(1)} %get-tuple-element.67) | copy-start | bytes 6148
  13.7 7.9 %copy-start.17 = (f32[1,1,512]{2,1,0:T(1,128)}, f32[1,1,512]{2,1,0:T(1,128)S(1)}, u32[]{:S(2)}) copy-start(f32[1,1,512]{2,1,0:T(1,128)S(1)} %get-tuple-element.68) | copy-start | bytes 6148
  17.5 3.9 %collective-permute-start.3 = (bf16[256,1024]{1,0:T(8,128)(2,1)}, bf16[256,1024]{1,0:T(8,128)(2,1)S(1)}, u32[]{:S(2)}, u32[]{:S(2)}) collective-permute-start(bf16[256,1024]{1,0:T(8,128)(2,1)} %collective-permute-done.2), channel_id=1, source_target_pairs={{0,1},{1,0},{2,3},{3,2},{4,5},{5,4},{6,7},{7,6},{8,9},{9,8},{10,11... | collective-permute-start | bytes 1572872 | tf_op jit(solution)/shard_map/ppermute | solution.py:32
  31.9 5.3 %collective-permute-start.6 = (f32[2,16,512]{2,1,0:T(8,128)S(1)}, f32[2,16,512]{2,1,0:T(8,128)S(1)}, u32[]{:S(2)}, u32[]{:S(2)}) collective-permute-start(f32[2,16,512]{2,1,0:T(8,128)S(1)} %pad_maximum_fusion.6), channel_id=1, source_target_pairs={{0,12},{4,8},{8,4},{12,0},{16,28},{20,24},{24,20},{28,16},{32,44},... | collective-permute-start | bytes 196616 | tf_op jit(solution)/shard_map/ppermute | solution.py:28
  32.8 7.2 %collective-permute-start.5 = (f32[2,16,512]{2,1,0:T(8,128)S(1)}, f32[2,16,512]{2,1,0:T(8,128)S(1)}, u32[]{:S(2)}, u32[]{:S(2)}) collective-permute-start(f32[2,16,512]{2,1,0:T(8,128)S(1)} %pad_maximum_fusion.6), channel_id=1, source_target_pairs={{0,8},{4,12},{8,0},{12,4},{16,24},{20,28},{24,16},{28,20},{32,40},... | collective-permute-start | bytes 196616 | tf_op jit(solution)/shard_map/ppermute | solution.py:28
  37.2 4.3 %collective-permute-start.4 = (f32[2,16,512]{2,1,0:T(8,128)S(1)}, f32[2,16,512]{2,1,0:T(8,128)S(1)}, u32[]{:S(2)}, u32[]{:S(2)}) collective-permute-start(f32[2,16,512]{2,1,0:T(8,128)S(1)} %pad_maximum_fusion.6), channel_id=1, source_target_pairs={{0,4},{4,0},{8,12},{12,8},{16,20},{20,16},{24,28},{28,24},{32,36},... | collective-permute-start | bytes 196616 | tf_op jit(solution)/shard_map/ppermute | solution.py:28
  42.4 7.3 %collective-permute-start.9 = (f32[2,16,512]{2,1,0:T(8,128)S(1)}, f32[2,16,512]{2,1,0:T(8,128)S(1)}, u32[]{:S(2)}, u32[]{:S(2)}) collective-permute-start(f32[2,16,512]{2,1,0:T(8,128)S(1)} %multiply_add_fusion.5), channel_id=1, source_target_pairs={{0,48},{4,52},{8,56},{12,60},{16,32},{20,36},{24,40},{28,44},{32,1... | collective-permute-start | bytes 196616 | tf_op jit(solution)/shard_map/ppermute | solution.py:28
  45.6 10.3 %collective-permute-start.8 = (f32[2,16,512]{2,1,0:T(8,128)S(1)}, f32[2,16,512]{2,1,0:T(8,128)S(1)}, u32[]{:S(2)}, u32[]{:S(2)}) collective-permute-start(f32[2,16,512]{2,1,0:T(8,128)S(1)} %multiply_add_fusion.5), channel_id=1, source_target_pairs={{0,32},{4,36},{8,40},{12,44},{16,48},{20,52},{24,56},{28,60},{32,0... | collective-permute-start | bytes 196616 | tf_op jit(solution)/shard_map/ppermute | solution.py:28
  49.6 6.6 %collective-permute-start.7 = (f32[2,16,512]{2,1,0:T(8,128)S(1)}, f32[2,16,512]{2,1,0:T(8,128)S(1)}, u32[]{:S(2)}, u32[]{:S(2)}) collective-permute-start(f32[2,16,512]{2,1,0:T(8,128)S(1)} %multiply_add_fusion.5), channel_id=1, source_target_pairs={{0,16},{4,20},{8,24},{12,28},{16,0},{20,4},{24,8},{28,12},{32,48},... | collective-permute-start | bytes 196616 | tf_op jit(solution)/shard_map/ppermute | solution.py:28
  56.3 13.9 %collective-permute-start.12 = (f32[2,16,512]{2,1,0:T(8,128)S(1)}, f32[2,16,512]{2,1,0:T(8,128)S(1)}, u32[]{:S(2)}, u32[]{:S(2)}) collective-permute-start(f32[2,16,512]{2,1,0:T(8,128)S(1)} %multiply_add_fusion.4), channel_id=1, source_target_pairs={{0,192},{4,196},{8,200},{12,204},{16,208},{20,212},{24,216},{28,22... | collective-permute-start | bytes 196616 | tf_op jit(solution)/shard_map/ppermute | solution.py:28
  67.9 5.8 %collective-permute-start.11 = (f32[2,16,512]{2,1,0:T(8,128)S(1)}, f32[2,16,512]{2,1,0:T(8,128)S(1)}, u32[]{:S(2)}, u32[]{:S(2)}) collective-permute-start(f32[2,16,512]{2,1,0:T(8,128)S(1)} %multiply_add_fusion.4), channel_id=1, source_target_pairs={{0,128},{4,132},{8,136},{12,140},{16,144},{20,148},{24,152},{28,15... | collective-permute-start | bytes 196616 | tf_op jit(solution)/shard_map/ppermute | solution.py:28
  69.4 4.3 %collective-permute-start.10 = (f32[2,16,512]{2,1,0:T(8,128)S(1)}, f32[2,16,512]{2,1,0:T(8,128)S(1)}, u32[]{:S(2)}, u32[]{:S(2)}) collective-permute-start(f32[2,16,512]{2,1,0:T(8,128)S(1)} %multiply_add_fusion.4), channel_id=1, source_target_pairs={{0,64},{4,68},{8,72},{12,76},{16,80},{20,84},{24,88},{28,92},{32,9... | collective-permute-start | bytes 196616 | tf_op jit(solution)/shard_map/ppermute | solution.py:28
  84.5 29.9 %collective-permute-start.13 = (bf16[512,1024]{1,0:T(8,128)(2,1)}, bf16[512,1024]{1,0:T(8,128)(2,1)}, u32[]{:S(2)}, u32[]{:S(2)}) collective-permute-start(bf16[512,1024]{1,0:T(8,128)(2,1)} %pad_maximum_fusion), channel_id=1, source_target_pairs={{0,1},{1,0},{2,3},{3,2},{4,5},{5,4},{6,7},{7,6},{8,9},{9,8},{10,11... | collective-permute-start | bytes 3145736 | tf_op jit(solution)/shard_map/ppermute | solution.py:32
  90.0 10.4 %copy-start.5 = (f32[17,512]{1,0:T(8,128)S(1)}, f32[17,512]{1,0:T(8,128)}, u32[]{:S(2)}) copy-start(f32[17,512]{1,0:T(8,128)} %get-tuple-element.22) | copy-start | bytes 104452
  93.6 8.3 %collective-permute-start.15 = (f32[3,2,512]{2,1,0:T(2,128)S(1)}, f32[3,2,512]{2,1,0:T(2,128)S(1)}, u32[]{:S(2)}, u32[]{:S(2)}) collective-permute-start(f32[3,2,512]{2,1,0:T(2,128)S(1)} %pad_maximum_fusion.7), channel_id=1, source_target_pairs={{4,0},{8,4},{12,8},{16,12},{20,16},{24,20},{28,24},{32,28},{36,32}... | collective-permute-start | bytes 36872 | tf_op jit(solution)/shard_map/ppermute | solution.py:37
  98.1 14.5 %collective-permute-start.27 = (bf16[256,1024]{1,0:T(8,128)(2,1)}, bf16[256,1024]{1,0:T(8,128)(2,1)}, u32[]{:S(2)}, u32[]{:S(2)}) collective-permute-start(bf16[256,1024]{1,0:T(8,128)(2,1)} %collective-permute-done.25), channel_id=1, source_target_pairs={{0,2},{1,3},{2,0},{3,1},{4,6},{5,7},{6,4},{7,5},{8,10},{9,11},{10,... | collective-permute-start | bytes 1572872 | tf_op jit(solution)/shard_map/ppermute | solution.py:32
  98.2 15.3 %collective-permute-start.31 = (bf16[256,512]{1,0:T(8,128)(2,1)S(1)}, bf16[256,512]{1,0:T(8,128)(2,1)S(1)}, u32[]{:S(2)}, u32[]{:S(2)}) collective-permute-start(bf16[256,512]{1,0:T(8,128)(2,1)S(1)} %fusion.52), channel_id=1, source_target_pairs={{0,192},{4,196},{8,200},{12,204},{16,208},{20,212},{24,216},{28,22... | collective-permute-start | bytes 786440 | tf_op jit(solution)/shard_map/ppermute | solution.py:28
  99.5 14.0 %collective-permute-start.30 = (bf16[256,512]{1,0:T(8,128)(2,1)S(1)}, bf16[256,512]{1,0:T(8,128)(2,1)S(1)}, u32[]{:S(2)}, u32[]{:S(2)}) collective-permute-start(bf16[256,512]{1,0:T(8,128)(2,1)S(1)} %fusion.52), channel_id=1, source_target_pairs={{0,128},{4,132},{8,136},{12,140},{16,144},{20,148},{24,152},{28,15... | collective-permute-start | bytes 786440 | tf_op jit(solution)/shard_map/ppermute | solution.py:28
  101.8 12.3 %collective-permute-start.29 = (bf16[256,512]{1,0:T(8,128)(2,1)S(1)}, bf16[256,512]{1,0:T(8,128)(2,1)S(1)}, u32[]{:S(2)}, u32[]{:S(2)}) collective-permute-start(bf16[256,512]{1,0:T(8,128)(2,1)S(1)} %fusion.52), channel_id=1, source_target_pairs={{0,64},{4,68},{8,72},{12,76},{16,80},{20,84},{24,88},{28,92},{32,9... | collective-permute-start | bytes 786440 | tf_op jit(solution)/shard_map/ppermute | solution.py:28
  112.5 10.5 %collective-permute-start.26 = (bf16[256,1024]{1,0:T(8,128)(2,1)}, bf16[256,1024]{1,0:T(8,128)(2,1)S(1)}, u32[]{:S(2)}, u32[]{:S(2)}) collective-permute-start(bf16[256,1024]{1,0:T(8,128)(2,1)} %collective-permute-done.25), channel_id=1, source_target_pairs={{0,1},{1,0},{2,3},{3,2},{4,5},{5,4},{6,7},{7,6},{8,9},{9,8},{10,11... | collective-permute-start | bytes 1572872 | tf_op jit(solution)/shard_map/ppermute | solution.py:32
  113.5 9.5 %collective-permute-start.28 = (bf16[256,1024]{1,0:T(8,128)(2,1)}, bf16[256,1024]{1,0:T(8,128)(2,1)S(1)}, u32[]{:S(2)}, u32[]{:S(2)}) collective-permute-start(bf16[256,1024]{1,0:T(8,128)(2,1)} %collective-permute-done.27), channel_id=1, source_target_pairs={{0,1},{1,0},{2,3},{3,2},{4,5},{5,4},{6,7},{7,6},{8,9},{9,8},{10,11... | collective-permute-start | bytes 1572872 | tf_op jit(solution)/shard_map/ppermute | solution.py:32
  118.3 16.4 %collective-permute-start.17 = (f32[26,512]{1,0:T(8,128)S(1)}, f32[26,512]{1,0:T(8,128)}, u32[]{:S(2)}, u32[]{:S(2)}) collective-permute-start(f32[26,512]{1,0:T(8,128)S(1)} %concatenate.141), channel_id=1, source_target_pairs={{0,8},{4,12},{8,0},{12,4},{16,24},{20,28},{24,16},{28,20},{32,40},... | collective-permute-start | bytes 159752 | tf_op jit(solution)/shard_map/ppermute | solution.py:28
  121.8 12.9 %collective-permute-start.18 = (f32[26,512]{1,0:T(8,128)S(1)}, f32[26,512]{1,0:T(8,128)}, u32[]{:S(2)}, u32[]{:S(2)}) collective-permute-start(f32[26,512]{1,0:T(8,128)S(1)} %concatenate.141), channel_id=1, source_target_pairs={{0,12},{4,8},{8,4},{12,0},{16,28},{20,24},{24,20},{28,16},{32,44},... | collective-permute-start | bytes 159752 | tf_op jit(solution)/shard_map/ppermute | solution.py:28
  121.8 12.9 %collective-permute-start.16 = (f32[26,512]{1,0:T(8,128)S(1)}, f32[26,512]{1,0:T(8,128)}, u32[]{:S(2)}, u32[]{:S(2)}) collective-permute-start(f32[26,512]{1,0:T(8,128)S(1)} %concatenate.141), channel_id=1, source_target_pairs={{0,4},{4,0},{8,12},{12,8},{16,20},{20,16},{24,28},{28,24},{32,36},... | collective-permute-start | bytes 159752 | tf_op jit(solution)/shard_map/ppermute | solution.py:28
  126.5 15.7 %copy-start.7 = (f32[1,1,512]{2,1,0:T(1,128)S(1)}, f32[1,1,512]{2,1,0:T(1,128)}, u32[]{:S(2)}) copy-start(f32[1,1,512]{2,1,0:T(1,128)} %copy-done.6) | copy-start | bytes 6148
  126.5 15.7 %copy-start.9 = (f32[1,1,512]{2,1,0:T(1,128)S(1)}, f32[1,1,512]{2,1,0:T(1,128)}, u32[]{:S(2)}) copy-start(f32[1,1,512]{2,1,0:T(1,128)} %copy-done.8) | copy-start | bytes 6148
  126.5 15.7 %copy-start.11 = (f32[1,1,512]{2,1,0:T(1,128)S(1)}, f32[1,1,512]{2,1,0:T(1,128)}, u32[]{:S(2)}) copy-start(f32[1,1,512]{2,1,0:T(1,128)} %copy-done.10) | copy-start | bytes 6148
  126.5 61.2 %all-to-all-start = ((bf16[16,64,512]{2,1,0:T(8,128)(2,1)}), bf16[16,64,512]{2,1,0:T(8,128)(2,1)S(1)}, u32[]{:S(2)}, u32[]{:S(2)}) async-start(bf16[16,64,512]{2,1,0:T(8,128)(2,1)} %bitcast.179), calls=%async_computation | async-start | bytes 2097152 | tf_op jit(solution)/shard_map/all_to_all | solution.py:323
  134.7 40.2 %copy-start.3 = (f32[512,16]{0,1:T(8,128)S(1)}, f32[512,16]{0,1:T(8,128)}, u32[]{:S(2)}) copy-start(f32[512,16]{0,1:T(8,128)} %param.10) | copy-start | bytes 98308
  135.6 24.9 %collective-permute-start.20 = (f32[26,512]{1,0:T(8,128)S(1)}, f32[26,512]{1,0:T(8,128)S(1)}, u32[]{:S(2)}, u32[]{:S(2)}) collective-permute-start(f32[26,512]{1,0:T(8,128)S(1)} %add_add_fusion.2), channel_id=1, source_target_pairs={{0,32},{4,36},{8,40},{12,44},{16,48},{20,52},{24,56},{28,60},{32,0... | collective-permute-start | bytes 159752 | tf_op jit(solution)/shard_map/ppermute | solution.py:28
  141.1 19.4 %collective-permute-start.21 = (f32[26,512]{1,0:T(8,128)S(1)}, f32[26,512]{1,0:T(8,128)S(1)}, u32[]{:S(2)}, u32[]{:S(2)}) collective-permute-start(f32[26,512]{1,0:T(8,128)S(1)} %add_add_fusion.2), channel_id=1, source_target_pairs={{0,48},{4,52},{8,56},{12,60},{16,32},{20,36},{24,40},{28,44},{32,1... | collective-permute-start | bytes 159752 | tf_op jit(solution)/shard_map/ppermute | solution.py:28
  141.6 18.8 %collective-permute-start.19 = (f32[26,512]{1,0:T(8,128)S(1)}, f32[26,512]{1,0:T(8,128)S(1)}, u32[]{:S(2)}, u32[]{:S(2)}) collective-permute-start(f32[26,512]{1,0:T(8,128)S(1)} %add_add_fusion.2), channel_id=1, source_target_pairs={{0,16},{4,20},{8,24},{12,28},{16,0},{20,4},{24,8},{28,12},{32,48},... | collective-permute-start | bytes 159752 | tf_op jit(solution)/shard_map/ppermute | solution.py:28
  160.5 13.1 %collective-permute-start.23 = (f32[26,512]{1,0:T(8,128)S(1)}, f32[26,512]{1,0:T(8,128)S(1)}, u32[]{:S(2)}, u32[]{:S(2)}) collective-permute-start(f32[26,512]{1,0:T(8,128)S(1)} %add_add_fusion.1), channel_id=1, source_target_pairs={{0,128},{4,132},{8,136},{12,140},{16,144},{20,148},{24,152},{28,15... | collective-permute-start | bytes 159752 | tf_op jit(solution)/shard_map/ppermute | solution.py:28
  162.5 11.1 %collective-permute-start.24 = (f32[26,512]{1,0:T(8,128)S(1)}, f32[26,512]{1,0:T(8,128)S(1)}, u32[]{:S(2)}, u32[]{:S(2)}) collective-permute-start(f32[26,512]{1,0:T(8,128)S(1)} %add_add_fusion.1), channel_id=1, source_target_pairs={{0,192},{4,196},{8,200},{12,204},{16,208},{20,212},{24,216},{28,22... | collective-permute-start | bytes 159752 | tf_op jit(solution)/shard_map/ppermute | solution.py:28
  164.5 9.1 %collective-permute-start.22 = (f32[26,512]{1,0:T(8,128)S(1)}, f32[26,512]{1,0:T(8,128)S(1)}, u32[]{:S(2)}, u32[]{:S(2)}) collective-permute-start(f32[26,512]{1,0:T(8,128)S(1)} %add_add_fusion.1), channel_id=1, source_target_pairs={{0,64},{4,68},{8,72},{12,76},{16,80},{20,84},{24,88},{28,92},{32,9... | collective-permute-start | bytes 159752 | tf_op jit(solution)/shard_map/ppermute | solution.py:28
  166.5 18.6 %collective-permute-start.14 = (bf16[256,1024]{1,0:T(8,128)(2,1)}, bf16[256,1024]{1,0:T(8,128)(2,1)}, u32[]{:S(2)}, u32[]{:S(2)}) collective-permute-start(bf16[256,1024]{1,0:T(8,128)(2,1)} %fusion.12), channel_id=1, source_target_pairs={{0,2},{1,3},{2,0},{3,1},{4,6},{5,7},{6,4},{7,5},{8,10},{9,11},{10,... | collective-permute-start | bytes 1572872 | tf_op jit(solution)/shard_map/ppermute | solution.py:32
  (3 other events, 10.0 us)

commit v3 on v2

--- a/solution.py
+++ b/solution.py
@@ -229,11 +229,9 @@
     return result
 
 
-def sum_over_seq(block):
-    for name in ("x", "z", "y"):
-        pieces = [swap(block, name, mask) for mask in (1, 2, 3)]
-        block = (block + pieces[0]) + (pieces[1] + pieces[2])
-    return block
+def sum_along(block, name):
+    pieces = [swap(block, name, mask) for mask in (1, 2, 3)]
+    return (block + pieces[0]) + (pieces[1] + pieces[2])
 
 
 def gather_ch(block):
@@ -264,7 +262,8 @@
         s, j = divmod(source, 4)
         y = s // 16
         route.append((source, (s - 16 * y + 16 * j) * 4 + y))
-    turned = lax.ppermute(out_grad, ("seq", "ch"), route)
+    before, held_grad = lax.optimization_barrier((before, out_grad))
+    turned = lax.ppermute(held_grad, ("seq", "ch"), route)
 
     padded = jnp.concatenate([before, features], axis=0).astype(F32)
     streams = [padded[:, i] for i in range(3)]
@@ -316,16 +315,6 @@
         ],
         axis=0,
     )
-    share = lax.dot_general(
-        turned_pieces, mixed_pieces, (((0,), (0,)), ((), ())), preferred_element_type=F32
-    ).astype(BF16)
-    groups = [[16 * y + i for i in range(16)] for y in range(4)]
-    shares = lax.all_to_all(
-        share, "seq", split_axis=0, concat_axis=0, axis_index_groups=groups, tiled=True
-    )
-    weight_grad = (
-        jnp.sum(shares.reshape(16, width // 16, channels).astype(F32), axis=0) * grad_scale
-    ).astype(BF16)
 
     back, dots = backward_apply(gate_grad, product, rate, amp, skip, back_entry, back_incoming)
     back = back.astype(BF16).astype(F32)
@@ -343,10 +332,24 @@
         feature_grad.append(grad.astype(BF16))
     modes = rate.shape[0]
     parts = jnp.concatenate([dots, jnp.stack(short_terms)], axis=0)
-    parts, far_sent = lax.optimization_barrier((parts, far_sent))
+    parts, mixed_pieces = lax.optimization_barrier((parts, mixed_pieces))
     far = flip_ch(far_sent, 2)
+    share = lax.dot_general(
+        turned_pieces, mixed_pieces, (((0,), (0,)), ((), ())), preferred_element_type=F32
+    ).astype(BF16)
+    sums = sum_along(parts, "x")
+    sums, far = lax.optimization_barrier((sums, far))
     block_out = (out_block(0) + got[:rows] + far.astype(F32)).astype(BF16)
-    sums = sum_over_seq(parts)
+    sums = sum_along(sums, "z")
+    sums, share = lax.optimization_barrier((sums, share))
+    groups = [[16 * y + i for i in range(16)] for y in range(4)]
+    shares = lax.all_to_all(
+        share, "seq", split_axis=0, concat_axis=0, axis_index_groups=groups, tiled=True
+    )
+    weight_grad = (
+        jnp.sum(shares.reshape(16, width // 16, channels).astype(F32), axis=0) * grad_scale
+    ).astype(BF16)
+    sums = sum_along(sums, "y")
     residue_grad = (sums[:modes] * norm * grad_scale).T
     skip_grad = sums[modes] * grad_scale
     short_grad = (sums[modes + 1 :] * grad_scale).reshape(3, taps, channels)

time: 190 us -> 175 us (0.921)
  waiting for transfers between devices: 48.1 us -> 33.8 us
  starting transfers between devices: 75.6 us -> 68.8 us
  other arithmetic: 21.3 us -> 25.2 us
    ppermute x21, waiting for transfers between devices: 32.9 us -> 16.8 us  [swap(): return lax.ppermute(block, 'seq', route)]
    ppermute x8, waiting for transfers between devices: 15.1 us -> 0.43 us  [flip_ch(): return lax.ppermute(block, 'ch', [(i, i ^ mask) for i in range(4)])]
    all_to_all x1, waiting for transfers between devices: 0.01 us -> 13 us  [body(): lax.all_to_all(share, 'seq', split_axis=0, concat_axis=0, axis_index_grou...]
    another operation x4, other arithmetic: 6.95 us -> 1.49 us  [body(): jnp.stack(feature_grad, axis=1)]
    ppermute x1, starting transfers between devices: 5.35 us -> 1.45 us  [body(): turned = lax.ppermute(held_grad, ('seq', 'ch'), route)]
    ppermute x2, waiting for transfers between devices: 0.01 us -> 3.64 us  [from_behind(): return lax.ppermute(block, 'seq', route)]
    convert_element_type x5, other arithmetic: 0.39 us -> 3.31 us  [entering(): fade = jnp.exp(-rate * (jnp.maximum(gap, 0) * span).astype(F32))]
    ppermute x2, starting transfers between devices: 7.56 us -> 5.04 us  [from_behind(): return lax.ppermute(block, 'seq', route)]
  transfers between devices with their start and end apart: 33 -> 33, of which waited for: 11 -> 13; matrix products, arithmetic and copies ran while one was open for 23% -> 26% of each run, Pallas kernels for 9% -> 6%
where the time goes in v3:
time: 175 us; the launch traced here: 172 us
  starting transfers between devices  68.8 us (39%)
  waiting for transfers between devices  33.8 us (19%)
  other arithmetic  25.2 us (14%)
  matrix products  18.1 us (10%)
  Pallas kernels  17.5 us (10%)
  local copies, waits for them, and re-layouts  7.26 us (4%)
    ppermute x21, starting transfers between devices, swap(): return lax.ppermute(block, 'seq', route)  46.6 us
    ppermute x21, waiting for transfers between devices, swap(): return lax.ppermute(block, 'seq', route)  16.8 us
    all_to_all x1, waiting for transfers between devices, body(): lax.all_to_all(share, 'seq', split_axis=0, concat_axis=0, axis_index_grou...  13 us
    all_to_all x1, starting transfers between devices, body(): lax.all_to_all(share, 'seq', split_axis=0, concat_axis=0, axis_index_grou...  8.38 us
    pallas_call x2, Pallas kernels, local_states(): pl.pallas_call(functools.partial(state_kernel, reverse=reverse), grid=(ch...  7.56 us
    dot_general x4, matrix products, out_block(): return jnp.dot(mixed_out, weight_block(mask), preferred_element_type=F32)  7.46 us
    ppermute x8, starting transfers between devices, flip_ch(): return lax.ppermute(block, 'ch', [(i, i ^ mask) for i in range(4)])  7.33 us
    dot_general x4, matrix products, body(): lax.dot_general(grad_pieces[mask], weight_block(mask), (((1,), (1,)), (()...  7.17 us
  transfers between devices with their start and end apart: 33, of which 13 were waited for; matrix products, arithmetic and copies ran while one was open for 26% of the time, Pallas kernels for 6%

profile of v3, /device:TPU:4, one launch (start us, length us, event | category | flops | bytes accessed | tf_op | source)
XLA Modules:
  0.0 172.2 jit_solution(9418160325906561712)
XLA Ops:
  0.7 2.0 %collective-permute-start.2 = (bf16[256,1024]{1,0:T(8,128)(2,1)}, bf16[256,1024]{1,0:T(8,128)(2,1)}, u32[]{:S(2)}, u32[]{:S(2)}) collective-permute-start(bf16[256,1024]{1,0:T(8,128)(2,1)} %param.13), channel_id=1, source_target_pairs={{0,2},{1,3},{2,0},{3,1},{4,6},{5,7},{6,4},{7,5},{8,10},{9,11},{10,... | collective-permute-start | bytes 1572872 | tf_op jit(solution)/shard_map/ppermute | solution.py:32
  3.5 3.1 %collective-permute-start = (bf16[2,3,512]{2,0,1:T(2,128)(2,1)S(1)}, bf16[2,3,512]{2,0,1:T(2,128)(2,1)}, u32[]{:S(2)}, u32[]{:S(2)}) collective-permute-start(bf16[2,3,512]{2,0,1:T(2,128)(2,1)S(1)} %slice.166), channel_id=1, source_target_pairs={{0,4},{4,8},{8,12},{12,16},{16,20},{20,24},{24,28},{28,32},{32,36}... | collective-permute-start | bytes 18440 | tf_op jit(solution)/shard_map/ppermute | solution.py:37
  12.0 1.4 fusion.76
  13.5 1.4 bitcast_multiply_fusion
  16.8 1.8 %fusion.26 = f32[512,256]{0,1:T(8,128)S(1)} fusion(bf16[256,1024]{1,0:T(8,128)(2,1)} %param.13, bf16[512,4096]{1,0:T(8,128)(2,1)} %param.12, s32[]{:T(128)S(6)} %select_n.84), kind=kOutput, calls=%fused_computation.33 | convolution fusion | flops 268435456 | bytes 2097156 | tf_op jit(solution)/shard_map/dot_general | solution.py:286
  20.5 1.8 %convolution_add_fusion.2 = f32[512,256]{0,1:T(8,128)S(1)} fusion(f32[512,256]{0,1:T(8,128)S(1)} %fusion.26, bf16[256,1024]{1,0:T(8,128)(2,1)S(1)} %collective-permute-done.1, bf16[512,4096]{1,0:T(8,128)(2,1)} %param.12, s32[]{:T(128)S(6)} %select_n.85), kind=kOutput, calls=%fused_computation.15 | convolution fusion | flops 268566528 | bytes 2621444 | tf_op jit(solution)/shard_map/dot_general | solution.py:286
  22.2 1.5 convolution_add_fusion.1
  24.0 2.0 %fusion.47 = (f32[256,512]{1,0:T(8,128)}, f32[256,512]{1,0:T(8,128)}, f32[256,512]{1,0:T(8,128)}, f32[256,512]{1,0:T(8,128)}, f32[256,512]{1,0:T(8,128)S(1)}, /*index=5*/f32[256,512]{1,0:T(8,128)}) fusion(f32[258,3,512]{2,0,1:T(8,128)S(1)} %maximum_convert_fusion, f32[512]{0:T(512)S(1)} %bitcast.198, f32[512]{0:T(512)S(1)} %bitcast.200, ...), kind=kOutput, calls=%fused_computation.92 | convolution fusion | flops 271319040 | bytes 9979908 | tf_op jit(solution)/shard_map/dot_general | solution.py:286
  26.1 3.8 %shard_map.118 = (f32[16,8,512]{2,1,0:T(8,128)}, f32[16,512]{1,0:T(8,128)}) custom-call(f32[256,512]{1,0:T(8,128)} %get-tuple-element.56.signal_ref.other_ref, f32[16,512]{1,0:T(8,128)} %bitcast.176), custom_call_target="tpu_custom_call" | custom-call | tf_op jit(solution)/shard_map/pallas_call | solution.py:154
  29.8 3.8 %shard_map.119 = (f32[16,8,512]{2,1,0:T(8,128)}, f32[16,512]{1,0:T(8,128)}) custom-call(f32[256,512]{1,0:T(8,128)} %get-tuple-element.61.signal_ref, f32[16,512]{1,0:T(8,128)} %bitcast.177), custom_call_target="tpu_custom_call" | custom-call | tf_op jit(solution)/shard_map/pallas_call | solution.py:154
  34.4 3.2 %collective-permute-start.4 = (f32[2,16,512]{2,1,0:T(8,128)S(1)}, f32[2,16,512]{2,1,0:T(8,128)S(1)}, u32[]{:S(2)}, u32[]{:S(2)}) collective-permute-start(f32[2,16,512]{2,1,0:T(8,128)S(1)} %pad_maximum_fusion.7), channel_id=1, source_target_pairs={{0,4},{4,0},{8,12},{12,8},{16,20},{20,16},{24,28},{28,24},{32,36},... | collective-permute-start | bytes 196616 | tf_op jit(solution)/shard_map/ppermute | solution.py:28
  37.6 1.6 collective-permute-start.6
  39.2 1.5 collective-permute-start.25
  40.7 2.7 %collective-permute-done.5 = f32[2,16,512]{2,1,0:T(8,128)S(1)} collective-permute-done((f32[2,16,512]{2,1,0:T(8,128)S(1)}, f32[2,16,512]{2,1,0:T(8,128)S(1)}, u32[]{:S(2)}, u32[]{:S(2)}) %collective-permute-start.5) | collective-permute-done | bytes 65568 | tf_op jit(solution)/shard_map/ppermute | solution.py:28
  44.3 3.7 %collective-permute-start.7 = (f32[2,16,512]{2,1,0:T(8,128)S(1)}, f32[2,16,512]{2,1,0:T(8,128)S(1)}, u32[]{:S(2)}, u32[]{:S(2)}) collective-permute-start(f32[2,16,512]{2,1,0:T(8,128)S(1)} %multiply_add_fusion.5), channel_id=1, source_target_pairs={{0,16},{4,20},{8,24},{12,28},{16,0},{20,4},{24,8},{28,12},{32,48},... | collective-permute-start | bytes 196616 | tf_op jit(solution)/shard_map/ppermute | solution.py:28
  48.0 2.7 %collective-permute-start.8 = (f32[2,16,512]{2,1,0:T(8,128)S(1)}, f32[2,16,512]{2,1,0:T(8,128)S(1)}, u32[]{:S(2)}, u32[]{:S(2)}) collective-permute-start(f32[2,16,512]{2,1,0:T(8,128)S(1)} %multiply_add_fusion.5), channel_id=1, source_target_pairs={{0,32},{4,36},{8,40},{12,44},{16,48},{20,52},{24,56},{28,60},{32,0... | collective-permute-start | bytes 196616 | tf_op jit(solution)/shard_map/ppermute | solution.py:28
  51.7 4.8 %collective-permute-done.8 = f32[2,16,512]{2,1,0:T(8,128)S(1)} collective-permute-done((f32[2,16,512]{2,1,0:T(8,128)S(1)}, f32[2,16,512]{2,1,0:T(8,128)S(1)}, u32[]{:S(2)}, u32[]{:S(2)}) %collective-permute-start.8) | collective-permute-done | bytes 65568 | tf_op jit(solution)/shard_map/ppermute | solution.py:28
  56.5 1.4 collective-permute-done.9
  59.1 9.0 %collective-permute-start.11 = (f32[2,16,512]{2,1,0:T(8,128)S(1)}, f32[2,16,512]{2,1,0:T(8,128)S(1)}, u32[]{:S(2)}, u32[]{:S(2)}) collective-permute-start(f32[2,16,512]{2,1,0:T(8,128)S(1)} %multiply_add_fusion.4), channel_id=1, source_target_pairs={{0,128},{4,132},{8,136},{12,140},{16,144},{20,148},{24,152},{28,15... | collective-permute-start | bytes 196616 | tf_op jit(solution)/shard_map/ppermute | solution.py:28
  68.1 3.3 %collective-permute-start.27 = (bf16[256,1024]{1,0:T(8,128)(2,1)}, bf16[256,1024]{1,0:T(8,128)(2,1)}, u32[]{:S(2)}, u32[]{:S(2)}) collective-permute-start(bf16[256,1024]{1,0:T(8,128)(2,1)} %collective-permute-done.25), channel_id=1, source_target_pairs={{0,2},{1,3},{2,0},{3,1},{4,6},{5,7},{6,4},{7,5},{8,10},{9,11},{10,... | collective-permute-start | bytes 1572872 | tf_op jit(solution)/shard_map/ppermute | solution.py:32
  71.6 2.0 %collective-permute-done.12 = f32[2,16,512]{2,1,0:T(8,128)S(1)} collective-permute-done((f32[2,16,512]{2,1,0:T(8,128)S(1)}, f32[2,16,512]{2,1,0:T(8,128)S(1)}, u32[]{:S(2)}, u32[]{:S(2)}) %collective-permute-start.12) | collective-permute-done | bytes 65568 | tf_op jit(solution)/shard_map/ppermute | solution.py:28
  75.2 4.4 %shard_map.120 = f32[256,512]{1,0:T(8,128)} custom-call(f32[256,512]{1,0:T(8,128)} %get-tuple-element.56.signal_ref.other_ref, f32[16,512]{1,0:T(8,128)} %bitcast.178, f32[16,512]{1,0:T(8,128)} %get-tuple-element.69.amp_ref, f32[1,512]{1,0:T(1,128)} %bitcast.185, f32[16,8,512]{2,1,0:T(8,128)} %get-tuple-element.23.entry_ref, ...), custom_call_target="tpu_custom_call" | custom-call | tf_op jit(solution)/shard_map/pallas_call | solution.py:169
  80.8 2.2 %collective-permute-start.15 = (bf16[256,512]{1,0:T(8,128)(2,1)S(1)}, bf16[256,512]{1,0:T(8,128)(2,1)}, u32[]{:S(2)}, u32[]{:S(2)}) collective-permute-start(bf16[256,512]{1,0:T(8,128)(2,1)S(1)} %fusion.43), channel_id=1, source_target_pairs={{0,128},{4,132},{8,136},{12,140},{16,144},{20,148},{24,152},{28,15... | collective-permute-start | bytes 786440 | tf_op jit(solution)/shard_map/ppermute | solution.py:28
  83.0 2.5 %collective-permute-start.16 = (bf16[256,512]{1,0:T(8,128)(2,1)S(1)}, bf16[256,512]{1,0:T(8,128)(2,1)}, u32[]{:S(2)}, u32[]{:S(2)}) collective-permute-start(bf16[256,512]{1,0:T(8,128)(2,1)S(1)} %fusion.43), channel_id=1, source_target_pairs={{0,192},{4,196},{8,200},{12,204},{16,208},{20,212},{24,216},{28,22... | collective-permute-start | bytes 786440 | tf_op jit(solution)/shard_map/ppermute | solution.py:28
  85.5 1.7 convolution_convert_fusion.1
  87.2 1.7 convolution_convert_fusion
  90.0 5.5 %shard_map.121 = (f32[256,512]{1,0:T(8,128)}, f32[17,512]{1,0:T(8,128)}) custom-call(f32[256,512]{1,0:T(8,128)} %get-tuple-element.61.signal_ref, f32[256,512]{1,0:T(8,128)} %get-tuple-element.56.signal_ref.other_ref, f32[16,512]{1,0:T(8,128)} %bitcast.179, f32[16,512]{1,0:T(8,128)} %get-tuple-element.69.amp_ref, f32[1,512]{1,0:T(1,128)} %bitcast.186, ...), custom_call_target="tpu_custom_call" | custom-call | tf_op jit(solution)/shard_map/pallas_call | solution.py:188
  95.5 3.4 %multiply_reduce_fusion = (f32[512]{0:T(512)S(1)}, f32[512]{0:T(512)S(1)}, f32[512]{0:T(512)S(1)}, f32[512]{0:T(512)S(1)}, f32[512]{0:T(512)S(1)}, /*index=5*/f3...) fusion(f32[258,3,512]{2,0,1:T(8,128)S(1)} %maximum_convert_fusi, ...), kind=kLoop, calls=%fused_computation.78 | loop fusion | flops 3272192 | bytes 8931328 | tf_op jit(solution)/shard_map/reduce_sum | solution.py:331
  98.9 1.5 concatenate.141
  101.8 1.2 pad_maximum_fusion.1
  103.2 2.2 %collective-permute-start.17 = (f32[26,512]{1,0:T(8,128)S(1)}, f32[26,512]{1,0:T(8,128)S(1)}, u32[]{:S(2)}, u32[]{:S(2)}) collective-permute-start(f32[26,512]{1,0:T(8,128)S(1)} %concatenate.141), channel_id=1, source_target_pairs={{0,4},{4,0},{8,12},{12,8},{16,20},{20,16},{24,28},{28,24},{32,36},... | collective-permute-start | bytes 159752 | tf_op jit(solution)/shard_map/ppermute | solution.py:28
  105.4 1.5 convert_element_type.247
  106.9 1.3 copy-done.1
  108.2 1.7 fusion.12
  109.9 1.2 collective-permute-start.20
  111.1 1.9 %collective-permute-start.21 = (f32[3,2,512]{2,1,0:T(2,128)S(1)}, f32[3,2,512]{2,1,0:T(2,128)S(1)}, u32[]{:S(2)}, u32[]{:S(2)}) collective-permute-start(f32[3,2,512]{2,1,0:T(2,128)S(1)} %pad_maximum_fusion.8), channel_id=1, source_target_pairs={{4,0},{8,4},{12,8},{16,12},{20,16},{24,20},{28,24},{32,28},{36,32}... | collective-permute-start | bytes 36872 | tf_op jit(solution)/shard_map/ppermute | solution.py:37
  113.1 3.6 %collective-permute-done.21 = f32[3,2,512]{2,1,0:T(2,128)S(1)} collective-permute-done((f32[3,2,512]{2,1,0:T(2,128)S(1)}, f32[3,2,512]{2,1,0:T(2,128)S(1)}, u32[]{:S(2)}, u32[]{:S(2)}) %collective-permute-start.21) | collective-permute-done | bytes 12320 | tf_op jit(solution)/shard_map/ppermute | solution.py:37
  116.7 4.6 %collective-permute-start.19 = (f32[26,512]{1,0:T(8,128)S(1)}, f32[26,512]{1,0:T(8,128)S(1)}, u32[]{:S(2)}, u32[]{:S(2)}) collective-permute-start(f32[26,512]{1,0:T(8,128)S(1)} %concatenate.141), channel_id=1, source_target_pairs={{0,12},{4,8},{8,4},{12,0},{16,28},{20,24},{24,20},{28,16},{32,44},... | collective-permute-start | bytes 159752 | tf_op jit(solution)/shard_map/ppermute | solution.py:28
  121.3 1.2 collective-permute-done.18
  124.0 3.2 %collective-permute-start.22 = (f32[26,512]{1,0:T(8,128)S(1)}, f32[26,512]{1,0:T(8,128)S(1)}, u32[]{:S(2)}, u32[]{:S(2)}) collective-permute-start(f32[26,512]{1,0:T(8,128)S(1)} %add_add_fusion.2), channel_id=1, source_target_pairs={{0,16},{4,20},{8,24},{12,28},{16,0},{20,4},{24,8},{28,12},{32,48},... | collective-permute-start | bytes 159752 | tf_op jit(solution)/shard_map/ppermute | solution.py:28
  127.2 5.0 %collective-permute-start.23 = (f32[26,512]{1,0:T(8,128)S(1)}, f32[26,512]{1,0:T(8,128)S(1)}, u32[]{:S(2)}, u32[]{:S(2)}) collective-permute-start(f32[26,512]{1,0:T(8,128)S(1)} %add_add_fusion.2), channel_id=1, source_target_pairs={{0,32},{4,36},{8,40},{12,44},{16,48},{20,52},{24,56},{28,60},{32,0... | collective-permute-start | bytes 159752 | tf_op jit(solution)/shard_map/ppermute | solution.py:28
  132.2 3.5 %fusion.8 = bf16[1024,512]{1,0:T(8,128)(2,1)} fusion(bf16[1024,512]{1,0:T(8,128)(2,1)S(1)} %pad_maximum_fusion.2, bf16[256,1024]{1,0:T(8,128)(2,1)S(1)} %collective-permute-done.28, bf16[256,1024]{1,0:T(8,128)(2,1)} %collective-permute-done.27, bf16[256,1024]{1,0:T(8,128)(2,1)S(1)} %collective-permute-done.26, bf16[256,1024]{1,0:T(8,128)(2,1)} %collective-permute-done.25), kind=kOutput, calls=%fused_computation.9 | convolution fusion | flops 1082654720 | bytes 4194304 | tf_op jit(solution)/shard_map/dot_general | solution.py:337
  136.0 2.6 %collective-permute-done.24 = f32[26,512]{1,0:T(8,128)S(1)} collective-permute-done((f32[26,512]{1,0:T(8,128)S(1)}, f32[26,512]{1,0:T(8,128)S(1)}, u32[]{:S(2)}, u32[]{:S(2)}) %collective-permute-start.24) | collective-permute-done | bytes 53280 | tf_op jit(solution)/shard_map/ppermute | solution.py:28
  138.6 8.4 %all-to-all-start = ((bf16[16,64,512]{2,1,0:T(8,128)(2,1)}), bf16[16,64,512]{2,1,0:T(8,128)(2,1)S(1)}, u32[]{:S(2)}, u32[]{:S(2)}) async-start(bf16[16,64,512]{2,1,0:T(8,128)(2,1)} %bitcast.180), calls=%async_computation | async-start | bytes 2097152 | tf_op jit(solution)/shard_map/all_to_all | solution.py:346
  148.6 2.5 %collective-permute-start.30 = (f32[26,512]{1,0:T(8,128)S(1)}, f32[26,512]{1,0:T(8,128)S(1)}, u32[]{:S(2)}, u32[]{:S(2)}) collective-permute-start(f32[26,512]{1,0:T(8,128)S(1)} %add_add_fusion.1), channel_id=1, source_target_pairs={{0,128},{4,132},{8,136},{12,140},{16,144},{20,148},{24,152},{28,15... | collective-permute-start | bytes 159752 | tf_op jit(solution)/shard_map/ppermute | solution.py:28
  151.1 2.2 %collective-permute-start.31 = (f32[26,512]{1,0:T(8,128)S(1)}, f32[26,512]{1,0:T(8,128)S(1)}, u32[]{:S(2)}, u32[]{:S(2)}) collective-permute-start(f32[26,512]{1,0:T(8,128)S(1)} %add_add_fusion.1), channel_id=1, source_target_pairs={{0,192},{4,196},{8,200},{12,204},{16,208},{20,212},{24,216},{28,22... | collective-permute-start | bytes 159752 | tf_op jit(solution)/shard_map/ppermute | solution.py:28
  153.3 2.5 %fusion.14 = bf16[256,1024]{1,0:T(8,128)(2,1)} fusion(f32[512,1024]{1,0:T(8,128)S(1)} %copy-done.2, bf16[256,1024]{1,0:T(8,128)(2,1)S(1)} %collective-permute-done.20, bf16[256,512]{1,0:T(8,128)(2,1)S(1)} %fusion.43, bf16[512,4096]{1,0:T(8,128)(2,1)} %param.12, s32[]{:T(128)S(6)} %select_n.84), kind=kOutput, calls=%fused_computation.20 | convolution fusion | flops 269484032 | bytes 3407876 | tf_op jit(solution)/shard_map/dot_general | solution.py:301
  158.5 13.0 %all-to-all-done = bf16[16,64,512]{2,1,0:T(8,128)(2,1)S(1)} async-done(((bf16[16,64,512]{2,1,0:T(8,128)(2,1)}), bf16[16,64,512]{2,1,0:T(8,128)(2,1)S(1)}, u32[]{:S(2)}, u32[]{:S(2)}) %all-to-all-start) | async-done | bytes 1048608 | tf_op jit(solution)/shard_map/all_to_all | solution.py:346
  (161 shorter events, 26.2 us)
Async XLA Ops:
  0.6 18.6 %copy-start.6 = (bf16[256,3,512]{2,0,1:T(8,128)(2,1)S(1)}, bf16[256,3,512]{2,0,1:T(8,128)(2,1)}, u32[]{:S(2)}) copy-start(bf16[256,3,512]{2,0,1:T(8,128)(2,1)} %param.7) | copy-start | bytes 2359300
  0.6 19.8 %collective-permute-start.1 = (bf16[256,1024]{1,0:T(8,128)(2,1)}, bf16[256,1024]{1,0:T(8,128)(2,1)S(1)}, u32[]{:S(2)}, u32[]{:S(2)}) collective-permute-start(bf16[256,1024]{1,0:T(8,128)(2,1)} %param.13), channel_id=1, source_target_pairs={{0,1},{1,0},{2,3},{3,2},{4,5},{5,4},{6,7},{7,6},{8,9},{9,8},{10,11... | collective-permute-start | bytes 1572872 | tf_op jit(solution)/shard_map/ppermute | solution.py:32
  0.7 19.6 %collective-permute-start.2 = (bf16[256,1024]{1,0:T(8,128)(2,1)}, bf16[256,1024]{1,0:T(8,128)(2,1)}, u32[]{:S(2)}, u32[]{:S(2)}) collective-permute-start(bf16[256,1024]{1,0:T(8,128)(2,1)} %param.13), channel_id=1, source_target_pairs={{0,2},{1,3},{2,0},{3,1},{4,6},{5,7},{6,4},{7,5},{8,10},{9,11},{10,... | collective-permute-start | bytes 1572872 | tf_op jit(solution)/shard_map/ppermute | solution.py:32
  3.5 15.7 %collective-permute-start = (bf16[2,3,512]{2,0,1:T(2,128)(2,1)S(1)}, bf16[2,3,512]{2,0,1:T(2,128)(2,1)}, u32[]{:S(2)}, u32[]{:S(2)}) collective-permute-start(bf16[2,3,512]{2,0,1:T(2,128)(2,1)S(1)} %slice.166), channel_id=1, source_target_pairs={{0,4},{4,8},{8,12},{12,16},{16,20},{20,24},{24,28},{28,32},{32,36}... | collective-permute-start | bytes 18440 | tf_op jit(solution)/shard_map/ppermute | solution.py:37
  20.4 3.4 %collective-permute-start.3 = (bf16[256,1024]{1,0:T(8,128)(2,1)}, bf16[256,1024]{1,0:T(8,128)(2,1)S(1)}, u32[]{:S(2)}, u32[]{:S(2)}) collective-permute-start(bf16[256,1024]{1,0:T(8,128)(2,1)} %collective-permute-done.2), channel_id=1, source_target_pairs={{0,1},{1,0},{2,3},{3,2},{4,5},{5,4},{6,7},{7,6},{8,9},{9,8},{10,11... | collective-permute-start | bytes 1572872 | tf_op jit(solution)/shard_map/ppermute | solution.py:32
  23.9 19.5 %copy-start.28 = (f32[2]{0:T(128)S(1)}, f32[2]{0:T(128)}, u32[]{:S(2)}) copy-start(f32[2]{0:T(128)} %get-tuple-element.85) | copy-start | bytes 28
  23.9 19.5 %copy-start.29 = (f32[2]{0:T(128)S(1)}, f32[2]{0:T(128)}, u32[]{:S(2)}) copy-start(f32[2]{0:T(128)} %get-tuple-element.86) | copy-start | bytes 28
  23.9 19.5 %copy-start.30 = (f32[2]{0:T(128)S(1)}, f32[2]{0:T(128)}, u32[]{:S(2)}) copy-start(f32[2]{0:T(128)} %get-tuple-element.87) | copy-start | bytes 28
  23.9 19.5 %copy-start.31 = (f32[2]{0:T(128)S(1)}, f32[2]{0:T(128)}, u32[]{:S(2)}) copy-start(f32[2]{0:T(128)} %get-tuple-element.88) | copy-start | bytes 28
  23.9 34.0 %copy-start.26 = (f32[2]{0:T(128)S(1)}, f32[2]{0:T(128)}, u32[]{:S(2)}) copy-start(f32[2]{0:T(128)} %get-tuple-element.89) | copy-start | bytes 28
  23.9 34.0 %copy-start.27 = (f32[2]{0:T(128)S(1)}, f32[2]{0:T(128)}, u32[]{:S(2)}) copy-start(f32[2]{0:T(128)} %get-tuple-element.90) | copy-start | bytes 28
  24.0 49.6 %copy-start.32 = (pred[2]{0:T(512)(128)(4,1)S(1)}, pred[2]{0:T(512)(128)(4,1)}, u32[]{:S(2)}) copy-start(pred[2]{0:T(512)(128)(4,1)} %get-tuple-element.107) | copy-start | bytes 10
  24.0 49.6 %copy-start.33 = (pred[2]{0:T(512)(128)(4,1)S(1)}, pred[2]{0:T(512)(128)(4,1)}, u32[]{:S(2)}) copy-start(pred[2]{0:T(512)(128)(4,1)} %get-tuple-element.108) | copy-start | bytes 10
  24.0 49.6 %copy-start.34 = (f32[2]{0:T(128)S(1)}, f32[2]{0:T(128)}, u32[]{:S(2)}) copy-start(f32[2]{0:T(128)} %get-tuple-element.97) | copy-start | bytes 28
  24.0 49.6 %copy-start.35 = (f32[2]{0:T(128)S(1)}, f32[2]{0:T(128)}, u32[]{:S(2)}) copy-start(f32[2]{0:T(128)} %get-tuple-element.98) | copy-start | bytes 28
  24.0 49.6 %copy-start.36 = (pred[2]{0:T(512)(128)(4,1)S(1)}, pred[2]{0:T(512)(128)(4,1)}, u32[]{:S(2)}) copy-start(pred[2]{0:T(512)(128)(4,1)} %get-tuple-element.105) | copy-start | bytes 10
  24.0 49.6 %copy-start.37 = (pred[2]{0:T(512)(128)(4,1)S(1)}, pred[2]{0:T(512)(128)(4,1)}, u32[]{:S(2)}) copy-start(pred[2]{0:T(512)(128)(4,1)} %get-tuple-element.106) | copy-start | bytes 10
  24.0 49.6 %copy-start.38 = (f32[2]{0:T(128)S(1)}, f32[2]{0:T(128)}, u32[]{:S(2)}) copy-start(f32[2]{0:T(128)} %get-tuple-element.95) | copy-start | bytes 28
  24.0 49.6 %copy-start.39 = (f32[2]{0:T(128)S(1)}, f32[2]{0:T(128)}, u32[]{:S(2)}) copy-start(f32[2]{0:T(128)} %get-tuple-element.96) | copy-start | bytes 28
  34.4 6.3 %collective-permute-start.4 = (f32[2,16,512]{2,1,0:T(8,128)S(1)}, f32[2,16,512]{2,1,0:T(8,128)S(1)}, u32[]{:S(2)}, u32[]{:S(2)}) collective-permute-start(f32[2,16,512]{2,1,0:T(8,128)S(1)} %pad_maximum_fusion.7), channel_id=1, source_target_pairs={{0,4},{4,0},{8,12},{12,8},{16,20},{20,16},{24,28},{28,24},{32,36},... | collective-permute-start | bytes 196616 | tf_op jit(solution)/shard_map/ppermute | solution.py:28
  37.6 5.8 %collective-permute-start.5 = (f32[2,16,512]{2,1,0:T(8,128)S(1)}, f32[2,16,512]{2,1,0:T(8,128)S(1)}, u32[]{:S(2)}, u32[]{:S(2)}) collective-permute-start(f32[2,16,512]{2,1,0:T(8,128)S(1)} %pad_maximum_fusion.7), channel_id=1, source_target_pairs={{0,8},{4,12},{8,0},{12,4},{16,24},{20,28},{24,16},{28,20},{32,40},... | collective-permute-start | bytes 196616 | tf_op jit(solution)/shard_map/ppermute | solution.py:28
  37.6 5.8 %collective-permute-start.6 = (f32[2,16,512]{2,1,0:T(8,128)S(1)}, f32[2,16,512]{2,1,0:T(8,128)S(1)}, u32[]{:S(2)}, u32[]{:S(2)}) collective-permute-start(f32[2,16,512]{2,1,0:T(8,128)S(1)} %pad_maximum_fusion.7), channel_id=1, source_target_pairs={{0,12},{4,8},{8,4},{12,0},{16,28},{20,24},{24,20},{28,16},{32,44},... | collective-permute-start | bytes 196616 | tf_op jit(solution)/shard_map/ppermute | solution.py:28
  39.2 28.9 %collective-permute-start.25 = (bf16[256,1024]{1,0:T(8,128)(2,1)S(1)}, bf16[256,1024]{1,0:T(8,128)(2,1)}, u32[]{:S(2)}, u32[]{:S(2)}) collective-permute-start(bf16[256,1024]{1,0:T(8,128)(2,1)S(1)} %copy-done.7), channel_id=1, source_target_pairs={{0,0},{1,64},{2,128},{3,192},{4,4},{5,68},{6,132},{7,196},{8,8},{9... | collective-permute-start | bytes 1572872 | tf_op jit(solution)/shard_map/ppermute | solution.py:266
  44.3 7.4 %collective-permute-start.7 = (f32[2,16,512]{2,1,0:T(8,128)S(1)}, f32[2,16,512]{2,1,0:T(8,128)S(1)}, u32[]{:S(2)}, u32[]{:S(2)}) collective-permute-start(f32[2,16,512]{2,1,0:T(8,128)S(1)} %multiply_add_fusion.5), channel_id=1, source_target_pairs={{0,16},{4,20},{8,24},{12,28},{16,0},{20,4},{24,8},{28,12},{32,48},... | collective-permute-start | bytes 196616 | tf_op jit(solution)/shard_map/ppermute | solution.py:28
  48.0 8.6 %collective-permute-start.8 = (f32[2,16,512]{2,1,0:T(8,128)S(1)}, f32[2,16,512]{2,1,0:T(8,128)S(1)}, u32[]{:S(2)}, u32[]{:S(2)}) collective-permute-start(f32[2,16,512]{2,1,0:T(8,128)S(1)} %multiply_add_fusion.5), channel_id=1, source_target_pairs={{0,32},{4,36},{8,40},{12,44},{16,48},{20,52},{24,56},{28,60},{32,0... | collective-permute-start | bytes 196616 | tf_op jit(solution)/shard_map/ppermute | solution.py:28
  50.7 7.3 %collective-permute-start.9 = (f32[2,16,512]{2,1,0:T(8,128)S(1)}, f32[2,16,512]{2,1,0:T(8,128)S(1)}, u32[]{:S(2)}, u32[]{:S(2)}) collective-permute-start(f32[2,16,512]{2,1,0:T(8,128)S(1)} %multiply_add_fusion.5), channel_id=1, source_target_pairs={{0,48},{4,52},{8,56},{12,60},{16,32},{20,36},{24,40},{28,44},{32,1... | collective-permute-start | bytes 196616 | tf_op jit(solution)/shard_map/ppermute | solution.py:28
  58.1 13.4 %collective-permute-start.10 = (f32[2,16,512]{2,1,0:T(8,128)S(1)}, f32[2,16,512]{2,1,0:T(8,128)S(1)}, u32[]{:S(2)}, u32[]{:S(2)}) collective-permute-start(f32[2,16,512]{2,1,0:T(8,128)S(1)} %multiply_add_fusion.4), channel_id=1, source_target_pairs={{0,64},{4,68},{8,72},{12,76},{16,80},{20,84},{24,88},{28,92},{32,9... | collective-permute-start | bytes 196616 | tf_op jit(solution)/shard_map/ppermute | solution.py:28
  59.1 12.5 %collective-permute-start.11 = (f32[2,16,512]{2,1,0:T(8,128)S(1)}, f32[2,16,512]{2,1,0:T(8,128)S(1)}, u32[]{:S(2)}, u32[]{:S(2)}) collective-permute-start(f32[2,16,512]{2,1,0:T(8,128)S(1)} %multiply_add_fusion.4), channel_id=1, source_target_pairs={{0,128},{4,132},{8,136},{12,140},{16,144},{20,148},{24,152},{28,15... | collective-permute-start | bytes 196616 | tf_op jit(solution)/shard_map/ppermute | solution.py:28
  68.1 5.5 %collective-permute-start.12 = (f32[2,16,512]{2,1,0:T(8,128)S(1)}, f32[2,16,512]{2,1,0:T(8,128)S(1)}, u32[]{:S(2)}, u32[]{:S(2)}) collective-permute-start(f32[2,16,512]{2,1,0:T(8,128)S(1)} %multiply_add_fusion.4), channel_id=1, source_target_pairs={{0,192},{4,196},{8,200},{12,204},{16,208},{20,212},{24,216},{28,22... | collective-permute-start | bytes 196616 | tf_op jit(solution)/shard_map/ppermute | solution.py:28
  68.1 33.1 %collective-permute-start.27 = (bf16[256,1024]{1,0:T(8,128)(2,1)}, bf16[256,1024]{1,0:T(8,128)(2,1)}, u32[]{:S(2)}, u32[]{:S(2)}) collective-permute-start(bf16[256,1024]{1,0:T(8,128)(2,1)} %collective-permute-done.25), channel_id=1, source_target_pairs={{0,2},{1,3},{2,0},{3,1},{4,6},{5,7},{6,4},{7,5},{8,10},{9,11},{10,... | collective-permute-start | bytes 1572872 | tf_op jit(solution)/shard_map/ppermute | solution.py:32
  80.7 21.0 %collective-permute-start.14 = (bf16[256,512]{1,0:T(8,128)(2,1)S(1)}, bf16[256,512]{1,0:T(8,128)(2,1)}, u32[]{:S(2)}, u32[]{:S(2)}) collective-permute-start(bf16[256,512]{1,0:T(8,128)(2,1)S(1)} %fusion.43), channel_id=1, source_target_pairs={{0,64},{4,68},{8,72},{12,76},{16,80},{20,84},{24,88},{28,92},{32,9... | collective-permute-start | bytes 786440 | tf_op jit(solution)/shard_map/ppermute | solution.py:28
  80.8 21.0 %collective-permute-start.15 = (bf16[256,512]{1,0:T(8,128)(2,1)S(1)}, bf16[256,512]{1,0:T(8,128)(2,1)}, u32[]{:S(2)}, u32[]{:S(2)}) collective-permute-start(bf16[256,512]{1,0:T(8,128)(2,1)S(1)} %fusion.43), channel_id=1, source_target_pairs={{0,128},{4,132},{8,136},{12,140},{16,144},{20,148},{24,152},{28,15... | collective-permute-start | bytes 786440 | tf_op jit(solution)/shard_map/ppermute | solution.py:28
  83.0 18.8 %collective-permute-start.16 = (bf16[256,512]{1,0:T(8,128)(2,1)S(1)}, bf16[256,512]{1,0:T(8,128)(2,1)}, u32[]{:S(2)}, u32[]{:S(2)}) collective-permute-start(bf16[256,512]{1,0:T(8,128)(2,1)S(1)} %fusion.43), channel_id=1, source_target_pairs={{0,192},{4,196},{8,200},{12,204},{16,208},{20,212},{24,216},{28,22... | collective-permute-start | bytes 786440 | tf_op jit(solution)/shard_map/ppermute | solution.py:28
  90.0 15.5 %collective-permute-start.13 = (bf16[512,1024]{1,0:T(8,128)(2,1)}, bf16[512,1024]{1,0:T(8,128)(2,1)}, u32[]{:S(2)}, u32[]{:S(2)}) collective-permute-start(bf16[512,1024]{1,0:T(8,128)(2,1)} %pad_maximum_fusion), channel_id=1, source_target_pairs={{0,1},{1,0},{2,3},{3,2},{4,5},{5,4},{6,7},{7,6},{8,9},{9,8},{10,11... | collective-permute-start | bytes 3145736 | tf_op jit(solution)/shard_map/ppermute | solution.py:32
  101.2 31.0 %collective-permute-start.26 = (bf16[256,1024]{1,0:T(8,128)(2,1)}, bf16[256,1024]{1,0:T(8,128)(2,1)S(1)}, u32[]{:S(2)}, u32[]{:S(2)}) collective-permute-start(bf16[256,1024]{1,0:T(8,128)(2,1)} %collective-permute-done.25), channel_id=1, source_target_pairs={{0,1},{1,0},{2,3},{3,2},{4,5},{5,4},{6,7},{7,6},{8,9},{9,8},{10,11... | collective-permute-start | bytes 1572872 | tf_op jit(solution)/shard_map/ppermute | solution.py:32
  101.7 30.5 %collective-permute-start.28 = (bf16[256,1024]{1,0:T(8,128)(2,1)}, bf16[256,1024]{1,0:T(8,128)(2,1)S(1)}, u32[]{:S(2)}, u32[]{:S(2)}) collective-permute-start(bf16[256,1024]{1,0:T(8,128)(2,1)} %collective-permute-done.27), channel_id=1, source_target_pairs={{0,1},{1,0},{2,3},{3,2},{4,5},{5,4},{6,7},{7,6},{8,9},{9,8},{10,11... | collective-permute-start | bytes 1572872 | tf_op jit(solution)/shard_map/ppermute | solution.py:32
  103.2 13.5 %collective-permute-start.17 = (f32[26,512]{1,0:T(8,128)S(1)}, f32[26,512]{1,0:T(8,128)S(1)}, u32[]{:S(2)}, u32[]{:S(2)}) collective-permute-start(f32[26,512]{1,0:T(8,128)S(1)} %concatenate.141), channel_id=1, source_target_pairs={{0,4},{4,0},{8,12},{12,8},{16,20},{20,16},{24,28},{28,24},{32,36},... | collective-permute-start | bytes 159752 | tf_op jit(solution)/shard_map/ppermute | solution.py:28
  109.9 14.1 %collective-permute-start.20 = (bf16[256,1024]{1,0:T(8,128)(2,1)S(1)}, bf16[256,1024]{1,0:T(8,128)(2,1)S(1)}, u32[]{:S(2)}, u32[]{:S(2)}) collective-permute-start(bf16[256,1024]{1,0:T(8,128)(2,1)S(1)} %fusion.12), channel_id=1, source_target_pairs={{0,2},{1,3},{2,0},{3,1},{4,6},{5,7},{6,4},{7,5},{8,10},{9,11},{10,... | collective-permute-start | bytes 1572872 | tf_op jit(solution)/shard_map/ppermute | solution.py:32
  111.1 5.6 %collective-permute-start.21 = (f32[3,2,512]{2,1,0:T(2,128)S(1)}, f32[3,2,512]{2,1,0:T(2,128)S(1)}, u32[]{:S(2)}, u32[]{:S(2)}) collective-permute-start(f32[3,2,512]{2,1,0:T(2,128)S(1)} %pad_maximum_fusion.8), channel_id=1, source_target_pairs={{4,0},{8,4},{12,8},{16,12},{20,16},{24,20},{28,24},{32,28},{36,32}... | collective-permute-start | bytes 36872 | tf_op jit(solution)/shard_map/ppermute | solution.py:37
  116.7 5.8 %collective-permute-start.18 = (f32[26,512]{1,0:T(8,128)S(1)}, f32[26,512]{1,0:T(8,128)S(1)}, u32[]{:S(2)}, u32[]{:S(2)}) collective-permute-start(f32[26,512]{1,0:T(8,128)S(1)} %concatenate.141), channel_id=1, source_target_pairs={{0,8},{4,12},{8,0},{12,4},{16,24},{20,28},{24,16},{28,20},{32,40},... | collective-permute-start | bytes 159752 | tf_op jit(solution)/shard_map/ppermute | solution.py:28
  116.7 6.8 %collective-permute-start.19 = (f32[26,512]{1,0:T(8,128)S(1)}, f32[26,512]{1,0:T(8,128)S(1)}, u32[]{:S(2)}, u32[]{:S(2)}) collective-permute-start(f32[26,512]{1,0:T(8,128)S(1)} %concatenate.141), channel_id=1, source_target_pairs={{0,12},{4,8},{8,4},{12,0},{16,28},{20,24},{24,20},{28,16},{32,44},... | collective-permute-start | bytes 159752 | tf_op jit(solution)/shard_map/ppermute | solution.py:28
  124.0 11.8 %collective-permute-start.22 = (f32[26,512]{1,0:T(8,128)S(1)}, f32[26,512]{1,0:T(8,128)S(1)}, u32[]{:S(2)}, u32[]{:S(2)}) collective-permute-start(f32[26,512]{1,0:T(8,128)S(1)} %add_add_fusion.2), channel_id=1, source_target_pairs={{0,16},{4,20},{8,24},{12,28},{16,0},{20,4},{24,8},{28,12},{32,48},... | collective-permute-start | bytes 159752 | tf_op jit(solution)/shard_map/ppermute | solution.py:28
  127.2 8.8 %collective-permute-start.23 = (f32[26,512]{1,0:T(8,128)S(1)}, f32[26,512]{1,0:T(8,128)S(1)}, u32[]{:S(2)}, u32[]{:S(2)}) collective-permute-start(f32[26,512]{1,0:T(8,128)S(1)} %add_add_fusion.2), channel_id=1, source_target_pairs={{0,32},{4,36},{8,40},{12,44},{16,48},{20,52},{24,56},{28,60},{32,0... | collective-permute-start | bytes 159752 | tf_op jit(solution)/shard_map/ppermute | solution.py:28
  132.2 6.4 %collective-permute-start.24 = (f32[26,512]{1,0:T(8,128)S(1)}, f32[26,512]{1,0:T(8,128)S(1)}, u32[]{:S(2)}, u32[]{:S(2)}) collective-permute-start(f32[26,512]{1,0:T(8,128)S(1)} %add_add_fusion.2), channel_id=1, source_target_pairs={{0,48},{4,52},{8,56},{12,60},{16,32},{20,36},{24,40},{28,44},{32,1... | collective-permute-start | bytes 159752 | tf_op jit(solution)/shard_map/ppermute | solution.py:28
  138.6 32.8 %all-to-all-start = ((bf16[16,64,512]{2,1,0:T(8,128)(2,1)}), bf16[16,64,512]{2,1,0:T(8,128)(2,1)S(1)}, u32[]{:S(2)}, u32[]{:S(2)}) async-start(bf16[16,64,512]{2,1,0:T(8,128)(2,1)} %bitcast.180), calls=%async_computation | async-start | bytes 2097152 | tf_op jit(solution)/shard_map/all_to_all | solution.py:346
  148.6 7.2 %collective-permute-start.29 = (f32[26,512]{1,0:T(8,128)S(1)}, f32[26,512]{1,0:T(8,128)S(1)}, u32[]{:S(2)}, u32[]{:S(2)}) collective-permute-start(f32[26,512]{1,0:T(8,128)S(1)} %add_add_fusion.1), channel_id=1, source_target_pairs={{0,64},{4,68},{8,72},{12,76},{16,80},{20,84},{24,88},{28,92},{32,9... | collective-permute-start | bytes 159752 | tf_op jit(solution)/shard_map/ppermute | solution.py:28
  148.6 7.2 %collective-permute-start.30 = (f32[26,512]{1,0:T(8,128)S(1)}, f32[26,512]{1,0:T(8,128)S(1)}, u32[]{:S(2)}, u32[]{:S(2)}) collective-permute-start(f32[26,512]{1,0:T(8,128)S(1)} %add_add_fusion.1), channel_id=1, source_target_pairs={{0,128},{4,132},{8,136},{12,140},{16,144},{20,148},{24,152},{28,15... | collective-permute-start | bytes 159752 | tf_op jit(solution)/shard_map/ppermute | solution.py:28
  151.1 5.5 %collective-permute-start.31 = (f32[26,512]{1,0:T(8,128)S(1)}, f32[26,512]{1,0:T(8,128)S(1)}, u32[]{:S(2)}, u32[]{:S(2)}) collective-permute-start(f32[26,512]{1,0:T(8,128)S(1)} %add_add_fusion.1), channel_id=1, source_target_pairs={{0,192},{4,196},{8,200},{12,204},{16,208},{20,212},{24,216},{28,22... | collective-permute-start | bytes 159752 | tf_op jit(solution)/shard_map/ppermute | solution.py:28
  (25 other events, 243.5 us)

commit v4 on v3

--- a/solution.py
+++ b/solution.py
@@ -278,6 +278,9 @@
     product = (keys * values).astype(BF16).astype(F32)
 
     entry, total = local_states(product, rate, False)
+    total, grad_pieces[2], grad_pieces[3] = lax.optimization_barrier(
+        (total, grad_pieces[2], grad_pieces[3])
+    )
     def weight_block(mask):
         return lax.dynamic_slice_in_dim(out_weight, (ch ^ mask) * width, width, 1)
 
@@ -317,6 +320,8 @@
     )
 
     back, dots = backward_apply(gate_grad, product, rate, amp, skip, back_entry, back_incoming)
+    back, far_sent = lax.optimization_barrier((back, far_sent))
+    far = flip_ch(far_sent, 2)
     back = back.astype(BF16).astype(F32)
     filtered_grad = [query_grad, back * values, back * keys]
     edge = from_behind(jnp.stack([g[: taps - 1] for g in filtered_grad]), -1)
@@ -332,16 +337,10 @@
         feature_grad.append(grad.astype(BF16))
     modes = rate.shape[0]
     parts = jnp.concatenate([dots, jnp.stack(short_terms)], axis=0)
-    parts, mixed_pieces = lax.optimization_barrier((parts, mixed_pieces))
-    far = flip_ch(far_sent, 2)
     share = lax.dot_general(
         turned_pieces, mixed_pieces, (((0,), (0,)), ((), ())), preferred_element_type=F32
     ).astype(BF16)
-    sums = sum_along(parts, "x")
-    sums, far = lax.optimization_barrier((sums, far))
-    block_out = (out_block(0) + got[:rows] + far.astype(F32)).astype(BF16)
-    sums = sum_along(sums, "z")
-    sums, share = lax.optimization_barrier((sums, share))
+    parts, share = lax.optimization_barrier((parts, share))
     groups = [[16 * y + i for i in range(16)] for y in range(4)]
     shares = lax.all_to_all(
         share, "seq", split_axis=0, concat_axis=0, axis_index_groups=groups, tiled=True
@@ -349,7 +348,11 @@
     weight_grad = (
         jnp.sum(shares.reshape(16, width // 16, channels).astype(F32), axis=0) * grad_scale
     ).astype(BF16)
-    sums = sum_along(sums, "y")
+    sums = sum_along(parts, "y")
+    sums, far = lax.optimization_barrier((sums, far))
+    block_out = (out_block(0) + got[:rows] + far.astype(F32)).astype(BF16)
+    sums = sum_along(sums, "x")
+    sums = sum_along(sums, "z")
     residue_grad = (sums[:modes] * norm * grad_scale).T
     skip_grad = sums[modes] * grad_scale
     short_grad = (sums[modes + 1 :] * grad_scale).reshape(3, taps, channels)

time: 175 us -> 167 us (0.954)
  starting transfers between devices: 68.8 us -> 61.3 us
  matrix products: 18.1 us -> 20.3 us
  local copies, waits for them, and re-layouts: 7.26 us -> 5.1 us
    ppermute x8, waiting for transfers between devices: 0.43 us -> 13.6 us  [flip_ch(): return lax.ppermute(block, 'ch', [(i, i ^ mask) for i in range(4)])]
    all_to_all x1, waiting for transfers between devices: 13 us -> 0.01 us  [body(): lax.all_to_all(share, 'seq', split_axis=0, concat_axis=0, axis_index_grou...]
    ppermute x21, starting transfers between devices: 46.6 us -> 39.9 us  [swap(): return lax.ppermute(block, 'seq', route)]
    ppermute x2, waiting for transfers between devices: 3.64 us -> 0.01 us  [from_behind(): return lax.ppermute(block, 'seq', route)]
    ppermute x21, waiting for transfers between devices: 16.8 us -> 20.2 us  [swap(): return lax.ppermute(block, 'seq', route)]
    reduce_sum x1, other arithmetic: 3.45 us -> 1.2 us  [body(): jnp.sum(filtered_grad[i] * streams[i][start:start + rows], axis=0)]
    convert_element_type x0 -> x1, other arithmetic: none -> 2.03 us  [body(): product = (keys * values).astype(BF16).astype(F32)]
  transfers between devices with their start and end apart: 33 -> 33, of which waited for: 13 -> 15; matrix products, arithmetic and copies ran while one was open for 26% -> 25% of each run, Pallas kernels for 6% -> 8%
where the time goes in v4:
time: 167 us; the launch traced here: 164 us
  starting transfers between devices  61.3 us (37%)
  waiting for transfers between devices  33.8 us (20%)
  other arithmetic  24.6 us (15%)
  matrix products  20.3 us (12%)
  Pallas kernels  17.5 us (10%)
  local copies, waits for them, and re-layouts  5.1 us (3%)
    ppermute x21, starting transfers between devices, swap(): return lax.ppermute(block, 'seq', route)  39.9 us
    ppermute x21, waiting for transfers between devices, swap(): return lax.ppermute(block, 'seq', route)  20.2 us
    ppermute x8, waiting for transfers between devices, flip_ch(): return lax.ppermute(block, 'ch', [(i, i ^ mask) for i in range(4)])  13.6 us
    all_to_all x1, starting transfers between devices, body(): lax.all_to_all(share, 'seq', split_axis=0, concat_axis=0, axis_index_grou...  8.79 us
    dot_general x4, matrix products, out_block(): return jnp.dot(mixed_out, weight_block(mask), preferred_element_type=F32)  8.56 us
    dot_general x4, matrix products, body(): lax.dot_general(grad_pieces[mask], weight_block(mask), (((1,), (1,)), (()...  8.23 us
    pallas_call x2, Pallas kernels, local_states(): pl.pallas_call(functools.partial(state_kernel, reverse=reverse), grid=(ch...  7.56 us
    ppermute x8, starting transfers between devices, flip_ch(): return lax.ppermute(block, 'ch', [(i, i ^ mask) for i in range(4)])  5.85 us
  transfers between devices with their start and end apart: 33, of which 15 were waited for; matrix products, arithmetic and copies ran while one was open for 25% of the time, Pallas kernels for 8%

profile of v4, /device:TPU:4, one launch (start us, length us, event | category | flops | bytes accessed | tf_op | source)
XLA Modules:
  0.0 164.0 jit_solution(11313790441899194623)
XLA Ops:
  0.6 2.0 %collective-permute-start.1 = (bf16[256,1024]{1,0:T(8,128)(2,1)}, bf16[256,1024]{1,0:T(8,128)(2,1)}, u32[]{:S(2)}, u32[]{:S(2)}) collective-permute-start(bf16[256,1024]{1,0:T(8,128)(2,1)} %param.13), channel_id=1, source_target_pairs={{0,2},{1,3},{2,0},{3,1},{4,6},{5,7},{6,4},{7,5},{8,10},{9,11},{10,... | collective-permute-start | bytes 1572872 | tf_op jit(solution)/shard_map/ppermute | solution.py:32
  3.4 3.1 %collective-permute-start = (bf16[2,3,512]{2,0,1:T(2,128)(2,1)S(1)}, bf16[2,3,512]{2,0,1:T(2,128)(2,1)}, u32[]{:S(2)}, u32[]{:S(2)}) collective-permute-start(bf16[2,3,512]{2,0,1:T(2,128)(2,1)S(1)} %slice.166), channel_id=1, source_target_pairs={{0,4},{4,8},{8,12},{12,16},{16,20},{20,24},{24,28},{28,32},{32,36}... | collective-permute-start | bytes 18440 | tf_op jit(solution)/shard_map/ppermute | solution.py:37
  11.9 1.4 fusion.85
  13.3 1.4 bitcast_multiply_fusion
  16.7 1.8 %fusion.35 = f32[512,256]{0,1:T(8,128)S(1)} fusion(bf16[256,1024]{1,0:T(8,128)(2,1)} %param.13, bf16[512,4096]{1,0:T(8,128)(2,1)} %param.12, s32[]{:T(128)S(6)} %select_n.84), kind=kOutput, calls=%fused_computation.40 | convolution fusion | flops 268435456 | bytes 2097156 | tf_op jit(solution)/shard_map/dot_general | solution.py:289
  20.5 2.0 %fusion.56 = (f32[256,512]{1,0:T(8,128)}, f32[256,512]{1,0:T(8,128)}, f32[256,512]{1,0:T(8,128)}) fusion(f32[258,3,512]{2,0,1:T(8,128)S(1)} %maximum_convert_fusion, f32[512]{0:T(512)S(1)} %bitcast.200, f32[512]{0:T(512)} %bitcast.202, f32[512]{0:T(512)S(1)} %bitcast.198, f32[512]{0:T(512)S(1)} %bitcast.192, f32[512]{0:T(512)S(1)} %bitcast.194, ...), kind=kLoop, calls=%fused_computation.99 | loop fusion | flops 1703936 | bytes 4730880 | tf_op jit(solution)/shard_map/convert_element_type | solution.py:278
  22.5 3.8 %shard_map.118 = (f32[16,8,512]{2,1,0:T(8,128)}, f32[16,512]{1,0:T(8,128)}) custom-call(f32[256,512]{1,0:T(8,128)} %get-tuple-element.64.signal_ref.other_ref, f32[16,512]{1,0:T(8,128)} %bitcast.175), custom_call_target="tpu_custom_call" | custom-call | tf_op jit(solution)/shard_map/pallas_call | solution.py:154
  26.3 1.7 %fusion.11 = f32[256,512]{1,0:T(8,128)S(1)} fusion(f32[512,256]{0,1:T(8,128)S(1)} %fusion.35, bf16[256,1024]{1,0:T(8,128)(2,1)S(1)} %collective-permute-done.3, bf16[512,4096]{1,0:T(8,128)(2,1)} %param.12, s32[]{:T(128)S(6)} %select_n.85), kind=kOutput, calls=%fused_computation.14 | convolution fusion | flops 268566528 | bytes 2621444 | tf_op jit(solution)/shard_map/dot_general | solution.py:289
  28.0 1.7 %fusion.24 = f32[256,512]{1,0:T(8,128)S(1)} fusion(bf16[256,1024]{1,0:T(8,128)(2,1)S(1)} %collective-permute-done.2, bf16[512,4096]{1,0:T(8,128)(2,1)} %param.12, s32[]{:T(128)S(6)} %select_n.87), kind=kOutput, calls=%fused_computation.31 | convolution fusion | flops 268435456 | bytes 2097156 | tf_op jit(solution)/shard_map/dot_general | solution.py:289
  29.9 3.0 %fusion.57 = (f32[256,512]{1,0:T(8,128)}, f32[256,512]{1,0:T(8,128)S(1)}, f32[256,512]{1,0:T(8,128)}) fusion(f32[258,3,512]{2,0,1:T(8,128)S(1)} %maximum_convert_fusion, f32[512]{0:T(512)S(1)} %bitcast.188, f32[512]{0:T(512)S(1)} %bitcast.190, f32[512]{0:T(512)S(1)} %bitcast.186, f32[256,512]{1,0:T(8,128)S(1)} %fusion.24, f32[256,512]{1,0:T(8,128)S(1)} %fusion.11, ...), kind=kOutput, calls=%fused_computation.100 | convolution fusion | flops 269746176 | bytes 5773316 | tf_op jit(solution)/shard_map/dot_general | solution.py:289
  32.9 3.8 %shard_map.119 = (f32[16,8,512]{2,1,0:T(8,128)}, f32[16,512]{1,0:T(8,128)}) custom-call(f32[256,512]{1,0:T(8,128)} %get-tuple-element.62.signal_ref, f32[16,512]{1,0:T(8,128)} %bitcast.176), custom_call_target="tpu_custom_call" | custom-call | tf_op jit(solution)/shard_map/pallas_call | solution.py:154
  38.3 4.4 %collective-permute-start.5 = (f32[2,16,512]{2,1,0:T(8,128)S(1)}, f32[2,16,512]{2,1,0:T(8,128)S(1)}, u32[]{:S(2)}, u32[]{:S(2)}) collective-permute-start(f32[2,16,512]{2,1,0:T(8,128)S(1)} %pad_maximum_fusion.6), channel_id=1, source_target_pairs={{0,8},{4,12},{8,0},{12,4},{16,24},{20,28},{24,16},{28,20},{32,40},... | collective-permute-start | bytes 196616 | tf_op jit(solution)/shard_map/ppermute | solution.py:28
  42.8 2.8 %collective-permute-done.5 = f32[2,16,512]{2,1,0:T(8,128)S(1)} collective-permute-done((f32[2,16,512]{2,1,0:T(8,128)S(1)}, f32[2,16,512]{2,1,0:T(8,128)S(1)}, u32[]{:S(2)}, u32[]{:S(2)}) %collective-permute-start.5) | collective-permute-done | bytes 65568 | tf_op jit(solution)/shard_map/ppermute | solution.py:28
  45.6 1.4 collective-permute-done.4
  47.9 3.4 %collective-permute-start.9 = (f32[2,16,512]{2,1,0:T(8,128)S(1)}, f32[2,16,512]{2,1,0:T(8,128)S(1)}, u32[]{:S(2)}, u32[]{:S(2)}) collective-permute-start(f32[2,16,512]{2,1,0:T(8,128)S(1)} %multiply_add_fusion.5), channel_id=1, source_target_pairs={{0,48},{4,52},{8,56},{12,60},{16,32},{20,36},{24,40},{28,44},{32,1... | collective-permute-start | bytes 196616 | tf_op jit(solution)/shard_map/ppermute | solution.py:28
  51.3 3.8 %collective-permute-start.8 = (f32[2,16,512]{2,1,0:T(8,128)S(1)}, f32[2,16,512]{2,1,0:T(8,128)S(1)}, u32[]{:S(2)}, u32[]{:S(2)}) collective-permute-start(f32[2,16,512]{2,1,0:T(8,128)S(1)} %multiply_add_fusion.5), channel_id=1, source_target_pairs={{0,32},{4,36},{8,40},{12,44},{16,48},{20,52},{24,56},{28,60},{32,0... | collective-permute-start | bytes 196616 | tf_op jit(solution)/shard_map/ppermute | solution.py:28
  55.9 5.2 %collective-permute-done.8 = f32[2,16,512]{2,1,0:T(8,128)S(1)} collective-permute-done((f32[2,16,512]{2,1,0:T(8,128)S(1)}, f32[2,16,512]{2,1,0:T(8,128)S(1)}, u32[]{:S(2)}, u32[]{:S(2)}) %collective-permute-start.8) | collective-permute-done | bytes 65568 | tf_op jit(solution)/shard_map/ppermute | solution.py:28
  61.7 3.1 %collective-permute-start.12 = (f32[2,16,512]{2,1,0:T(8,128)S(1)}, f32[2,16,512]{2,1,0:T(8,128)S(1)}, u32[]{:S(2)}, u32[]{:S(2)}) collective-permute-start(f32[2,16,512]{2,1,0:T(8,128)S(1)} %multiply_add_fusion.4), channel_id=1, source_target_pairs={{0,192},{4,196},{8,200},{12,204},{16,208},{20,212},{24,216},{28,22... | collective-permute-start | bytes 196616 | tf_op jit(solution)/shard_map/ppermute | solution.py:28
  65.9 1.4 collective-permute-start.14
  67.4 3.1 %collective-permute-done.11 = f32[2,16,512]{2,1,0:T(8,128)S(1)} collective-permute-done((f32[2,16,512]{2,1,0:T(8,128)S(1)}, f32[2,16,512]{2,1,0:T(8,128)S(1)}, u32[]{:S(2)}, u32[]{:S(2)}) %collective-permute-start.11) | collective-permute-done | bytes 65568 | tf_op jit(solution)/shard_map/ppermute | solution.py:28
  70.6 1.0 multiply_add_fusion.3
  72.2 4.4 %shard_map.120 = f32[256,512]{1,0:T(8,128)} custom-call(f32[256,512]{1,0:T(8,128)} %get-tuple-element.64.signal_ref.other_ref, f32[16,512]{1,0:T(8,128)} %bitcast.177, f32[16,512]{1,0:T(8,128)} %get-tuple-element.73.amp_ref, f32[1,512]{1,0:T(1,128)} %bitcast.204, f32[16,8,512]{2,1,0:T(8,128)} %get-tuple-element.26.entry_ref, ...), custom_call_target="tpu_custom_call" | custom-call | tf_op jit(solution)/shard_map/pallas_call | solution.py:169
  76.6 1.1 fusion.52
  77.7 1.7 %convolution_convert_fusion = bf16[256,1024]{1,0:T(8,128)(2,1)S(1)} fusion(bf16[256,512]{1,0:T(8,128)(2,1)S(1)} %fusion.52, bf16[512,4096]{1,0:T(8,128)(2,1)} %param.12, s32[]{:T(128)S(6)} %select_n.87), kind=kOutput, calls=%fused_computation.10 | convolution fusion | flops 268697600 | bytes 1835012 | tf_op jit(solution)/shard_map/dot_general | solution.py:304
  79.4 1.7 %convolution_convert_fusion.1 = bf16[256,1024]{1,0:T(8,128)(2,1)S(1)} fusion(bf16[256,512]{1,0:T(8,128)(2,1)S(1)} %fusion.52, bf16[512,4096]{1,0:T(8,128)(2,1)} %param.12, s32[]{:T(128)S(6)} %select_n.85), kind=kOutput, calls=%fused_computation.11 | convolution fusion | flops 268697600 | bytes 1835012 | tf_op jit(solution)/shard_map/dot_general | solution.py:304
  81.1 1.1 pad_maximum_fusion
  82.2 3.2 %collective-permute-start.16 = (bf16[256,1024]{1,0:T(8,128)(2,1)}, bf16[256,1024]{1,0:T(8,128)(2,1)}, u32[]{:S(2)}, u32[]{:S(2)}) collective-permute-start(bf16[256,1024]{1,0:T(8,128)(2,1)} %collective-permute-done.14), channel_id=1, source_target_pairs={{0,2},{1,3},{2,0},{3,1},{4,6},{5,7},{6,4},{7,5},{8,10},{9,11},{10,... | collective-permute-start | bytes 1572872 | tf_op jit(solution)/shard_map/ppermute | solution.py:32
  85.4 1.2 collective-permute-start.20
  86.6 1.2 collective-permute-start.19
  87.7 1.7 %collective-permute-start.18 = (bf16[256,512]{1,0:T(8,128)(2,1)S(1)}, bf16[256,512]{1,0:T(8,128)(2,1)}, u32[]{:S(2)}, u32[]{:S(2)}) collective-permute-start(bf16[256,512]{1,0:T(8,128)(2,1)S(1)} %fusion.52), channel_id=1, source_target_pairs={{0,64},{4,68},{8,72},{12,76},{16,80},{20,84},{24,88},{28,92},{32,9... | collective-permute-start | bytes 786440 | tf_op jit(solution)/shard_map/ppermute | solution.py:28
  89.5 5.5 %shard_map.121 = (f32[256,512]{1,0:T(8,128)}, f32[17,512]{1,0:T(8,128)}) custom-call(f32[256,512]{1,0:T(8,128)} %get-tuple-element.62.signal_ref, f32[256,512]{1,0:T(8,128)} %get-tuple-element.64.signal_ref.other_ref, f32[16,512]{1,0:T(8,128)} %bitcast.178, f32[16,512]{1,0:T(8,128)} %get-tuple-element.73.amp_ref, f32[1,512]{1,0:T(1,128)} %bitcast.205, ...), custom_call_target="tpu_custom_call" | custom-call | tf_op jit(solution)/shard_map/pallas_call | solution.py:188
  95.0 2.1 %collective-permute-done.16 = bf16[256,1024]{1,0:T(8,128)(2,1)} collective-permute-done((bf16[256,1024]{1,0:T(8,128)(2,1)}, bf16[256,1024]{1,0:T(8,128)(2,1)}, u32[]{:S(2)}, u32[]{:S(2)}) %collective-permute-start.16) | collective-permute-done | bytes 524320 | tf_op jit(solution)/shard_map/ppermute | solution.py:32
  97.1 2.4 %collective-permute-done.20 = bf16[256,512]{1,0:T(8,128)(2,1)S(1)} collective-permute-done((bf16[256,512]{1,0:T(8,128)(2,1)S(1)}, bf16[256,512]{1,0:T(8,128)(2,1)S(1)}, u32[]{:S(2)}, u32[]{:S(2)}) %collective-permute-start.20) | collective-permute-done | bytes 262176 | tf_op jit(solution)/shard_map/ppermute | solution.py:28
  100.2 1.1 pad_maximum_fusion.1
  101.6 1.3 copy-done
  103.0 2.6 %fusion.13 = bf16[256,1024]{1,0:T(8,128)(2,1)} fusion(f32[512,1024]{1,0:T(8,128)S(1)} %convert_element_type.247, bf16[256,512]{1,0:T(8,128)(2,1)S(1)} %fusion.52, bf16[512,4096]{1,0:T(8,128)(2,1)} %param.12, s32[]{:T(128)S(6)} %select_n.86), kind=kOutput, calls=%fused_computation.17 | convolution fusion | flops 268959744 | bytes 2883588 | tf_op jit(solution)/shard_map/dot_general | solution.py:304
  105.6 1.2 multiply_reduce_fusion
  106.9 2.3 %collective-permute-start.25 = (f32[3,2,512]{2,1,0:T(2,128)S(1)}, f32[3,2,512]{2,1,0:T(2,128)S(1)}, u32[]{:S(2)}, u32[]{:S(2)}) collective-permute-start(f32[3,2,512]{2,1,0:T(2,128)S(1)} %pad_maximum_fusion.7), channel_id=1, source_target_pairs={{4,0},{8,4},{12,8},{16,12},{20,16},{24,20},{28,24},{32,28},{36,32}... | collective-permute-start | bytes 36872 | tf_op jit(solution)/shard_map/ppermute | solution.py:37
  109.3 3.5 %fusion.8 = bf16[1024,512]{1,0:T(8,128)(2,1)} fusion(bf16[256,1024]{1,0:T(8,128)(2,1)S(1)} %collective-permute-done.17, bf16[256,1024]{1,0:T(8,128)(2,1)} %collective-permute-done.16, bf16[256,1024]{1,0:T(8,128)(2,1)S(1)} %collective-permute-done.15, bf16[256,1024]{1,0:T(8,128)(2,1)} %collective-permute-done.14, bf16[256,512]{1,0:T(8,128)(2,1)S(1)} %get-tuple-element.68, ...), kind=kOutput, calls=%fused_computation.9 | convolution fusion | flops 1086849024 | bytes 4194304 | tf_op jit(solution)/shard_map/dot_general | solution.py:340
  112.9 3.3 %collective-permute-start.22 = (f32[26,512]{1,0:T(8,128)S(1)}, f32[26,512]{1,0:T(8,128)}, u32[]{:S(2)}, u32[]{:S(2)}) collective-permute-start(f32[26,512]{1,0:T(8,128)S(1)} %concatenate.141), channel_id=1, source_target_pairs={{0,128},{4,132},{8,136},{12,140},{16,144},{20,148},{24,152},{28,15... | collective-permute-start | bytes 159752 | tf_op jit(solution)/shard_map/ppermute | solution.py:28
  117.4 8.8 %all-to-all-start = ((bf16[16,64,512]{2,1,0:T(8,128)(2,1)}), bf16[16,64,512]{2,1,0:T(8,128)(2,1)S(1)}, u32[]{:S(2)}, u32[]{:S(2)}) async-start(bf16[16,64,512]{2,1,0:T(8,128)(2,1)} %bitcast.179), calls=%async_computation | async-start | bytes 2097152 | tf_op jit(solution)/shard_map/all_to_all | solution.py:345
  126.8 1.1 add_add_fusion.2
  128.0 11.5 %collective-permute-done.24 = bf16[256,1024]{1,0:T(8,128)(2,1)} collective-permute-done((bf16[256,1024]{1,0:T(8,128)(2,1)}, bf16[256,1024]{1,0:T(8,128)(2,1)}, u32[]{:S(2)}, u32[]{:S(2)}) %collective-permute-start.24) | collective-permute-done | bytes 524320 | tf_op jit(solution)/shard_map/ppermute | solution.py:32
  139.4 7.2 %collective-permute-start.27 = (f32[26,512]{1,0:T(8,128)S(1)}, f32[26,512]{1,0:T(8,128)S(1)}, u32[]{:S(2)}, u32[]{:S(2)}) collective-permute-start(f32[26,512]{1,0:T(8,128)S(1)} %add_add_fusion.2), channel_id=1, source_target_pairs={{0,8},{4,12},{8,0},{12,4},{16,24},{20,28},{24,16},{28,20},{32,40},... | collective-permute-start | bytes 159752 | tf_op jit(solution)/shard_map/ppermute | solution.py:28
  146.6 1.2 collective-permute-start.26
  149.2 2.1 %collective-permute-done.28 = f32[26,512]{1,0:T(8,128)S(1)} collective-permute-done((f32[26,512]{1,0:T(8,128)S(1)}, f32[26,512]{1,0:T(8,128)S(1)}, u32[]{:S(2)}, u32[]{:S(2)}) %collective-permute-start.28) | collective-permute-done | bytes 53280 | tf_op jit(solution)/shard_map/ppermute | solution.py:28
  152.1 6.3 %collective-permute-start.29 = (f32[26,512]{1,0:T(8,128)S(1)}, f32[26,512]{1,0:T(8,128)S(1)}, u32[]{:S(2)}, u32[]{:S(2)}) collective-permute-start(f32[26,512]{1,0:T(8,128)S(1)} %add_add_fusion.1), channel_id=1, source_target_pairs={{0,16},{4,20},{8,24},{12,28},{16,0},{20,4},{24,8},{28,12},{32,48},... | collective-permute-start | bytes 159752 | tf_op jit(solution)/shard_map/ppermute | solution.py:28
  158.3 2.6 %fusion.15 = bf16[256,1024]{1,0:T(8,128)(2,1)} fusion(f32[512,1024]{1,0:T(8,128)S(1)} %copy-done.1, bf16[256,1024]{1,0:T(8,128)(2,1)} %collective-permute-done.24, bf16[256,512]{1,0:T(8,128)(2,1)S(1)} %fusion.52, bf16[512,4096]{1,0:T(8,128)(2,1)} %param.12, s32[]{:T(128)S(6)} %select_n.84), kind=kOutput, calls=%fused_computation.20 | convolution fusion | flops 269484032 | bytes 3407876 | tf_op jit(solution)/shard_map/dot_general | solution.py:304
  (153 shorter events, 23.9 us)
Async XLA Ops:
  0.6 18.6 %copy-start.7 = (bf16[256,3,512]{2,0,1:T(8,128)(2,1)S(1)}, bf16[256,3,512]{2,0,1:T(8,128)(2,1)}, u32[]{:S(2)}) copy-start(bf16[256,3,512]{2,0,1:T(8,128)(2,1)} %param.7) | copy-start | bytes 2359300
  0.6 19.5 %collective-permute-start.1 = (bf16[256,1024]{1,0:T(8,128)(2,1)}, bf16[256,1024]{1,0:T(8,128)(2,1)}, u32[]{:S(2)}, u32[]{:S(2)}) collective-permute-start(bf16[256,1024]{1,0:T(8,128)(2,1)} %param.13), channel_id=1, source_target_pairs={{0,2},{1,3},{2,0},{3,1},{4,6},{5,7},{6,4},{7,5},{8,10},{9,11},{10,... | collective-permute-start | bytes 1572872 | tf_op jit(solution)/shard_map/ppermute | solution.py:32
  2.6 23.6 %collective-permute-start.3 = (bf16[256,1024]{1,0:T(8,128)(2,1)}, bf16[256,1024]{1,0:T(8,128)(2,1)S(1)}, u32[]{:S(2)}, u32[]{:S(2)}) collective-permute-start(bf16[256,1024]{1,0:T(8,128)(2,1)} %param.13), channel_id=1, source_target_pairs={{0,1},{1,0},{2,3},{3,2},{4,5},{5,4},{6,7},{7,6},{8,9},{9,8},{10,11... | collective-permute-start | bytes 1572872 | tf_op jit(solution)/shard_map/ppermute | solution.py:32
  3.4 15.8 %collective-permute-start = (bf16[2,3,512]{2,0,1:T(2,128)(2,1)S(1)}, bf16[2,3,512]{2,0,1:T(2,128)(2,1)}, u32[]{:S(2)}, u32[]{:S(2)}) collective-permute-start(bf16[2,3,512]{2,0,1:T(2,128)(2,1)S(1)} %slice.166), channel_id=1, source_target_pairs={{0,4},{4,8},{8,12},{12,16},{16,20},{20,24},{24,28},{28,32},{32,36}... | collective-permute-start | bytes 18440 | tf_op jit(solution)/shard_map/ppermute | solution.py:37
  20.2 7.8 %collective-permute-start.2 = (bf16[256,1024]{1,0:T(8,128)(2,1)}, bf16[256,1024]{1,0:T(8,128)(2,1)S(1)}, u32[]{:S(2)}, u32[]{:S(2)}) collective-permute-start(bf16[256,1024]{1,0:T(8,128)(2,1)} %collective-permute-done.1), channel_id=1, source_target_pairs={{0,1},{1,0},{2,3},{3,2},{4,5},{5,4},{6,7},{7,6},{8,9},{9,8},{10,11... | collective-permute-start | bytes 1572872 | tf_op jit(solution)/shard_map/ppermute | solution.py:32
  29.7 17.2 %copy-start.24 = (f32[2]{0:T(128)S(1)}, f32[2]{0:T(128)}, u32[]{:S(2)}) copy-start(f32[2]{0:T(128)} %get-tuple-element.89) | copy-start | bytes 28
  29.7 17.2 %copy-start.25 = (f32[2]{0:T(128)S(1)}, f32[2]{0:T(128)}, u32[]{:S(2)}) copy-start(f32[2]{0:T(128)} %get-tuple-element.90) | copy-start | bytes 28
  29.8 31.8 %copy-start.22 = (f32[2]{0:T(128)S(1)}, f32[2]{0:T(128)}, u32[]{:S(2)}) copy-start(f32[2]{0:T(128)} %get-tuple-element.93) | copy-start | bytes 28
  29.8 31.8 %copy-start.23 = (f32[2]{0:T(128)S(1)}, f32[2]{0:T(128)}, u32[]{:S(2)}) copy-start(f32[2]{0:T(128)} %get-tuple-element.94) | copy-start | bytes 28
  29.8 36.1 %copy-start.8 = (bf16[256,1024]{1,0:T(8,128)(2,1)S(1)}, bf16[256,1024]{1,0:T(8,128)(2,1)}, u32[]{:S(2)}) copy-start(bf16[256,1024]{1,0:T(8,128)(2,1)} %param.13) | copy-start | bytes 1572868
  29.8 40.7 %copy-start.28 = (f32[2]{0:T(128)S(1)}, f32[2]{0:T(128)}, u32[]{:S(2)}) copy-start(f32[2]{0:T(128)} %get-tuple-element.97) | copy-start | bytes 28
  29.8 40.7 %copy-start.29 = (f32[2]{0:T(128)S(1)}, f32[2]{0:T(128)}, u32[]{:S(2)}) copy-start(f32[2]{0:T(128)} %get-tuple-element.98) | copy-start | bytes 28
  29.8 40.7 %copy-start.30 = (pred[2]{0:T(512)(128)(4,1)S(1)}, pred[2]{0:T(512)(128)(4,1)}, u32[]{:S(2)}) copy-start(pred[2]{0:T(512)(128)(4,1)} %get-tuple-element.107) | copy-start | bytes 10
  29.8 40.7 %copy-start.31 = (pred[2]{0:T(512)(128)(4,1)S(1)}, pred[2]{0:T(512)(128)(4,1)}, u32[]{:S(2)}) copy-start(pred[2]{0:T(512)(128)(4,1)} %get-tuple-element.108) | copy-start | bytes 10
  29.8 40.7 %copy-start.32 = (f32[2]{0:T(128)S(1)}, f32[2]{0:T(128)}, u32[]{:S(2)}) copy-start(f32[2]{0:T(128)} %get-tuple-element.99) | copy-start | bytes 28
  29.9 40.7 %copy-start.33 = (f32[2]{0:T(128)S(1)}, f32[2]{0:T(128)}, u32[]{:S(2)}) copy-start(f32[2]{0:T(128)} %get-tuple-element.100) | copy-start | bytes 28
  29.9 40.7 %copy-start.34 = (pred[2]{0:T(512)(128)(4,1)S(1)}, pred[2]{0:T(512)(128)(4,1)}, u32[]{:S(2)}) copy-start(pred[2]{0:T(512)(128)(4,1)} %get-tuple-element.109) | copy-start | bytes 10
  29.9 40.7 %copy-start.35 = (pred[2]{0:T(512)(128)(4,1)S(1)}, pred[2]{0:T(512)(128)(4,1)}, u32[]{:S(2)}) copy-start(pred[2]{0:T(512)(128)(4,1)} %get-tuple-element.110) | copy-start | bytes 10
  37.4 5.3 %collective-permute-start.6 = (f32[2,16,512]{2,1,0:T(8,128)S(1)}, f32[2,16,512]{2,1,0:T(8,128)S(1)}, u32[]{:S(2)}, u32[]{:S(2)}) collective-permute-start(f32[2,16,512]{2,1,0:T(8,128)S(1)} %pad_maximum_fusion.6), channel_id=1, source_target_pairs={{0,12},{4,8},{8,4},{12,0},{16,28},{20,24},{24,20},{28,16},{32,44},... | collective-permute-start | bytes 196616 | tf_op jit(solution)/shard_map/ppermute | solution.py:28
  38.3 7.3 %collective-permute-start.5 = (f32[2,16,512]{2,1,0:T(8,128)S(1)}, f32[2,16,512]{2,1,0:T(8,128)S(1)}, u32[]{:S(2)}, u32[]{:S(2)}) collective-permute-start(f32[2,16,512]{2,1,0:T(8,128)S(1)} %pad_maximum_fusion.6), channel_id=1, source_target_pairs={{0,8},{4,12},{8,0},{12,4},{16,24},{20,28},{24,16},{28,20},{32,40},... | collective-permute-start | bytes 196616 | tf_op jit(solution)/shard_map/ppermute | solution.py:28
  42.7 4.3 %collective-permute-start.4 = (f32[2,16,512]{2,1,0:T(8,128)S(1)}, f32[2,16,512]{2,1,0:T(8,128)S(1)}, u32[]{:S(2)}, u32[]{:S(2)}) collective-permute-start(f32[2,16,512]{2,1,0:T(8,128)S(1)} %pad_maximum_fusion.6), channel_id=1, source_target_pairs={{0,4},{4,0},{8,12},{12,8},{16,20},{20,16},{24,28},{28,24},{32,36},... | collective-permute-start | bytes 196616 | tf_op jit(solution)/shard_map/ppermute | solution.py:28
  47.9 8.1 %collective-permute-start.9 = (f32[2,16,512]{2,1,0:T(8,128)S(1)}, f32[2,16,512]{2,1,0:T(8,128)S(1)}, u32[]{:S(2)}, u32[]{:S(2)}) collective-permute-start(f32[2,16,512]{2,1,0:T(8,128)S(1)} %multiply_add_fusion.5), channel_id=1, source_target_pairs={{0,48},{4,52},{8,56},{12,60},{16,32},{20,36},{24,40},{28,44},{32,1... | collective-permute-start | bytes 196616 | tf_op jit(solution)/shard_map/ppermute | solution.py:28
  51.3 9.9 %collective-permute-start.8 = (f32[2,16,512]{2,1,0:T(8,128)S(1)}, f32[2,16,512]{2,1,0:T(8,128)S(1)}, u32[]{:S(2)}, u32[]{:S(2)}) collective-permute-start(f32[2,16,512]{2,1,0:T(8,128)S(1)} %multiply_add_fusion.5), channel_id=1, source_target_pairs={{0,32},{4,36},{8,40},{12,44},{16,48},{20,52},{24,56},{28,60},{32,0... | collective-permute-start | bytes 196616 | tf_op jit(solution)/shard_map/ppermute | solution.py:28
  55.1 6.5 %collective-permute-start.7 = (f32[2,16,512]{2,1,0:T(8,128)S(1)}, f32[2,16,512]{2,1,0:T(8,128)S(1)}, u32[]{:S(2)}, u32[]{:S(2)}) collective-permute-start(f32[2,16,512]{2,1,0:T(8,128)S(1)} %multiply_add_fusion.5), channel_id=1, source_target_pairs={{0,16},{4,20},{8,24},{12,28},{16,0},{20,4},{24,8},{28,12},{32,48},... | collective-permute-start | bytes 196616 | tf_op jit(solution)/shard_map/ppermute | solution.py:28
  61.7 5.8 %collective-permute-start.12 = (f32[2,16,512]{2,1,0:T(8,128)S(1)}, f32[2,16,512]{2,1,0:T(8,128)S(1)}, u32[]{:S(2)}, u32[]{:S(2)}) collective-permute-start(f32[2,16,512]{2,1,0:T(8,128)S(1)} %multiply_add_fusion.4), channel_id=1, source_target_pairs={{0,192},{4,196},{8,200},{12,204},{16,208},{20,212},{24,216},{28,22... | collective-permute-start | bytes 196616 | tf_op jit(solution)/shard_map/ppermute | solution.py:28
  64.8 5.8 %collective-permute-start.11 = (f32[2,16,512]{2,1,0:T(8,128)S(1)}, f32[2,16,512]{2,1,0:T(8,128)S(1)}, u32[]{:S(2)}, u32[]{:S(2)}) collective-permute-start(f32[2,16,512]{2,1,0:T(8,128)S(1)} %multiply_add_fusion.4), channel_id=1, source_target_pairs={{0,128},{4,132},{8,136},{12,140},{16,144},{20,148},{24,152},{28,15... | collective-permute-start | bytes 196616 | tf_op jit(solution)/shard_map/ppermute | solution.py:28
  65.4 5.1 %collective-permute-start.10 = (f32[2,16,512]{2,1,0:T(8,128)S(1)}, f32[2,16,512]{2,1,0:T(8,128)S(1)}, u32[]{:S(2)}, u32[]{:S(2)}) collective-permute-start(f32[2,16,512]{2,1,0:T(8,128)S(1)} %multiply_add_fusion.4), channel_id=1, source_target_pairs={{0,64},{4,68},{8,72},{12,76},{16,80},{20,84},{24,88},{28,92},{32,9... | collective-permute-start | bytes 196616 | tf_op jit(solution)/shard_map/ppermute | solution.py:28
  65.9 16.3 %collective-permute-start.14 = (bf16[256,1024]{1,0:T(8,128)(2,1)S(1)}, bf16[256,1024]{1,0:T(8,128)(2,1)}, u32[]{:S(2)}, u32[]{:S(2)}) collective-permute-start(bf16[256,1024]{1,0:T(8,128)(2,1)S(1)} %copy-done.8), channel_id=1, source_target_pairs={{0,0},{1,64},{2,128},{3,192},{4,4},{5,68},{6,132},{7,196},{8,8},{9... | collective-permute-start | bytes 1572872 | tf_op jit(solution)/shard_map/ppermute | solution.py:266
  82.2 19.2 %collective-permute-start.13 = (bf16[512,1024]{1,0:T(8,128)(2,1)}, bf16[512,1024]{1,0:T(8,128)(2,1)S(1)}, u32[]{:S(2)}, u32[]{:S(2)}) collective-permute-start(bf16[512,1024]{1,0:T(8,128)(2,1)} %pad_maximum_fusion), channel_id=1, source_target_pairs={{0,1},{1,0},{2,3},{3,2},{4,5},{5,4},{6,7},{7,6},{8,9},{9,8},{10,11... | collective-permute-start | bytes 3145736 | tf_op jit(solution)/shard_map/ppermute | solution.py:32
  82.2 14.9 %collective-permute-start.16 = (bf16[256,1024]{1,0:T(8,128)(2,1)}, bf16[256,1024]{1,0:T(8,128)(2,1)}, u32[]{:S(2)}, u32[]{:S(2)}) collective-permute-start(bf16[256,1024]{1,0:T(8,128)(2,1)} %collective-permute-done.14), channel_id=1, source_target_pairs={{0,2},{1,3},{2,0},{3,1},{4,6},{5,7},{6,4},{7,5},{8,10},{9,11},{10,... | collective-permute-start | bytes 1572872 | tf_op jit(solution)/shard_map/ppermute | solution.py:32
  85.4 14.1 %collective-permute-start.20 = (bf16[256,512]{1,0:T(8,128)(2,1)S(1)}, bf16[256,512]{1,0:T(8,128)(2,1)S(1)}, u32[]{:S(2)}, u32[]{:S(2)}) collective-permute-start(bf16[256,512]{1,0:T(8,128)(2,1)S(1)} %fusion.52), channel_id=1, source_target_pairs={{0,192},{4,196},{8,200},{12,204},{16,208},{20,212},{24,216},{28,22... | collective-permute-start | bytes 786440 | tf_op jit(solution)/shard_map/ppermute | solution.py:28
  86.6 12.9 %collective-permute-start.19 = (bf16[256,512]{1,0:T(8,128)(2,1)S(1)}, bf16[256,512]{1,0:T(8,128)(2,1)S(1)}, u32[]{:S(2)}, u32[]{:S(2)}) collective-permute-start(bf16[256,512]{1,0:T(8,128)(2,1)S(1)} %fusion.52), channel_id=1, source_target_pairs={{0,128},{4,132},{8,136},{12,140},{16,144},{20,148},{24,152},{28,15... | collective-permute-start | bytes 786440 | tf_op jit(solution)/shard_map/ppermute | solution.py:28
  87.7 12.4 %collective-permute-start.18 = (bf16[256,512]{1,0:T(8,128)(2,1)S(1)}, bf16[256,512]{1,0:T(8,128)(2,1)}, u32[]{:S(2)}, u32[]{:S(2)}) collective-permute-start(bf16[256,512]{1,0:T(8,128)(2,1)S(1)} %fusion.52), channel_id=1, source_target_pairs={{0,64},{4,68},{8,72},{12,76},{16,80},{20,84},{24,88},{28,92},{32,9... | collective-permute-start | bytes 786440 | tf_op jit(solution)/shard_map/ppermute | solution.py:28
  97.1 12.1 %collective-permute-start.15 = (bf16[256,1024]{1,0:T(8,128)(2,1)}, bf16[256,1024]{1,0:T(8,128)(2,1)S(1)}, u32[]{:S(2)}, u32[]{:S(2)}) collective-permute-start(bf16[256,1024]{1,0:T(8,128)(2,1)} %collective-permute-done.14), channel_id=1, source_target_pairs={{0,1},{1,0},{2,3},{3,2},{4,5},{5,4},{6,7},{7,6},{8,9},{9,8},{10,11... | collective-permute-start | bytes 1572872 | tf_op jit(solution)/shard_map/ppermute | solution.py:32
  99.5 9.7 %collective-permute-start.17 = (bf16[256,1024]{1,0:T(8,128)(2,1)}, bf16[256,1024]{1,0:T(8,128)(2,1)S(1)}, u32[]{:S(2)}, u32[]{:S(2)}) collective-permute-start(bf16[256,1024]{1,0:T(8,128)(2,1)} %collective-permute-done.16), channel_id=1, source_target_pairs={{0,1},{1,0},{2,3},{3,2},{4,5},{5,4},{6,7},{7,6},{8,9},{9,8},{10,11... | collective-permute-start | bytes 1572872 | tf_op jit(solution)/shard_map/ppermute | solution.py:32
  106.9 19.4 %collective-permute-start.25 = (f32[3,2,512]{2,1,0:T(2,128)S(1)}, f32[3,2,512]{2,1,0:T(2,128)S(1)}, u32[]{:S(2)}, u32[]{:S(2)}) collective-permute-start(f32[3,2,512]{2,1,0:T(2,128)S(1)} %pad_maximum_fusion.7), channel_id=1, source_target_pairs={{4,0},{8,4},{12,8},{16,12},{20,16},{24,20},{28,24},{32,28},{36,32}... | collective-permute-start | bytes 36872 | tf_op jit(solution)/shard_map/ppermute | solution.py:37
  112.9 13.9 %collective-permute-start.22 = (f32[26,512]{1,0:T(8,128)S(1)}, f32[26,512]{1,0:T(8,128)}, u32[]{:S(2)}, u32[]{:S(2)}) collective-permute-start(f32[26,512]{1,0:T(8,128)S(1)} %concatenate.141), channel_id=1, source_target_pairs={{0,128},{4,132},{8,136},{12,140},{16,144},{20,148},{24,152},{28,15... | collective-permute-start | bytes 159752 | tf_op jit(solution)/shard_map/ppermute | solution.py:28
  116.2 10.6 %collective-permute-start.23 = (f32[26,512]{1,0:T(8,128)S(1)}, f32[26,512]{1,0:T(8,128)}, u32[]{:S(2)}, u32[]{:S(2)}) collective-permute-start(f32[26,512]{1,0:T(8,128)S(1)} %concatenate.141), channel_id=1, source_target_pairs={{0,192},{4,196},{8,200},{12,204},{16,208},{20,212},{24,216},{28,22... | collective-permute-start | bytes 159752 | tf_op jit(solution)/shard_map/ppermute | solution.py:28
  117.1 9.8 %collective-permute-start.21 = (f32[26,512]{1,0:T(8,128)S(1)}, f32[26,512]{1,0:T(8,128)}, u32[]{:S(2)}, u32[]{:S(2)}) collective-permute-start(f32[26,512]{1,0:T(8,128)S(1)} %concatenate.141), channel_id=1, source_target_pairs={{0,64},{4,68},{8,72},{12,76},{16,80},{20,84},{24,88},{28,92},{32,9... | collective-permute-start | bytes 159752 | tf_op jit(solution)/shard_map/ppermute | solution.py:28
  117.1 22.4 %collective-permute-start.24 = (bf16[256,1024]{1,0:T(8,128)(2,1)}, bf16[256,1024]{1,0:T(8,128)(2,1)}, u32[]{:S(2)}, u32[]{:S(2)}) collective-permute-start(bf16[256,1024]{1,0:T(8,128)(2,1)} %fusion.13), channel_id=1, source_target_pairs={{0,2},{1,3},{2,0},{3,1},{4,6},{5,7},{6,4},{7,5},{8,10},{9,11},{10,... | collective-permute-start | bytes 1572872 | tf_op jit(solution)/shard_map/ppermute | solution.py:32
  117.4 45.8 %all-to-all-start = ((bf16[16,64,512]{2,1,0:T(8,128)(2,1)}), bf16[16,64,512]{2,1,0:T(8,128)(2,1)S(1)}, u32[]{:S(2)}, u32[]{:S(2)}) async-start(bf16[16,64,512]{2,1,0:T(8,128)(2,1)} %bitcast.179), calls=%async_computation | async-start | bytes 2097152 | tf_op jit(solution)/shard_map/all_to_all | solution.py:345
  126.4 31.9 %copy-start.1 = (f32[512,1024]{1,0:T(8,128)S(1)}, f32[512,1024]{1,0:T(8,128)}, u32[]{:S(2)}) copy-start(f32[512,1024]{1,0:T(8,128)} %copy-done) | copy-start | bytes 6291460
  139.4 9.8 %collective-permute-start.27 = (f32[26,512]{1,0:T(8,128)S(1)}, f32[26,512]{1,0:T(8,128)S(1)}, u32[]{:S(2)}, u32[]{:S(2)}) collective-permute-start(f32[26,512]{1,0:T(8,128)S(1)} %add_add_fusion.2), channel_id=1, source_target_pairs={{0,8},{4,12},{8,0},{12,4},{16,24},{20,28},{24,16},{28,20},{32,40},... | collective-permute-start | bytes 159752 | tf_op jit(solution)/shard_map/ppermute | solution.py:28
  146.6 4.7 %collective-permute-start.28 = (f32[26,512]{1,0:T(8,128)S(1)}, f32[26,512]{1,0:T(8,128)S(1)}, u32[]{:S(2)}, u32[]{:S(2)}) collective-permute-start(f32[26,512]{1,0:T(8,128)S(1)} %add_add_fusion.2), channel_id=1, source_target_pairs={{0,12},{4,8},{8,4},{12,0},{16,28},{20,24},{24,20},{28,16},{32,44},... | collective-permute-start | bytes 159752 | tf_op jit(solution)/shard_map/ppermute | solution.py:28
  146.6 5.1 %collective-permute-start.26 = (f32[26,512]{1,0:T(8,128)S(1)}, f32[26,512]{1,0:T(8,128)S(1)}, u32[]{:S(2)}, u32[]{:S(2)}) collective-permute-start(f32[26,512]{1,0:T(8,128)S(1)} %add_add_fusion.2), channel_id=1, source_target_pairs={{0,4},{4,0},{8,12},{12,8},{16,20},{20,16},{24,28},{28,24},{32,36},... | collective-permute-start | bytes 159752 | tf_op jit(solution)/shard_map/ppermute | solution.py:28
  151.7 9.2 %collective-permute-start.30 = (f32[26,512]{1,0:T(8,128)S(1)}, f32[26,512]{1,0:T(8,128)S(1)}, u32[]{:S(2)}, u32[]{:S(2)}) collective-permute-start(f32[26,512]{1,0:T(8,128)S(1)} %add_add_fusion.1), channel_id=1, source_target_pairs={{0,32},{4,36},{8,40},{12,44},{16,48},{20,52},{24,56},{28,60},{32,0... | collective-permute-start | bytes 159752 | tf_op jit(solution)/shard_map/ppermute | solution.py:28
  151.8 9.1 %collective-permute-start.31 = (f32[26,512]{1,0:T(8,128)S(1)}, f32[26,512]{1,0:T(8,128)S(1)}, u32[]{:S(2)}, u32[]{:S(2)}) collective-permute-start(f32[26,512]{1,0:T(8,128)S(1)} %add_add_fusion.1), channel_id=1, source_target_pairs={{0,48},{4,52},{8,56},{12,60},{16,32},{20,36},{24,40},{28,44},{32,1... | collective-permute-start | bytes 159752 | tf_op jit(solution)/shard_map/ppermute | solution.py:28
  152.1 9.2 %collective-permute-start.29 = (f32[26,512]{1,0:T(8,128)S(1)}, f32[26,512]{1,0:T(8,128)S(1)}, u32[]{:S(2)}, u32[]{:S(2)}) collective-permute-start(f32[26,512]{1,0:T(8,128)S(1)} %add_add_fusion.1), channel_id=1, source_target_pairs={{0,16},{4,20},{8,24},{12,28},{16,0},{20,4},{24,8},{28,12},{32,48},... | collective-permute-start | bytes 159752 | tf_op jit(solution)/shard_map/ppermute | solution.py:28
  (21 other events, 118.9 us)
